TPU v7x, 512 devices: a whole 4x4x16 slice. The times are simulated.
512 devices in a mesh: grp: 8 (over y, core), own: 64 (over z, x).
Axes of the slice: x: 4, y: 4, z: 16, core: 2. Of those that a mesh axis runs over, the one named last changes fastest.
Arguments:
- amplitudes: bfloat16 [3072, 128, 128], P('own', 'grp'), may hold values from -6 to 6
- integrals: bfloat16 [49152, 8192], P('own', 'grp'), may hold values from -0.02734375 to 0.02734375
- tile_block: int32 [3072], P('own'), may hold values from 0 to 7, as said below
- tile_index: int32 [3072], P('own'), may hold values from 0 to 383, as said below
Outputs:
- ladder: float32 [1024, 8192], P('own', 'grp')
Inputs may be any that keep to these rules, and one draw needn't show every extreme that they name: Each pair (tile_block, tile_index) is named by at most one of the 3072 tile rows. Of the 48 rows of one own index, at most 2 have tile_index in one owner's range o * 6 to (o + 1) * 6 - 1, and exactly 2 do for some owners. Exactly 48 of all tile rows have tile_index in each owner's range. `tile_index`: owner o holds integral rows of tiles o * 6 to (o + 1) * 6 - 1.
All inputs are finite; a program needn't handle non-finite values.
Results may differ from a plain program's by a relative error of at most 0.0003.
Values may be sent and summed in bfloat16 or wider, within the bound.
No kernel may reach another device: no remote copies, remote signals or barrier semaphores. Data moves between devices by JAX's collectives and lax.ppermute only.
A program may use at most 64 MiB of HBM per device.

v0:
```python
import jax
import jax.numpy as jnp
from jax import lax
from jax.sharding import PartitionSpec as P

NB = 8
CAP = 2


def local(amplitudes, integrals, tile_block, tile_index):
    own_count = lax.axis_size("own")
    tile_width = amplitudes.shape[2]
    tile_dev = integrals.shape[0] // tile_width
    tile_owner = tile_index // tile_dev
    local_tile = tile_index - tile_owner * tile_dev
    tile_key = tile_block * tile_dev + local_tile
    one_hot = (tile_owner[:, None] == jnp.arange(own_count)[None, :]).astype(jnp.int32)
    slot_rank = jnp.sum((jnp.cumsum(one_hot, axis=0) - one_hot) * one_hot, axis=1)
    key_buffer = jnp.full((own_count, CAP), -1, jnp.int32).at[tile_owner, slot_rank].set(tile_key)
    gathered = lax.all_gather(amplitudes, "grp", axis=1, tiled=True)
    buffer = jnp.zeros((own_count, CAP) + gathered.shape[1:], gathered.dtype)
    received = lax.all_to_all(
        buffer.at[tile_owner, slot_rank].set(gathered),
        "own",
        split_axis=0,
        concat_axis=0,
        tiled=True,
    )
    recv_keys = lax.all_to_all(key_buffer, "own", split_axis=0, concat_axis=0, tiled=True)
    occ_rows = received.shape[2]
    slots = received.reshape(own_count * CAP, occ_rows, tile_width)
    flat_keys = recv_keys.reshape(own_count * CAP)
    recv_block = jnp.where(flat_keys >= 0, flat_keys // tile_dev, -1)
    recv_tile = jnp.where(flat_keys >= 0, flat_keys % tile_dev, 0)
    total_rows = NB * occ_rows
    row_count = total_rows // own_count * lax.axis_size("own")
    first_row = recv_block * occ_rows - jnp.int32(0)
    row_index = first_row[:, None] + jnp.arange(occ_rows)[None, :]
    in_range = (recv_block[:, None] >= 0) & (row_index >= 0) & (row_index < row_count)
    row_index = jnp.where(in_range, row_index, row_count)
    tile_slot = jnp.broadcast_to(recv_tile[:, None], row_index.shape)
    placed = jnp.zeros((row_count, tile_dev, tile_width), slots.dtype)
    placed = placed.at[row_index, tile_slot].set(slots, mode="drop")
    return lax.psum_scatter(
        jnp.dot(
            placed.reshape(row_count, tile_dev * tile_width),
            integrals,
            preferred_element_type=jnp.float32,
        ),
        "own",
        scatter_dimension=0,
        tiled=True,
    )


def solution(mesh):
    return jax.shard_map(
        local,
        mesh=mesh,
        in_specs=(P("own", "grp", None), P("own", "grp"), P("own"), P("own")),
        out_specs=P("own", "grp"),
        check_vma=False,
    )
```

profile of v0, /device:TPU:6, one launch (start us, length us, event | category | flops | bytes accessed | tf_op | source)
XLA Modules:
  0.0 993.3 jit_solution(9781323741597554394)
XLA Ops:
  6.5 0.7 all-gather.2.cloned.1.call-update
  7.3 0.7 subtract_add_fusion
  8.1 0.2 select_reduce_fusion
  8.3 2.8 scatter_fusion
  11.1 0.7 copy.18
  11.8 18.6 %all-to-all-start = ((s32[64,1,2]{2,1,0:T(1,128)}), s32[64,1,2]{2,1,0:T(1,128)S(1)}, u32[]{:S(2)}, u32[]{:S(2)}) async-start(s32[64,1,2]{2,1,0:T(1,128)} %copy.18), calls=%async_computation | async-start | bytes 65536 | tf_op jit(solution)/shard_map/all_to_all | solution.py:29
  30.4 16.4 %all-gather.2.cloned.1.call-done = bf16[48,128,128]{2,1,0:T(8,128)(2,1)} async-done(((bf16[48,16,128]{2,1,0:T(8,128)(2,1)}), bf16[48,128,128]{2,1,0:T(8,128)(2,1)}) %all-gather.2.cloned.1.call-update) | async-done | bytes 1572880 | tf_op jit(solution)/shard_map/all_gather | solution.py:20
  46.8 3.0 broadcast_in_dim.43
  49.7 7.1 scatter_fusion.1
  56.9 16.0 %all-to-all-start.1 = ((bf16[64,2,128,128]{3,2,1,0:T(8,128)(2,1)}), bf16[64,2,128,128]{3,2,1,0:T(8,128)(2,1)}, u32[]{:S(2)}, u32[]{:S(2)}) async-start(bf16[64,2,128,128]{3,2,1,0:T(8,128)(2,1)} %scatter_fusion.1), calls=%async_computation.1 | async-start | bytes 8388608 | tf_op jit(solution)/shard_map/all_to_all | solution.py:22
  73.0 0.2 compare_reduce_fusion
  73.2 0.1 ne.69
  73.4 0.1 ge.37
  73.5 0.3 divide_reduce_fusion
  73.8 0.1 div.24
  73.9 0.1 rem.39
  74.1 0.2 compare_select_fusion
  74.3 0.1 multiply_reduce_fusion
  74.4 0.1 and_reduce_fusion
  74.5 188.8 %all-to-all-done.1 = bf16[64,2,128,128]{3,2,1,0:T(8,128)(2,1)} async-done(((bf16[64,2,128,128]{3,2,1,0:T(8,128)(2,1)}), bf16[64,2,128,128]{3,2,1,0:T(8,128)(2,1)}, u32[]{:S(2)}, u32[]{:S(2)}) %all-to-all-start.1) | async-done | bytes 4194336 | tf_op jit(solution)/shard_map/all_to_all | solution.py:22
  263.3 41.9 %scatter_custom_fusion.2 = bf16[6144,128]{1,0:T(8,128)(2,1)S(1)} fusion(s32[16384]{0:T(1024)S(1)} %select_bitcast_fusion, bf16[16384,128]{1,0:T(8,128)(2,1)} %bitcast.5, bf16[]{:T(256)} %constant.16.clone.1), kind=kCustom, calls=%fused_computation.3 | custom fusion | bytes 1573376
  305.2 1.6 copy.19
  306.8 5.2 fusion.14
  312.0 674.4 %reduce-scatter.2.cloned.1.call-done = f32[16,1024]{1,0:T(8,128)} async-done(((f32[1024,1024]{1,0:T(8,128)}), f32[16,1024]{1,0:T(8,128)}) %reduce-scatter.2.cloned.1.call-update) | async-done | bytes 65552 | tf_op jit(solution)/shard_map/reduce_scatter | solution.py:44
  (20 shorter events, 0.3 us)
Async XLA Ops:
  6.5 300.3 %copy-start = (bf16[768,1024]{1,0:T(8,128)(2,1)S(1)}, bf16[768,1024]{1,0:T(8,128)(2,1)}, u32[]{:S(2)}) copy-start(bf16[768,1024]{1,0:T(8,128)(2,1)} %param.5) | copy-start | bytes 4718596
  6.5 40.2 %all-gather.2.cloned.1.call-start = ((), (), s32[]{:S(2)}) async-start(), calls=%async_computation.3 | async-start | bytes 1769472 | tf_op jit(solution)/shard_map/all_gather | solution.py:20
  11.8 45.1 %all-to-all-start = ((s32[64,1,2]{2,1,0:T(1,128)}), s32[64,1,2]{2,1,0:T(1,128)S(1)}, u32[]{:S(2)}, u32[]{:S(2)}) async-start(s32[64,1,2]{2,1,0:T(1,128)} %copy.18), calls=%async_computation | async-start | bytes 65536 | tf_op jit(solution)/shard_map/all_to_all | solution.py:29
  46.8 3.0 copy-start.1
  56.9 17.4 %copy-start.3 = (s32[2]{0:T(128)S(1)}, s32[2]{0:T(128)}, u32[]{:S(2)}) copy-start(s32[2]{0:T(128)} %constant.53) | copy-start | bytes 28
  56.9 17.5 %copy-start.2 = (s32[2]{0:T(128)S(1)}, s32[2]{0:T(128)}, u32[]{:S(2)}) copy-start(s32[2]{0:T(128)} %constant.56) | copy-start | bytes 28
  56.9 206.4 %all-to-all-start.1 = ((bf16[64,2,128,128]{3,2,1,0:T(8,128)(2,1)}), bf16[64,2,128,128]{3,2,1,0:T(8,128)(2,1)}, u32[]{:S(2)}, u32[]{:S(2)}) async-start(bf16[64,2,128,128]{3,2,1,0:T(8,128)(2,1)} %scatter_fusion.1), calls=%async_computation.1 | async-start | bytes 8388608 | tf_op jit(solution)/shard_map/all_to_all | solution.py:22
  72.9 913.5 %reduce-scatter.2.cloned.1.call-start = ((), (), s32[]{:S(2)}) async-start(), calls=%async_computation.4 | async-start | bytes 4259840 | tf_op jit(solution)/shard_map/reduce_scatter | solution.py:44
Sparse Core Ops, SparseCore 0:
  9.5 37.2 all-gather.1
  312.1 674.2 reduce-scatter.1
where the time goes:
time: 995 us; the launch traced here: 993 us
  waiting for transfers between devices  880 us (88%)
  local copies, waits for them, and re-layouts  57.7 us (6%)
  starting transfers between devices  34.7 us (3%)
  between operations  13.5 us (1%)
    reduce_scatter x1, waiting for transfers between devices, local(): lax.psum_scatter(jnp.dot(placed.reshape(row_count, tile_dev * tile_width)...  674 us
    all_to_all x1, waiting for transfers between devices, local(): lax.all_to_all(buffer.at[tile_owner, slot_rank].set(gathered), 'own', spl...  189 us
    unnamed x9, local copies, waits for them, and re-layouts  41.9 us
  transfers between devices with their start and end apart: 4, of which 3 were waited for; matrix products, arithmetic and copies ran while one was open for 2% of the time, Pallas kernels for 0%

commit v1 on v0

v1 whole, which is shorter than its diff:
```python
import jax
import jax.numpy as jnp
from jax import lax
from jax.experimental import pallas as pl
from jax.experimental.pallas import tpu as pltpu
from jax.sharding import PartitionSpec as P

NB = 8
CAP = 2
NX = 4
TOP = 32767.0
STEPS = 64.0
TINY = 1e-30
VMEM = pl.BlockSpec(memory_space=pltpu.VMEM)
SMEM = pl.BlockSpec(memory_space=pltpu.SMEM)
PARAMS = pltpu.CompilerParams(vmem_limit_bytes=40 << 20)


def code_of(largest):
    return jnp.ceil(jnp.log2(jnp.maximum(largest, TINY)) * STEPS)


def coded(values, code):
    scaled = values * (jnp.exp2(code * (-1.0 / STEPS)) * (TOP - 1.0))
    return jnp.round(scaled).astype(jnp.int32).astype(jnp.int16)


def scale_of(code16):
    code = code16.astype(jnp.int32).astype(jnp.float32)
    return jnp.exp2(code * (1.0 / STEPS)) * (1.0 / (TOP - 1.0))


def plain(values16):
    return values16.astype(jnp.int32).astype(jnp.float32)


def pack(tile_dev, nz, amp, block, index, out, keys, count):
    rows = amp.shape[0]
    owners = nz * NX

    def clear(o, _):
        count[o] = 0
        return 0

    lax.fori_loop(0, owners, clear, 0)
    keys[...] = jnp.full(keys.shape, -1.0, jnp.float32)
    for r in range(rows):
        tile = index[r]
        owner = tile // tile_dev
        rank = count[owner]
        count[owner] = rank + 1
        key = block[r] * tile_dev + (tile - owner * tile_dev)
        z = owner // NX
        x = owner - z * NX
        slot = z * CAP + rank
        out[x, slot] = amp[r]
        keys[x, pl.ds(slot, 1), :] = jnp.full((1, keys.shape[2]), key, jnp.int32).astype(jnp.float32)
    slots = nz * CAP
    occ = amp.shape[1]
    for x in range(NX):
        for part in range(slots // occ):
            out[x, slots + part] = keys[x, part * occ : (part + 1) * occ, :].astype(out.dtype)


def repack(nz, got, out, keys):
    occ = got.shape[2]
    slots = nz * CAP
    for x in range(NX):
        for part in range(slots // occ):
            keys[x, part * occ : (part + 1) * occ, :] = got[x, slots + part].astype(jnp.float32)
    for z in range(nz):
        for x in range(NX):
            for s in range(CAP):
                out[z, x * CAP + s] = got[x, z * CAP + s]
    width = NX * CAP
    for z in range(nz):
        lines = [keys[x, z * CAP : (z + 1) * CAP, :] for x in range(NX)]
        lines += [jnp.full((occ - width, keys.shape[2]), -1.0, jnp.float32)]
        out[z, width] = jnp.concatenate(lines, axis=0).astype(out.dtype)


def place(tile_dev, got, out, held, row, key, sem):
    nz, _, occ, width = got.shape
    per = NX * CAP
    count = nz * per
    marks = jnp.concatenate([got[z, per].astype(jnp.float32)[:per] for z in range(nz)], axis=0)
    at = lax.broadcasted_iota(jnp.int32, (count, width), 0)
    of = lax.broadcasted_iota(jnp.int32, (count, width), 1)
    line = jnp.sum(jnp.where(at == of, marks, 0.0), axis=0, keepdims=True)
    row[...] = line.astype(jnp.int32)
    copy = pltpu.make_async_copy(row, key, sem)
    copy.start()
    copy.wait()
    spare = NB * tile_dev
    for z in range(nz):
        for s in range(per):
            k = key[0, z * per + s]
            held[jnp.where(k < 0, spare, k)] = got[z, s]
    for b in range(NB):
        for t in range(tile_dev):
            out[b * occ : (b + 1) * occ, t * width : (t + 1) * width] = held[b * tile_dev + t]


def multiply(a, v, out):
    rows, cols = a.shape[1], v.shape[1]
    parts = a.shape[0] // NX
    for x in range(NX):
        for h in range(parts):
            p = jnp.dot(a[x + NX * h], v[...], preferred_element_type=jnp.float32)
            grouped = p.reshape(rows // 8, 8, cols)
            code = code_of(jnp.max(jnp.abs(grouped), axis=0))
            q = coded(grouped, code[None])
            out[x, h * rows : (h + 1) * rows, :] = q.reshape(rows, cols)
            out[x, parts * rows + 8 * h : parts * rows + 8 * (h + 1), :] = code.astype(jnp.int32).astype(jnp.int16)


def add_x(rows, got, out):
    parts = (got.shape[1] - 16) // rows
    cols = got.shape[2]
    occ = rows // NB
    tiles = cols // 128
    for h in range(parts):
        total = None
        for x in range(NX):
            scale = scale_of(got[x, parts * rows + 8 * h : parts * rows + 8 * (h + 1), :])
            term = plain(got[x, h * rows : (h + 1) * rows, :]).reshape(rows // 8, 8, cols) * scale[None]
            total = term if total is None else total + term
        total = total.reshape(rows, cols)
        for b in range(NB):
            chunk = total[b * occ : (b + 1) * occ]
            lanes = [chunk[:, 128 * t : 128 * (t + 1)] for t in range(tiles)]
            largest = jnp.abs(lanes[0])
            for lane in lanes[1:]:
                largest = jnp.maximum(largest, jnp.abs(lane))
            code = code_of(largest)
            z = parts * b + h
            for t in range(tiles):
                out[z, t * occ : (t + 1) * occ, :] = coded(lanes[t], code)
            out[z, tiles * occ : (tiles + 1) * occ, :] = code.astype(jnp.int32).astype(jnp.int16)


def add_z(got, out):
    nz = got.shape[0]
    occ = out.shape[0]
    tiles = out.shape[1] // 128
    scales = [scale_of(got[z, tiles * occ : (tiles + 1) * occ, :]) for z in range(nz)]
    for t in range(tiles):
        total = None
        for z in range(nz):
            term = plain(got[z, t * occ : (t + 1) * occ, :]) * scales[z]
            total = term if total is None else total + term
        out[:, 128 * t : 128 * (t + 1)] = total


def call(body, out, ins, scratch=()):
    return pl.pallas_call(
        body, out_shape=out, in_specs=ins, out_specs=VMEM, scratch_shapes=list(scratch), compiler_params=PARAMS
    )


def local(amplitudes, integrals, tile_block, tile_index):
    own = lax.axis_size("own")
    nz = own // NX
    x_groups = [[z * NX + x for x in range(NX)] for z in range(nz)]
    z_groups = [[z * NX + x for z in range(nz)] for x in range(NX)]

    def exchange(array, groups):
        return lax.all_to_all(array, "own", 0, 0, axis_index_groups=groups, tiled=True)

    _, occ, width = amplitudes.shape
    tile_dev = integrals.shape[0] // width
    cols = integrals.shape[1]
    slots = nz * CAP
    dtype = amplitudes.dtype
    struct = jax.ShapeDtypeStruct

    packed = call(
        lambda *refs: pack(tile_dev, nz, *refs),
        struct((NX, slots + slots // occ, occ, width), dtype),
        [VMEM, SMEM, SMEM],
        [pltpu.VMEM((NX, slots, width), jnp.float32), pltpu.SMEM((own,), jnp.int32)],
    )(amplitudes, tile_block, tile_index)
    got = exchange(packed, x_groups)
    turned = call(
        lambda *refs: repack(nz, *refs),
        struct((nz, NX * CAP + 1, occ, width), dtype),
        [VMEM],
        [pltpu.VMEM((NX, slots, width), jnp.float32)],
    )(got)
    got = exchange(turned, z_groups)
    mine = call(
        lambda *refs: place(tile_dev, *refs),
        struct((NB * occ, tile_dev * width), dtype),
        [VMEM],
        [
            pltpu.VMEM((NB * tile_dev + 1, occ, width), dtype),
            pltpu.VMEM((1, width), jnp.int32),
            pltpu.SMEM((1, width), jnp.int32),
            pltpu.SemaphoreType.DMA,
        ],
    )(got)
    dense = lax.all_gather(mine, "grp", axis=0)
    rows = NB * occ
    parts = dense.shape[0] // NX
    sent = call(multiply, struct((NX, parts * rows + 8 * parts, cols), jnp.int16), [VMEM, VMEM])(dense, integrals)
    got = exchange(sent, x_groups)
    sent = call(
        lambda *refs: add_x(rows, *refs),
        struct((nz, (cols // 128 + 1) * occ, 128), jnp.int16),
        [VMEM],
    )(got)
    got = exchange(sent, z_groups)
    return call(add_z, struct((occ, cols), jnp.float32), [VMEM])(got)


def solution(mesh):
    return jax.shard_map(
        local,
        mesh=mesh,
        in_specs=(P("own", "grp", None), P("own", "grp"), P("own"), P("own")),
        out_specs=P("own", "grp"),
        check_vma=False,
    )
```

time: 995 us -> 188 us (0.19)
  waiting for transfers between devices: 880 us -> 24.3 us
  blocking collectives: 0 us -> 138 us
  local copies, waits for them, and re-layouts: 57.7 us -> 3.65 us
  starting transfers between devices: 34.7 us -> 0.01 us
    reduce_scatter x1 -> x0, waiting for transfers between devices: 674 us -> none  [local(): lax.psum_scatter(jnp.dot(placed.reshape(row_count, tile_dev * tile_width)...]
    all_to_all x2 -> x0, waiting for transfers between devices: 189 us -> none  [the longest x1 189 us: local(): lax.all_to_all(buffer.at[tile_owner, slot_rank].set(gathered), 'own', spl...]
    all_to_all x0 -> x4, blocking collectives: none -> 138 us  [exchange(): lax.all_to_all(array, 'own', 0, 0, axis_index_groups=groups, tiled=True)]
    unnamed x9 -> x10, local copies, waits for them, and re-layouts: 41.9 us -> 3.65 us
    all_to_all x2 -> x0, starting transfers between devices: 34.6 us -> none  [the longest x1 18.6 us: local(): lax.all_to_all(key_buffer, 'own', split_axis=0, concat_axis=0, tiled=True)]
    scatter x3 -> x0, local copies, waits for them, and re-layouts: 11.5 us -> none  [the longest x1 7.13 us: local(): buffer.at[tile_owner, slot_rank].set(gathered)]
  transfers between devices with their start and end apart: 4 -> 1, of which waited for: 3 -> 1; matrix products, arithmetic and copies ran while one was open for 2% -> 0% of each run, Pallas kernels for 0% -> 0%
where the time goes in v1:
time: 188 us; the launch traced here: 187 us
  blocking collectives  138 us (73%)
  waiting for transfers between devices  24.3 us (13%)
  between operations  13.4 us (7%)
  Pallas kernels  7.23 us (4%)
  local copies, waits for them, and re-layouts  3.65 us (2%)
    all_to_all x4, blocking collectives, exchange(): lax.all_to_all(array, 'own', 0, 0, axis_index_groups=groups, tiled=True)  138 us
    all_gather x1, waiting for transfers between devices, local(): dense = lax.all_gather(mine, 'grp', axis=0)  24.3 us
  transfers between devices with their start and end apart: 1, of which 1 were waited for; matrix products, arithmetic and copies ran while one was open for 0% of the time, Pallas kernels for 0%

profile of v1, /device:TPU:6, one launch (start us, length us, event | category | flops | bytes accessed | tf_op | source)
XLA Modules:
  0.0 186.9 jit_solution(16007188080310993397)
XLA Ops:
  6.5 0.0 all-gather.3.cloned.1.call-start
  6.5 0.0 copy-start.2
  6.5 0.9 copy-done.2
  7.5 0.0 copy-start.3
  7.5 0.7 copy-done.3
  8.1 0.0 copy-start.4
  8.1 0.7 copy-done.4
  8.8 1.7 shard_map.46
  10.4 0.0 copy-start
  10.5 14.5 %all_to_all.20.refs_0_ = bf16[4,34,16,128]{3,2,1,0:T(8,128)(2,1)S(1)} all-to-all(bf16[4,34,16,128]{3,2,1,0:T(8,128)(2,1)S(1)} %shard_map.46), channel_id=1, replica_groups={{0,1,2,3},{4,5,6,7},{8,9,10,11},{12,13,14,15},{16,17,18,19},{20,21,22,2..., dimensions={0} | all-to-all | bytes 1114112 | tf_op jit(solution)/shard_map/all_to_all | solution.py:168
  25.0 0.1 shard_map.47
  25.1 46.6 %all_to_all.21.refs_0_ = bf16[16,9,16,128]{3,2,1,0:T(8,128)(2,1)S(1)} all-to-all(bf16[16,9,16,128]{3,2,1,0:T(8,128)(2,1)S(1)} %shard_map.47), channel_id=1, replica_groups={{0,4,8,12,16,20,24,28,32,36,40,44,48,52,56,60},{1,5,9,13,17,21,25,29,33..., dimensions={0} | all-to-all | bytes 1179648 | tf_op jit(solution)/shard_map/all_to_all | solution.py:168
  71.7 1.5 shard_map.48
  73.1 0.0 all-gather.3.cloned.1.call-update
  73.2 24.3 %all-gather.3.cloned.1.call-done = bf16[1024,768]{1,0:T(8,128)(2,1)} async-done(((bf16[128,768]{1,0:T(8,128)(2,1)}), bf16[1024,768]{1,0:T(8,128)(2,1)}) %all-gather.3.cloned.1.call-update) | async-done | bytes 1572880 | tf_op jit(solution)/shard_map/all_gather | solution.py:202
  97.5 0.0 copy-done
  97.5 0.0 copy-start.1
  97.5 1.4 copy-done.1
  98.9 2.4 %shard_map.49 = s16[4,272,1024]{2,1,0:T(8,128)(2,1)S(1)} custom-call(bf16[8,128,768]{2,1,0:T(8,128)(2,1)S(1)} %bitcast.1, bf16[768,1024]{1,0:T(8,128)(2,1)S(1)} %copy-done), custom_call_target="tpu_custom_call" | custom-call | tf_op jit(solution)/shard_map/pallas_call | solution.py:205
  101.3 30.7 %all_to_all.22.refs_0_ = s16[4,272,1024]{2,1,0:T(8,128)(2,1)S(1)} all-to-all(s16[4,272,1024]{2,1,0:T(8,128)(2,1)S(1)} %shard_map.49), channel_id=1, replica_groups={{0,1,2,3},{4,5,6,7},{8,9,10,11},{12,13,14,15},{16,17,18,19},{20,21,22,2..., dimensions={0} | all-to-all | bytes 4456448 | tf_op jit(solution)/shard_map/all_to_all | solution.py:168
  132.0 0.8 shard_map.50
  132.8 46.4 %all_to_all.23.got = s16[16,144,128]{2,1,0:T(8,128)(2,1)S(1)} all-to-all(s16[16,144,128]{2,1,0:T(8,128)(2,1)S(1)} %shard_map.50), channel_id=1, replica_groups={{0,4,8,12,16,20,24,28,32,36,40,44,48,52,56,60},{1,5,9,13,17,21,25,29,33..., dimensions={0} | all-to-all | bytes 1179648 | tf_op jit(solution)/shard_map/all_to_all | solution.py:168
  179.2 0.8 shard_map.51
Async XLA Ops:
  6.5 90.9 %all-gather.3.cloned.1.call-start = ((), (), s32[]{:S(2)}) async-start(), calls=%async_computation.4 | async-start | bytes 1769472 | tf_op jit(solution)/shard_map/all_gather | solution.py:202
  6.5 0.9 copy-start.2
  7.5 0.7 copy-start.3
  8.1 0.7 copy-start.4
  10.4 87.0 %copy-start = (bf16[768,1024]{1,0:T(8,128)(2,1)S(1)}, bf16[768,1024]{1,0:T(8,128)(2,1)}, u32[]{:S(2)}) copy-start(bf16[768,1024]{1,0:T(8,128)(2,1)} %v.1) | copy-start | bytes 4718596
  97.5 1.4 copy-start.1
Sparse Core Ops, SparseCore 0:
  73.3 24.1 all-gather.2

commit v2 on v0

v2 whole, which is shorter than its diff:
```python
import jax
import jax.numpy as jnp
from jax import lax
from jax.experimental import pallas as pl
from jax.experimental.pallas import tpu as pltpu
from jax.sharding import PartitionSpec as P

NB = 8
CAP = 2
NX = 4
CHUNKS = 2
CORES = 2
LOWS = 4
TOP = 32767.0
STEPS = 64.0
TINY = 1e-30
VMEM = pl.BlockSpec(memory_space=pltpu.VMEM)
SMEM = pl.BlockSpec(memory_space=pltpu.SMEM)
PARAMS = pltpu.CompilerParams(vmem_limit_bytes=40 << 20)


def code_of(largest):
    return jnp.ceil(jnp.log2(jnp.maximum(largest, TINY)) * STEPS)


def coded(values, code):
    scaled = values * (jnp.exp2(code * (-1.0 / STEPS)) * (TOP - 1.0))
    return jnp.round(scaled).astype(jnp.int32).astype(jnp.int16)


def scale_of(code16):
    code = code16.astype(jnp.int32).astype(jnp.float32)
    return jnp.exp2(code * (1.0 / STEPS)) * (1.0 / (TOP - 1.0))


def plain(values16):
    return values16.astype(jnp.int32).astype(jnp.float32)


def pack(tile_dev, amp, block, index, *refs):
    outs, (keys, count) = refs[:CHUNKS], refs[CHUNKS:]
    owners, lines, lanes = keys.shape

    def clear(o, _):
        count[o] = 0
        return 0

    lax.fori_loop(0, owners, clear, 0)
    keys[...] = jnp.full(keys.shape, -1.0, jnp.float32)
    occ = outs[0].shape[2]
    for r in range(amp.shape[0]):
        tile = index[r]
        owner = tile // tile_dev
        rank = count[owner]
        count[owner] = rank + 1
        key = block[r] * tile_dev + (tile - owner * tile_dev)
        for c, out in enumerate(outs):
            out[owner, rank] = amp[r, c * occ : (c + 1) * occ, :]
        keys[owner, pl.ds(rank, 1), :] = jnp.full((1, lanes), key, jnp.int32).astype(jnp.float32)
    for o in range(owners):
        outs[0][o, CAP] = keys[o].astype(outs[0].dtype)


def place(tile_dev, first, got, out, held, row, key, sem):
    sources, _, occ, width = got.shape
    line = lax.broadcasted_iota(jnp.int32, (occ, width), 0)
    lane = lax.broadcasted_iota(jnp.int32, (occ, width), 1)
    slot = jnp.where(line < CAP, lane - line, -1)
    marks = jnp.zeros((occ, width), jnp.float32)
    for s in range(sources):
        marks = jnp.where(slot == CAP * s, first[s, CAP].astype(jnp.float32), marks)
    row[...] = jnp.sum(marks, axis=0, keepdims=True).astype(jnp.int32)
    copy = pltpu.make_async_copy(row, key, sem)
    copy.start()
    copy.wait()
    spare = NB * tile_dev
    for s in range(sources):
        for r in range(CAP):
            k = key[0, s * CAP + r]
            held[jnp.where(k < 0, spare, k)] = got[s, r]
    for b in range(NB):
        for t in range(tile_dev):
            tile = held[b * tile_dev + t]
            for y in range(out.shape[0]):
                out[y, b * occ : (b + 1) * occ, t * width : (t + 1) * width] = tile


def multiply(mine, theirs, v, core, out):
    rows, cols = mine.shape[1], v.shape[1]
    parts = mine.shape[0] * CORES // NX
    for other, a in enumerate((mine, theirs)):
        c = core[0] if other == 0 else 1 - core[0]
        for even in range(NX // CORES):
            x = even * CORES + c
            sums = [
                jnp.dot(a[even + h * (NX // CORES)], v[...], preferred_element_type=jnp.float32)
                .reshape(rows // 8, 8, cols)
                for h in range(parts)
            ]
            code = None
            for p in sums:
                largest = jnp.max(jnp.abs(p), axis=0)
                code = largest if code is None else jnp.maximum(code, largest)
            code = code_of(code)
            for h, p in enumerate(sums):
                out[x, h * rows : (h + 1) * rows, :] = coded(p, code[None]).reshape(rows, cols)
            out[x, parts * rows : parts * rows + 8, :] = code.astype(jnp.int32).astype(jnp.int16)


def recoded(tiles, out, z):
    largest = jnp.abs(tiles[0])
    for tile in tiles[1:]:
        largest = jnp.maximum(largest, jnp.abs(tile))
    code = code_of(largest)
    lines = code.shape[0]
    for t, tile in enumerate([*tiles, None]):
        out[z, t * lines : (t + 1) * lines, :] = (
            code.astype(jnp.int32).astype(jnp.int16) if tile is None else coded(tile, code)
        )


def decoded(got, lines):
    sources, count = got.shape[0], got.shape[1] // lines - 1
    scales = [scale_of(got[s, count * lines :, :]) for s in range(sources)]
    tiles = []
    for t in range(count):
        total = None
        for s in range(sources):
            term = plain(got[s, t * lines : (t + 1) * lines, :]) * scales[s]
            total = term if total is None else total + term
        tiles.append(total)
    return tiles


def add_x(rows, got, out):
    parts = (got.shape[1] - 8) // rows
    cols = got.shape[2]
    occ = rows // NB
    lows = out.shape[0]
    scales = [scale_of(got[x, parts * rows : parts * rows + 8, :]) for x in range(NX)]
    tiles = [[] for _ in range(lows)]
    for b in range(NB):
        for h in range(parts):
            total = None
            at = h * rows + b * occ
            for x in range(NX):
                term = plain(got[x, at : at + occ, :]) * scales[x]
                total = term if total is None else total + term
            z = parts * b + h
            tiles[z % lows] += [total[:, 128 * t : 128 * (t + 1)] for t in range(cols // 128)]
    for low in range(lows):
        recoded(tiles[low], out, low)


def add_low(occ, got, out):
    tiles = decoded(got, occ)
    count = len(tiles) // out.shape[0]
    for high in range(out.shape[0]):
        recoded(tiles[high * count : (high + 1) * count], out, high)


def add_high(*refs):
    *gots, out = refs
    occ = out.shape[0] // len(gots)
    for c, got in enumerate(gots):
        for t, tile in enumerate(decoded(got, occ)):
            out[c * occ : (c + 1) * occ, 128 * t : 128 * (t + 1)] = tile


def call(body, out, ins, scratch=()):
    specs = [VMEM] * len(out) if isinstance(out, list) else VMEM
    return pl.pallas_call(
        body, out_shape=out, in_specs=ins, out_specs=specs, scratch_shapes=list(scratch), compiler_params=PARAMS
    )


def local(amplitudes, integrals, tile_block, tile_index):
    own, grp = lax.axis_size("own"), lax.axis_size("grp")
    nz, ny = own // NX, grp // CORES
    highs = nz // LOWS
    x_groups = [[z * NX + x for x in range(NX)] for z in range(nz)]
    low_groups = [[(high * LOWS + low) * NX + x for low in range(LOWS)] for high in range(highs) for x in range(NX)]
    high_groups = [[(high * LOWS + low) * NX + x for high in range(highs)] for low in range(LOWS) for x in range(NX)]
    y_groups = [[y * CORES + c for y in range(ny)] for c in range(CORES)]
    core_pairs = [(y * CORES + c, y * CORES + 1 - c) for y in range(ny) for c in range(CORES)]

    def exchange(array, groups=None, axis="own"):
        return lax.all_to_all(array, axis, 0, 0, axis_index_groups=groups, tiled=True)

    _, occ, width = amplitudes.shape
    occ = occ // CHUNKS
    tile_dev = integrals.shape[0] // width
    cols = integrals.shape[1]
    rows = NB * occ
    parts = grp // NX
    tiles = cols // 128
    dtype = amplitudes.dtype
    struct = jax.ShapeDtypeStruct
    core = jnp.reshape(lax.axis_index("grp") % CORES, (1,)).astype(jnp.int32)

    packed = call(
        lambda *refs: pack(tile_dev, *refs),
        [struct((own, CAP + (c == 0), occ, width), dtype) for c in range(CHUNKS)],
        [VMEM, SMEM, SMEM],
        [pltpu.VMEM((own, occ, width), jnp.float32), pltpu.SMEM((own,), jnp.int32)],
    )(amplitudes, tile_block, tile_index)
    moved = [exchange(part) for part in packed]
    sums = []
    for part in moved:
        copies = call(
            lambda *refs: place(tile_dev, *refs),
            struct((ny, rows, tile_dev * width), dtype),
            [VMEM, VMEM],
            [
                pltpu.VMEM((NB * tile_dev + 1, occ, width), dtype),
                pltpu.VMEM((1, width), jnp.int32),
                pltpu.SMEM((1, width), jnp.int32),
                pltpu.SemaphoreType.DMA,
            ],
        )(moved[0], part)
        mine = exchange(copies, y_groups, "grp")
        theirs = lax.ppermute(mine, "grp", core_pairs)
        sent = call(
            multiply, struct((NX, parts * rows + 8, cols), jnp.int16), [VMEM, VMEM, VMEM, SMEM]
        )(mine, theirs, integrals, core)
        sent = call(
            lambda *refs: add_x(rows, *refs), struct((LOWS, (highs * tiles + 1) * occ, 128), jnp.int16), [VMEM]
        )(exchange(sent, x_groups))
        sent = call(
            lambda *refs: add_low(occ, *refs), struct((highs, (tiles + 1) * occ, 128), jnp.int16), [VMEM]
        )(exchange(sent, low_groups))
        sums.append(exchange(sent, high_groups))
    return call(add_high, struct((occ * CHUNKS, cols), jnp.float32), [VMEM] * CHUNKS)(*sums)


def solution(mesh):
    return jax.shard_map(
        local,
        mesh=mesh,
        in_specs=(P("own", "grp", None), P("own", "grp"), P("own"), P("own")),
        out_specs=P("own", "grp"),
        check_vma=False,
    )
```

time: 995 us -> 197 us (0.20)
  waiting for transfers between devices: 880 us -> 50.8 us
  blocking collectives: 0 us -> 99 us
  local copies, waits for them, and re-layouts: 57.7 us -> 4.22 us
  between operations: 13.5 us -> 0.14 us
  Pallas kernels: 0 us -> 12.4 us
    reduce_scatter x1 -> x0, waiting for transfers between devices: 674 us -> none  [local(): lax.psum_scatter(jnp.dot(placed.reshape(row_count, tile_dev * tile_width)...]
    all_to_all x2 -> x6, waiting for transfers between devices: 189 us -> 49.1 us  [exchange(): lax.all_to_all(array, axis, 0, 0, axis_index_groups=groups, tiled=True)]
    all_to_all x0 -> x4, blocking collectives: none -> 99 us  [exchange(): lax.all_to_all(array, axis, 0, 0, axis_index_groups=groups, tiled=True)]
    unnamed x9 -> x12, local copies, waits for them, and re-layouts: 41.9 us -> 4.22 us
    all_gather x1 -> x0, waiting for transfers between devices: 16.4 us -> none  [local(): gathered = lax.all_gather(amplitudes, 'grp', axis=1, tiled=True)]
    pallas_call x0 -> x10, Pallas kernels: none -> 12.4 us  [the longest x2 4.81 us: local(): call(multiply, struct((NX, parts * rows + 8, cols), jnp.int16), [VMEM, VM...]
    scatter x3 -> x0, local copies, waits for them, and re-layouts: 11.5 us -> none  [the longest x1 7.13 us: local(): buffer.at[tile_owner, slot_rank].set(gathered)]
    all_to_all x2 -> x6, starting transfers between devices: 34.6 us -> 25 us  [exchange(): lax.all_to_all(array, axis, 0, 0, axis_index_groups=groups, tiled=True)]
  transfers between devices with their start and end apart: 4 -> 8, of which waited for: 3 -> 7; matrix products, arithmetic and copies ran while one was open for 2% -> 0% of each run, Pallas kernels for 0% -> 5%
where the time goes in v2:
time: 197 us; the launch traced here: 195 us
  blocking collectives  99 us (50%)
  waiting for transfers between devices  50.8 us (26%)
  starting transfers between devices  29 us (15%)
  Pallas kernels  12.4 us (6%)
  local copies, waits for them, and re-layouts  4.22 us (2%)
    all_to_all x4, blocking collectives, exchange(): lax.all_to_all(array, axis, 0, 0, axis_index_groups=groups, tiled=True)  99 us
    all_to_all x6, waiting for transfers between devices, exchange(): lax.all_to_all(array, axis, 0, 0, axis_index_groups=groups, tiled=True)  49.1 us
    all_to_all x6, starting transfers between devices, exchange(): lax.all_to_all(array, axis, 0, 0, axis_index_groups=groups, tiled=True)  25 us
    pallas_call x2, Pallas kernels, local(): call(multiply, struct((NX, parts * rows + 8, cols), jnp.int16), [VMEM, VM...  4.81 us
    unnamed x12, local copies, waits for them, and re-layouts  4.22 us
    ppermute x2, starting transfers between devices, local(): theirs = lax.ppermute(mine, 'grp', core_pairs)  3.95 us
  transfers between devices with their start and end apart: 8, of which 7 were waited for; matrix products, arithmetic and copies ran while one was open for 0% of the time, Pallas kernels for 5%

profile of v2, /device:TPU:6, one launch (start us, length us, event | category | flops | bytes accessed | tf_op | source)
XLA Modules:
  0.0 195.4 jit_solution(4392106568605872522)
XLA Ops:
  2.2 1.5 shard_map.46
  3.7 39.9 %all_to_all.50.refs_1_ = bf16[64,2,8,128]{3,2,1,0:T(8,128)(2,1)S(1)} all-to-all(bf16[64,2,8,128]{3,2,1,0:T(8,128)(2,1)S(1)} %get-tuple-element.8), channel_id=1, replica_groups=mesh['grp'=8,'own'=64] {'own'}, dimensions={0} | all-to-all | bytes 524288 | tf_op jit(solution)/shard_map/all_to_all | solution.py:188
  43.6 32.0 %all_to_all.51.refs_0_.refs_1_ = bf16[64,3,8,128]{3,2,1,0:T(8,128)(2,1)S(1)} all-to-all(bf16[64,3,8,128]{3,2,1,0:T(8,128)(2,1)S(1)} %get-tuple-element.7), channel_id=1, replica_groups=mesh['grp'=8,'own'=64] {'own'}, dimensions={0} | all-to-all | bytes 786432 | tf_op jit(solution)/shard_map/all_to_all | solution.py:188
  76.4 11.6 %all_to_all.52.mine = bf16[4,64,768]{2,1,0:T(8,128)(2,1)S(1)} all-to-all(bf16[4,64,768]{2,1,0:T(8,128)(2,1)S(1)} %shard_map.51), channel_id=1, replica_groups={{0,128,256,384},{64,192,320,448},{1,129,257,385},{65,193,321,449},{2,13..., dimensions={0} | all-to-all | bytes 786432 | tf_op jit(solution)/shard_map/all_to_all | solution.py:188
  88.0 2.0 %collective-permute-start.1 = (bf16[4,64,768]{2,1,0:T(8,128)(2,1)S(1)}, bf16[4,64,768]{2,1,0:T(8,128)(2,1)S(1)}, u32[]{:S(2)}, u32[]{:S(2)}) collective-permute-start(bf16[4,64,768]{2,1,0:T(8,128)(2,1)S(1)} %all_to_all.52.mine), channel_id=1, source_target_pairs={{0,64},{64,0},{128,192},{192,128},{256,320},{320,256},{384,448},{4... | collective-permute-start | bytes 1179656 | tf_op jit(solution)/shard_map/ppermute | solution.py:222
  90.1 1.6 shard_map.47
  91.6 3.5 %all-to-all-start.1 = ((bf16[4,64,768]{2,1,0:T(8,128)(2,1)}), bf16[4,64,768]{2,1,0:T(8,128)(2,1)S(1)}, u32[]{:S(2)}, u32[]{:S(2)}) async-start(bf16[4,64,768]{2,1,0:T(8,128)(2,1)} %shard_map.47), calls=%async_computation.1 | async-start | bytes 786432 | tf_op jit(solution)/shard_map/all_to_all | solution.py:188
  95.2 2.4 %shard_map.52 = s16[4,136,1024]{2,1,0:T(8,128)(2,1)S(1)} custom-call(bf16[4,64,768]{2,1,0:T(8,128)(2,1)S(1)} %all_to_all.52.mine, bf16[4,64,768]{2,1,0:T(8,128)(2,1)S(1)} %collective-permute-done.1.theirs, bf16[768,1024]{1,0:T(8,128)(2,1)S(1)} %copy-done, s32[1]{0:T(128)} %bitcast.core), custom_call_target="tpu_custom_call" | custom-call | tf_op jit(solution)/shard_map/pallas_call | solution.py:223
  98.6 5.5 %all-to-all-done.1.mine = bf16[4,64,768]{2,1,0:T(8,128)(2,1)S(1)} async-done(((bf16[4,64,768]{2,1,0:T(8,128)(2,1)}), bf16[4,64,768]{2,1,0:T(8,128)(2,1)S(1)}, u32[]{:S(2)}, u32[]{:S(2)}) %all-to-all-start.1) | async-done | bytes 393248 | tf_op jit(solution)/shard_map/all_to_all | solution.py:188
  104.1 4.8 %all-to-all-start.7 = ((s16[4,136,1024]{2,1,0:T(8,128)(2,1)}), s16[4,136,1024]{2,1,0:T(8,128)(2,1)S(1)}, u32[]{:S(2)}, u32[]{:S(2)}) async-start(s16[4,136,1024]{2,1,0:T(8,128)(2,1)} %copy-done.1), calls=%async_computation.7 | async-start | bytes 2228224 | tf_op jit(solution)/shard_map/all_to_all | solution.py:188
  108.9 1.9 collective-permute-start
  110.8 1.7 collective-permute-done.theirs
  112.5 2.4 %shard_map.48 = s16[4,136,1024]{2,1,0:T(8,128)(2,1)S(1)} custom-call(bf16[4,64,768]{2,1,0:T(8,128)(2,1)S(1)} %all-to-all-done.1.mine, bf16[4,64,768]{2,1,0:T(8,128)(2,1)S(1)} %collective-permute-done.theirs, bf16[768,1024]{1,0:T(8,128)(2,1)S(1)} %copy-done, s32[1]{0:T(128)} %bitcast.core), custom_call_target="tpu_custom_call" | custom-call | tf_op jit(solution)/shard_map/pallas_call | solution.py:223
  115.9 6.8 %all-to-all-done.7.refs_0_ = s16[4,136,1024]{2,1,0:T(8,128)(2,1)S(1)} async-done(((s16[4,136,1024]{2,1,0:T(8,128)(2,1)}), s16[4,136,1024]{2,1,0:T(8,128)(2,1)S(1)}, u32[]{:S(2)}, u32[]{:S(2)}) %all-to-all-start.7) | async-done | bytes 1114144 | tf_op jit(solution)/shard_map/all_to_all | solution.py:188
  122.7 5.6 %all-to-all-start.2 = ((s16[4,136,1024]{2,1,0:T(8,128)(2,1)}), s16[4,136,1024]{2,1,0:T(8,128)(2,1)S(1)}, u32[]{:S(2)}, u32[]{:S(2)}) async-start(s16[4,136,1024]{2,1,0:T(8,128)(2,1)} %copy-done.2), calls=%async_computation.2 | async-start | bytes 2228224 | tf_op jit(solution)/shard_map/all_to_all | solution.py:188
  128.2 1.1 shard_map.53
  129.3 11.8 %all-to-all-done.2.refs_0_ = s16[4,136,1024]{2,1,0:T(8,128)(2,1)S(1)} async-done(((s16[4,136,1024]{2,1,0:T(8,128)(2,1)}), s16[4,136,1024]{2,1,0:T(8,128)(2,1)S(1)}, u32[]{:S(2)}, u32[]{:S(2)}) %all-to-all-start.2) | async-done | bytes 1114144 | tf_op jit(solution)/shard_map/all_to_all | solution.py:188
  141.1 3.4 %all-to-all-start.8 = ((s16[4,264,128]{2,1,0:T(8,128)(2,1)}), s16[4,264,128]{2,1,0:T(8,128)(2,1)S(1)}, u32[]{:S(2)}, u32[]{:S(2)}) async-start(s16[4,264,128]{2,1,0:T(8,128)(2,1)} %shard_map.53), calls=%async_computation.8 | async-start | bytes 540672 | tf_op jit(solution)/shard_map/all_to_all | solution.py:188
  145.7 5.7 %all-to-all-done.8.refs_0_ = s16[4,264,128]{2,1,0:T(8,128)(2,1)S(1)} async-done(((s16[4,264,128]{2,1,0:T(8,128)(2,1)}), s16[4,264,128]{2,1,0:T(8,128)(2,1)S(1)}, u32[]{:S(2)}, u32[]{:S(2)}) %all-to-all-start.8) | async-done | bytes 270368 | tf_op jit(solution)/shard_map/all_to_all | solution.py:188
  151.4 3.5 %all-to-all-start.3 = ((s16[4,264,128]{2,1,0:T(8,128)(2,1)}), s16[4,264,128]{2,1,0:T(8,128)(2,1)S(1)}, u32[]{:S(2)}, u32[]{:S(2)}) async-start(s16[4,264,128]{2,1,0:T(8,128)(2,1)} %shard_map.49), calls=%async_computation.3 | async-start | bytes 540672 | tf_op jit(solution)/shard_map/all_to_all | solution.py:188
  155.6 6.1 %all-to-all-done.3.refs_0_ = s16[4,264,128]{2,1,0:T(8,128)(2,1)S(1)} async-done(((s16[4,264,128]{2,1,0:T(8,128)(2,1)}), s16[4,264,128]{2,1,0:T(8,128)(2,1)S(1)}, u32[]{:S(2)}, u32[]{:S(2)}) %all-to-all-start.3) | async-done | bytes 270368 | tf_op jit(solution)/shard_map/all_to_all | solution.py:188
  161.7 4.3 %all-to-all-start.9 = ((s16[4,72,128]{2,1,0:T(8,128)(2,1)}), s16[4,72,128]{2,1,0:T(8,128)(2,1)S(1)}, u32[]{:S(2)}, u32[]{:S(2)}) async-start(s16[4,72,128]{2,1,0:T(8,128)(2,1)} %shard_map.54), calls=%async_computation.9 | async-start | bytes 147456 | tf_op jit(solution)/shard_map/all_to_all | solution.py:188
  166.1 13.2 %all-to-all-done.9.refs_1_ = s16[4,72,128]{2,1,0:T(8,128)(2,1)S(1)} async-done(((s16[4,72,128]{2,1,0:T(8,128)(2,1)}), s16[4,72,128]{2,1,0:T(8,128)(2,1)S(1)}, u32[]{:S(2)}, u32[]{:S(2)}) %all-to-all-start.9) | async-done | bytes 73760 | tf_op jit(solution)/shard_map/all_to_all | solution.py:188
  179.3 15.5 %all_to_all.53.refs_0_ = s16[4,72,128]{2,1,0:T(8,128)(2,1)S(1)} all-to-all(s16[4,72,128]{2,1,0:T(8,128)(2,1)S(1)} %shard_map.50), channel_id=1, replica_groups={{0,16,32,48},{1,17,33,49},{2,18,34,50},{3,19,35,51},{4,20,36,52},{5,21,..., dimensions={0} | all-to-all | bytes 147456 | tf_op jit(solution)/shard_map/all_to_all | solution.py:188
  (18 shorter events, 7.7 us)
Async XLA Ops:
  0.0 0.9 copy-start.3
  0.9 0.7 copy-start.4
  1.6 0.7 copy-start.5
  88.0 7.1 %copy-start = (bf16[768,1024]{1,0:T(8,128)(2,1)S(1)}, bf16[768,1024]{1,0:T(8,128)(2,1)}, u32[]{:S(2)}) copy-start(bf16[768,1024]{1,0:T(8,128)(2,1)} %v.3) | copy-start | bytes 4718596
  88.0 7.1 %collective-permute-start.1 = (bf16[4,64,768]{2,1,0:T(8,128)(2,1)S(1)}, bf16[4,64,768]{2,1,0:T(8,128)(2,1)S(1)}, u32[]{:S(2)}, u32[]{:S(2)}) collective-permute-start(bf16[4,64,768]{2,1,0:T(8,128)(2,1)S(1)} %all_to_all.52.mine), channel_id=1, source_target_pairs={{0,64},{64,0},{128,192},{192,128},{256,320},{320,256},{384,448},{4... | collective-permute-start | bytes 1179656 | tf_op jit(solution)/shard_map/ppermute | solution.py:222
  91.6 12.5 %all-to-all-start.1 = ((bf16[4,64,768]{2,1,0:T(8,128)(2,1)}), bf16[4,64,768]{2,1,0:T(8,128)(2,1)S(1)}, u32[]{:S(2)}, u32[]{:S(2)}) async-start(bf16[4,64,768]{2,1,0:T(8,128)(2,1)} %shard_map.47), calls=%async_computation.1 | async-start | bytes 786432 | tf_op jit(solution)/shard_map/all_to_all | solution.py:188
  97.6 1.0 copy-start.1
  104.1 18.6 %all-to-all-start.7 = ((s16[4,136,1024]{2,1,0:T(8,128)(2,1)}), s16[4,136,1024]{2,1,0:T(8,128)(2,1)S(1)}, u32[]{:S(2)}, u32[]{:S(2)}) async-start(s16[4,136,1024]{2,1,0:T(8,128)(2,1)} %copy-done.1), calls=%async_computation.7 | async-start | bytes 2228224 | tf_op jit(solution)/shard_map/all_to_all | solution.py:188
  108.9 3.6 %collective-permute-start = (bf16[4,64,768]{2,1,0:T(8,128)(2,1)S(1)}, bf16[4,64,768]{2,1,0:T(8,128)(2,1)S(1)}, u32[]{:S(2)}, u32[]{:S(2)}) collective-permute-start(bf16[4,64,768]{2,1,0:T(8,128)(2,1)S(1)} %all-to-all-done.1.mine), channel_id=1, source_target_pairs={{0,64},{64,0},{128,192},{192,128},{256,320},{320,256},{384,448},{4... | collective-permute-start | bytes 1179656 | tf_op jit(solution)/shard_map/ppermute | solution.py:222
  114.9 1.0 copy-start.2
  122.7 18.4 %all-to-all-start.2 = ((s16[4,136,1024]{2,1,0:T(8,128)(2,1)}), s16[4,136,1024]{2,1,0:T(8,128)(2,1)S(1)}, u32[]{:S(2)}, u32[]{:S(2)}) async-start(s16[4,136,1024]{2,1,0:T(8,128)(2,1)} %copy-done.2), calls=%async_computation.2 | async-start | bytes 2228224 | tf_op jit(solution)/shard_map/all_to_all | solution.py:188
  141.1 10.3 %all-to-all-start.8 = ((s16[4,264,128]{2,1,0:T(8,128)(2,1)}), s16[4,264,128]{2,1,0:T(8,128)(2,1)S(1)}, u32[]{:S(2)}, u32[]{:S(2)}) async-start(s16[4,264,128]{2,1,0:T(8,128)(2,1)} %shard_map.53), calls=%async_computation.8 | async-start | bytes 540672 | tf_op jit(solution)/shard_map/all_to_all | solution.py:188
  151.4 10.3 %all-to-all-start.3 = ((s16[4,264,128]{2,1,0:T(8,128)(2,1)}), s16[4,264,128]{2,1,0:T(8,128)(2,1)S(1)}, u32[]{:S(2)}, u32[]{:S(2)}) async-start(s16[4,264,128]{2,1,0:T(8,128)(2,1)} %shard_map.49), calls=%async_computation.3 | async-start | bytes 540672 | tf_op jit(solution)/shard_map/all_to_all | solution.py:188
  161.7 17.6 %all-to-all-start.9 = ((s16[4,72,128]{2,1,0:T(8,128)(2,1)}), s16[4,72,128]{2,1,0:T(8,128)(2,1)S(1)}, u32[]{:S(2)}, u32[]{:S(2)}) async-start(s16[4,72,128]{2,1,0:T(8,128)(2,1)} %shard_map.54), calls=%async_computation.9 | async-start | bytes 147456 | tf_op jit(solution)/shard_map/all_to_all | solution.py:188

commit v3 on v2

v3 whole, which is shorter than its diff:
```python
import jax
import jax.numpy as jnp
from jax import lax
from jax.experimental import pallas as pl
from jax.experimental.pallas import tpu as pltpu
from jax.sharding import PartitionSpec as P

NB = 8
CAP = 2
NX = 4
UNIT = 8
CORES = 2
LOWS = 4
TOP = 32767.0
STEPS = 64.0
TINY = 1e-30
VMEM = pl.BlockSpec(memory_space=pltpu.VMEM)
SMEM = pl.BlockSpec(memory_space=pltpu.SMEM)
PARAMS = pltpu.CompilerParams(vmem_limit_bytes=40 << 20)


def code_of(largest):
    return jnp.ceil(jnp.log2(jnp.maximum(largest, TINY)) * STEPS)


def coded(values, code):
    scaled = values * (jnp.exp2(code * (-1.0 / STEPS)) * (TOP - 1.0))
    return jnp.round(scaled).astype(jnp.int32).astype(jnp.int16)


def scale_of(code16):
    code = code16.astype(jnp.int32).astype(jnp.float32)
    return jnp.exp2(code * (1.0 / STEPS)) * (1.0 / (TOP - 1.0))


def plain(values16):
    return values16.astype(jnp.int32).astype(jnp.float32)


def pack(tile_dev, amp, block, index, out, keys, count):
    owners, _, lanes = keys.shape
    units = amp.shape[1] // UNIT

    def clear(o, _):
        count[o] = 0
        return 0

    lax.fori_loop(0, owners, clear, 0)
    keys[...] = jnp.full(keys.shape, -1.0, jnp.float32)
    for r in range(amp.shape[0]):
        tile = index[r]
        owner = tile // tile_dev
        rank = count[owner]
        count[owner] = rank + 1
        key = block[r] * tile_dev + (tile - owner * tile_dev)
        for u in range(units):
            out[owner, rank * units + u] = amp[r, u * UNIT : (u + 1) * UNIT, :]
        keys[owner, pl.ds(rank, 1), :] = jnp.full((1, lanes), key, jnp.int32).astype(jnp.float32)
    for o in range(owners):
        out[o, CAP * units] = keys[o].astype(out.dtype)


def place(tile_dev, got, out, held, row, key, sem):
    sources, units, _, width = got.shape
    units = (units - 1) // CAP
    line = lax.broadcasted_iota(jnp.int32, (UNIT, width), 0)
    lane = lax.broadcasted_iota(jnp.int32, (UNIT, width), 1)
    slot = jnp.where(line < CAP, lane - line, -1)
    marks = jnp.zeros((UNIT, width), jnp.float32)
    for s in range(sources):
        marks = jnp.where(slot == CAP * s, got[s, CAP * units].astype(jnp.float32), marks)
    row[...] = jnp.sum(marks, axis=0, keepdims=True).astype(jnp.int32)
    copy = pltpu.make_async_copy(row, key, sem)
    copy.start()
    copy.wait()
    spare = NB * tile_dev
    for s in range(sources):
        for r in range(CAP):
            k = key[0, s * CAP + r]
            to = jnp.where(k < 0, spare, k)
            for u in range(units):
                held[to, u] = got[s, r * units + u]
    for b in range(NB):
        for t in range(tile_dev):
            for u in range(units):
                tile = held[b * tile_dev + t, u]
                at = (b * units + u) * UNIT
                for y in range(out.shape[0]):
                    out[y, at : at + UNIT, t * width : (t + 1) * width] = tile


def multiply(a, mine, theirs, which, out):
    rows, cols = a.shape[1], out.shape[1]
    half = NX // CORES

    def block(v):
        sums = [
            jnp.dot(a[which[0] + half * h], v[...], preferred_element_type=jnp.float32).reshape(rows // 8, 8, cols)
            for h in range(a.shape[0] // half)
        ]
        largest = None
        for p in sums:
            top = jnp.max(jnp.abs(p), axis=0)
            largest = top if largest is None else jnp.maximum(largest, top)
        code = code_of(largest)
        for h, p in enumerate(sums):
            out[h * rows : (h + 1) * rows, :] = coded(p, code[None]).reshape(rows, cols)
        out[len(sums) * rows :, :] = code.astype(jnp.int32).astype(jnp.int16)

    @pl.when(which[1] == 0)
    def _():
        block(mine)

    @pl.when(which[1] != 0)
    def _():
        block(theirs)


def recoded(tiles, out, z):
    largest = jnp.abs(tiles[0])
    for tile in tiles[1:]:
        largest = jnp.maximum(largest, jnp.abs(tile))
    code = code_of(largest)
    lines = code.shape[0]
    for t, tile in enumerate([*tiles, None]):
        out[z, t * lines : (t + 1) * lines, :] = (
            code.astype(jnp.int32).astype(jnp.int16) if tile is None else coded(tile, code)
        )


def decoded(got, lines):
    sources, count = got.shape[0], got.shape[1] // lines - 1
    scales = [scale_of(got[s, count * lines :, :]) for s in range(sources)]
    tiles = []
    for t in range(count):
        total = None
        for s in range(sources):
            term = plain(got[s, t * lines : (t + 1) * lines, :]) * scales[s]
            total = term if total is None else total + term
        tiles.append(total)
    return tiles


def add_x(rows, *refs):
    *gots, out = refs
    parts = (gots[0].shape[0] - 8) // rows
    cols = gots[0].shape[1]
    occ = rows // NB
    lows = out.shape[0]
    scales = [scale_of(got[parts * rows :, :]) for got in gots]
    tiles = [[] for _ in range(lows)]
    for b in range(NB):
        for h in range(parts):
            z = parts * b + h
            for u in range(occ // UNIT):
                total = None
                at = h * rows + b * occ + u * UNIT
                for got, scale in zip(gots, scales):
                    term = plain(got[at : at + UNIT, :]) * scale
                    total = term if total is None else total + term
                tiles[z % lows] += [total[:, 128 * t : 128 * (t + 1)] for t in range(cols // 128)]
    for low in range(lows):
        recoded(tiles[low], out, low)


def add_low(got, out):
    tiles = decoded(got, UNIT)
    count = len(tiles) // out.shape[0]
    for high in range(out.shape[0]):
        recoded(tiles[high * count : (high + 1) * count], out, high)


def add_high(got, out):
    lanes = out.shape[1] // 128
    for n, tile in enumerate(decoded(got, UNIT)):
        u, t = n // lanes, n % lanes
        out[u * UNIT : (u + 1) * UNIT, 128 * t : 128 * (t + 1)] = tile


def call(body, out, ins, scratch=()):
    specs = [VMEM] * len(out) if isinstance(out, list) else VMEM
    return pl.pallas_call(
        body, out_shape=out, in_specs=ins, out_specs=specs, scratch_shapes=list(scratch), compiler_params=PARAMS
    )


def local(amplitudes, integrals, tile_block, tile_index):
    own, grp = lax.axis_size("own"), lax.axis_size("grp")
    nz, ny = own // NX, grp // CORES
    highs, half = nz // LOWS, NX // CORES
    low_groups = [[(high * LOWS + low) * NX + x for low in range(LOWS)] for high in range(highs) for x in range(NX)]
    high_groups = [[(high * LOWS + low) * NX + x for high in range(highs)] for low in range(LOWS) for x in range(NX)]
    y_groups = [[y * CORES + c for y in range(ny)] for c in range(CORES)]
    core_pairs = [(y * CORES + c, y * CORES + 1 - c) for y in range(ny) for c in range(CORES)]

    def target(r, x):
        return (r // CORES) ^ (x // CORES), (r % CORES) ^ (x % CORES)

    def round_pairs(r):
        pairs = []
        for g in range(grp):
            for o in range(own):
                y, c, z, x = g // CORES, g % CORES, o // NX, o % NX
                a, to = target(r, x)
                pairs.append((g * own + o, (y * CORES + to) * own + z * NX + a * CORES + c))
        return pairs

    def exchange(array, groups=None, axis="own"):
        return lax.all_to_all(array, axis, 0, 0, axis_index_groups=groups, tiled=True)

    _, occ, width = amplitudes.shape
    units = occ // UNIT
    tile_dev = integrals.shape[0] // width
    cols = integrals.shape[1]
    rows = NB * occ
    parts = grp // NX
    tiles = cols // 128
    dtype = amplitudes.dtype
    struct = jax.ShapeDtypeStruct
    core = lax.axis_index("grp") % CORES
    x = lax.axis_index("own") % NX

    packed = call(
        lambda *refs: pack(tile_dev, *refs),
        struct((own, CAP * units + 1, UNIT, width), dtype),
        [VMEM, SMEM, SMEM],
        [pltpu.VMEM((own, UNIT, width), jnp.float32), pltpu.SMEM((own,), jnp.int32)],
    )(amplitudes, tile_block, tile_index)
    theirs = lax.ppermute(integrals, "grp", core_pairs)
    copies = call(
        lambda *refs: place(tile_dev, *refs),
        struct((ny, rows, tile_dev * width), dtype),
        [VMEM],
        [
            pltpu.VMEM((NB * tile_dev + 1, units, UNIT, width), dtype),
            pltpu.VMEM((1, width), jnp.int32),
            pltpu.SMEM((1, width), jnp.int32),
            pltpu.SemaphoreType.DMA,
        ],
    )(exchange(packed))
    mine = exchange(copies, y_groups, "grp")
    gots = []
    for r in range(half * CORES):
        a, to = target(r, x)
        which = jnp.stack([a, to ^ core]).astype(jnp.int32)
        sent = call(multiply, struct((parts * rows + 8, cols), jnp.int16), [VMEM, VMEM, VMEM, SMEM])(
            mine, integrals, theirs, which
        )
        gots.append(lax.ppermute(sent, ("grp", "own"), round_pairs(r)))
    sent = call(
        lambda *refs: add_x(rows, *refs),
        struct((LOWS, (highs * units * tiles + 1) * UNIT, 128), jnp.int16),
        [VMEM] * len(gots),
    )(*gots)
    sent = call(add_low, struct((highs, (units * tiles + 1) * UNIT, 128), jnp.int16), [VMEM])(
        exchange(sent, low_groups)
    )
    return call(add_high, struct((occ, cols), jnp.float32), [VMEM])(exchange(sent, high_groups))


def solution(mesh):
    return jax.shard_map(
        local,
        mesh=mesh,
        in_specs=(P("own", "grp", None), P("own", "grp"), P("own"), P("own")),
        out_specs=P("own", "grp"),
        check_vma=False,
    )
```

time: 197 us -> 156 us (0.79)
  blocking collectives: 99 us -> 38 us
  waiting for transfers between devices: 50.8 us -> 63.3 us
  starting transfers between devices: 29 us -> 37.6 us
    all_to_all x4 -> x2, blocking collectives: 99 us -> 38 us  [exchange(): lax.all_to_all(array, axis, 0, 0, axis_index_groups=groups, tiled=True)]
    ppermute x2 -> x5, waiting for transfers between devices: 1.69 us -> 15.9 us  [the longest x4 15.9 us: local(): gots.append(lax.ppermute(sent, ('grp', 'own'), round_pairs(r)))]
    ppermute x2 -> x5, starting transfers between devices: 3.95 us -> 14.4 us  [the longest x4 12.4 us: local(): gots.append(lax.ppermute(sent, ('grp', 'own'), round_pairs(r)))]
    all_to_all x6 -> x2, starting transfers between devices: 25 us -> 23.2 us  [exchange(): lax.all_to_all(array, axis, 0, 0, axis_index_groups=groups, tiled=True)]
    all_to_all x6 -> x2, waiting for transfers between devices: 49.1 us -> 47.4 us  [exchange(): lax.all_to_all(array, axis, 0, 0, axis_index_groups=groups, tiled=True)]
    unnamed x12 -> x10, local copies, waits for them, and re-layouts: 4.22 us -> 3.15 us
  transfers between devices with their start and end apart: 8 -> 7, of which waited for: 7 -> 5; matrix products, arithmetic and copies ran while one was open for 0% -> 0% of each run, Pallas kernels for 5% -> 5%
where the time goes in v3:
time: 156 us
  waiting for transfers between devices  63.3 us (41%)
  blocking collectives  38 us (24%)
  starting transfers between devices  37.6 us (24%)
  Pallas kernels  13.2 us (8%)
  local copies, waits for them, and re-layouts  3.15 us (2%)
    all_to_all x2, waiting for transfers between devices, exchange(): lax.all_to_all(array, axis, 0, 0, axis_index_groups=groups, tiled=True)  47.4 us
    all_to_all x2, blocking collectives, exchange(): lax.all_to_all(array, axis, 0, 0, axis_index_groups=groups, tiled=True)  38 us
    all_to_all x2, starting transfers between devices, exchange(): lax.all_to_all(array, axis, 0, 0, axis_index_groups=groups, tiled=True)  23.2 us
    ppermute x4, waiting for transfers between devices, local(): gots.append(lax.ppermute(sent, ('grp', 'own'), round_pairs(r)))  15.9 us
    ppermute x4, starting transfers between devices, local(): gots.append(lax.ppermute(sent, ('grp', 'own'), round_pairs(r)))  12.4 us
    pallas_call x4, Pallas kernels, local(): call(multiply, struct((parts * rows + 8, cols), jnp.int16), [VMEM, VMEM,...  7.33 us
    unnamed x10, local copies, waits for them, and re-layouts  3.15 us
  transfers between devices with their start and end apart: 7, of which 5 were waited for; matrix products, arithmetic and copies ran while one was open for 0% of the time, Pallas kernels for 5%

profile of v3, /device:TPU:6, one launch (start us, length us, event | category | flops | bytes accessed | tf_op | source)
XLA Modules:
  0.0 155.7 jit_solution(2549420023184788756)
XLA Ops:
  0.0 0.9 copy-done.2
  2.2 2.3 %shard_map.46 = bf16[64,5,8,128]{3,2,1,0:T(8,128)(2,1)} custom-call(bf16[48,16,128]{2,1,0:T(8,128)(2,1)S(1)} %copy-done.2, s32[48]{0:T(128)S(1)} %copy-done.3, s32[48]{0:T(128)S(1)} %copy-done.4), custom_call_target="tpu_custom_call" | custom-call | tf_op jit(solution)/shard_map/pallas_call | solution.py:223
  4.5 18.8 %all-to-all-start = ((bf16[64,5,8,128]{3,2,1,0:T(8,128)(2,1)}), bf16[64,5,8,128]{3,2,1,0:T(8,128)(2,1)}, u32[]{:S(2)}, u32[]{:S(2)}) async-start(bf16[64,5,8,128]{3,2,1,0:T(8,128)(2,1)} %shard_map.46), calls=%async_computation | async-start | bytes 1310720 | tf_op jit(solution)/shard_map/all_to_all | solution.py:209
  23.3 1.9 %collective-permute-start = (bf16[768,1024]{1,0:T(8,128)(2,1)S(1)}, bf16[768,1024]{1,0:T(8,128)(2,1)S(1)}, u32[]{:S(2)}, u32[]{:S(2)}) collective-permute-start(bf16[768,1024]{1,0:T(8,128)(2,1)S(1)} %copy-done), channel_id=1, source_target_pairs={{0,64},{64,0},{128,192},{192,128},{256,320},{320,256},{384,448},{4... | collective-permute-start | bytes 4718600 | tf_op jit(solution)/shard_map/ppermute | solution.py:229
  25.2 36.4 %all-to-all-done.refs_0_ = bf16[64,5,8,128]{3,2,1,0:T(8,128)(2,1)} async-done(((bf16[64,5,8,128]{3,2,1,0:T(8,128)(2,1)}), bf16[64,5,8,128]{3,2,1,0:T(8,128)(2,1)}, u32[]{:S(2)}, u32[]{:S(2)}) %all-to-all-start) | async-done | bytes 655392 | tf_op jit(solution)/shard_map/all_to_all | solution.py:209
  61.6 2.0 %shard_map.47 = bf16[4,128,768]{2,1,0:T(8,128)(2,1)S(1)} custom-call(bf16[64,5,8,128]{3,2,1,0:T(8,128)(2,1)} %all-to-all-done.refs_0_), custom_call_target="tpu_custom_call" | custom-call | tf_op jit(solution)/shard_map/pallas_call | solution.py:230
  63.5 0.9 copy-done.1
  64.5 4.5 %all-to-all-start.1 = ((bf16[4,128,768]{2,1,0:T(8,128)(2,1)}), bf16[4,128,768]{2,1,0:T(8,128)(2,1)}, u32[]{:S(2)}, u32[]{:S(2)}) async-start(bf16[4,128,768]{2,1,0:T(8,128)(2,1)} %copy-done.1), calls=%async_computation.1 | async-start | bytes 1572864 | tf_op jit(solution)/shard_map/all_to_all | solution.py:209
  69.2 11.1 %all-to-all-done.1.a = bf16[4,128,768]{2,1,0:T(8,128)(2,1)} async-done(((bf16[4,128,768]{2,1,0:T(8,128)(2,1)}), bf16[4,128,768]{2,1,0:T(8,128)(2,1)}, u32[]{:S(2)}, u32[]{:S(2)}) %all-to-all-start.1) | async-done | bytes 786464 | tf_op jit(solution)/shard_map/all_to_all | solution.py:209
  80.3 1.8 %shard_map.48 = s16[264,1024]{1,0:T(8,128)(2,1)S(1)} custom-call(bf16[4,128,768]{2,1,0:T(8,128)(2,1)} %all-to-all-done.1.a, bf16[768,1024]{1,0:T(8,128)(2,1)S(1)} %copy-done, bf16[768,1024]{1,0:T(8,128)(2,1)S(1)} %collective-permute-done.theirs, s32[2]{0:T(128)S(1)} %pad_add_fusion.1.which), custom_call_target="tpu_custom_call" | custom-call | tf_op jit(solution)/shard_map/pallas_call | solution.py:246
  82.1 1.9 %collective-permute-start.1 = (s16[264,1024]{1,0:T(8,128)(2,1)S(1)}, s16[264,1024]{1,0:T(8,128)(2,1)S(1)}, u32[]{:S(2)}, u32[]{:S(2)}) collective-permute-start(s16[264,1024]{1,0:T(8,128)(2,1)S(1)} %shard_map.48), channel_id=1, source_target_pairs={{0,0},{1,64},{2,2},{3,66},{4,4},{5,68},{6,6},{7,70},{8,8},{9,72},{... | collective-permute-start | bytes 1622024 | tf_op jit(solution)/shard_map/ppermute | solution.py:249
  84.0 1.8 %shard_map.49 = s16[264,1024]{1,0:T(8,128)(2,1)S(1)} custom-call(bf16[4,128,768]{2,1,0:T(8,128)(2,1)} %all-to-all-done.1.a, bf16[768,1024]{1,0:T(8,128)(2,1)S(1)} %copy-done, bf16[768,1024]{1,0:T(8,128)(2,1)S(1)} %collective-permute-done.theirs, s32[2]{0:T(128)S(1)} %pad_add_fusion.2.which), custom_call_target="tpu_custom_call" | custom-call | tf_op jit(solution)/shard_map/pallas_call | solution.py:246
  85.9 1.9 %collective-permute-start.2 = (s16[264,1024]{1,0:T(8,128)(2,1)S(1)}, s16[264,1024]{1,0:T(8,128)(2,1)S(1)}, u32[]{:S(2)}, u32[]{:S(2)}) collective-permute-start(s16[264,1024]{1,0:T(8,128)(2,1)S(1)} %shard_map.49), channel_id=1, source_target_pairs={{0,64},{1,0},{2,66},{3,2},{4,68},{5,4},{6,70},{7,6},{8,72},{9,8},{... | collective-permute-start | bytes 1622024 | tf_op jit(solution)/shard_map/ppermute | solution.py:249
  87.8 1.8 %shard_map.50 = s16[264,1024]{1,0:T(8,128)(2,1)S(1)} custom-call(bf16[4,128,768]{2,1,0:T(8,128)(2,1)} %all-to-all-done.1.a, bf16[768,1024]{1,0:T(8,128)(2,1)S(1)} %copy-done, bf16[768,1024]{1,0:T(8,128)(2,1)S(1)} %collective-permute-done.theirs, s32[2]{0:T(128)S(1)} %pad_add_fusion.which), custom_call_target="tpu_custom_call" | custom-call | tf_op jit(solution)/shard_map/pallas_call | solution.py:246
  89.7 2.1 %collective-permute-start.3 = (s16[264,1024]{1,0:T(8,128)(2,1)S(1)}, s16[264,1024]{1,0:T(8,128)(2,1)S(1)}, u32[]{:S(2)}, u32[]{:S(2)}) collective-permute-start(s16[264,1024]{1,0:T(8,128)(2,1)S(1)} %shard_map.50), channel_id=1, source_target_pairs={{0,2},{1,66},{2,0},{3,64},{4,6},{5,70},{6,4},{7,68},{8,10},{9,74},... | collective-permute-start | bytes 1622024 | tf_op jit(solution)/shard_map/ppermute | solution.py:249
  91.8 1.8 %shard_map.51 = s16[264,1024]{1,0:T(8,128)(2,1)S(1)} custom-call(bf16[4,128,768]{2,1,0:T(8,128)(2,1)} %all-to-all-done.1.a, bf16[768,1024]{1,0:T(8,128)(2,1)S(1)} %copy-done, bf16[768,1024]{1,0:T(8,128)(2,1)S(1)} %collective-permute-done.theirs, s32[2]{0:T(128)S(1)} %pad_add_fusion.3.which), custom_call_target="tpu_custom_call" | custom-call | tf_op jit(solution)/shard_map/pallas_call | solution.py:246
  93.6 6.5 %collective-permute-start.4 = (s16[264,1024]{1,0:T(8,128)(2,1)S(1)}, s16[264,1024]{1,0:T(8,128)(2,1)S(1)}, u32[]{:S(2)}, u32[]{:S(2)}) collective-permute-start(s16[264,1024]{1,0:T(8,128)(2,1)S(1)} %shard_map.51), channel_id=1, source_target_pairs={{0,66},{1,2},{2,64},{3,0},{4,70},{5,6},{6,68},{7,4},{8,74},{9,10},... | collective-permute-start | bytes 1622024 | tf_op jit(solution)/shard_map/ppermute | solution.py:249
  100.1 0.7 collective-permute-done.2.refs_1_
  100.9 12.3 %collective-permute-done.3.refs_2_ = s16[264,1024]{1,0:T(8,128)(2,1)S(1)} collective-permute-done((s16[264,1024]{1,0:T(8,128)(2,1)S(1)}, s16[264,1024]{1,0:T(8,128)(2,1)S(1)}, u32[]{:S(2)}, u32[]{:S(2)}) %collective-permute-start.3) | collective-permute-done | bytes 540704 | tf_op jit(solution)/shard_map/ppermute | solution.py:249
  113.1 2.9 %collective-permute-done.4.refs_3_ = s16[264,1024]{1,0:T(8,128)(2,1)S(1)} collective-permute-done((s16[264,1024]{1,0:T(8,128)(2,1)S(1)}, s16[264,1024]{1,0:T(8,128)(2,1)S(1)}, u32[]{:S(2)}, u32[]{:S(2)}) %collective-permute-start.4) | collective-permute-done | bytes 540704 | tf_op jit(solution)/shard_map/ppermute | solution.py:249
  116.0 0.8 shard_map.52
  116.8 19.6 %all_to_all.20.got = s16[4,520,128]{2,1,0:T(8,128)(2,1)S(1)} all-to-all(s16[4,520,128]{2,1,0:T(8,128)(2,1)S(1)} %shard_map.52), channel_id=1, replica_groups={{0,4,8,12},{1,5,9,13},{2,6,10,14},{3,7,11,15},{16,20,24,28},{17,21,25,2..., dimensions={0} | all-to-all | bytes 1064960 | tf_op jit(solution)/shard_map/all_to_all | solution.py:209
  136.6 18.4 %all_to_all.21.got = s16[4,136,128]{2,1,0:T(8,128)(2,1)S(1)} all-to-all(s16[4,136,128]{2,1,0:T(8,128)(2,1)S(1)} %shard_map.53), channel_id=1, replica_groups={{0,16,32,48},{1,17,33,49},{2,18,34,50},{3,19,35,51},{4,20,36,52},{5,21,..., dimensions={0} | all-to-all | bytes 278528 | tf_op jit(solution)/shard_map/all_to_all | solution.py:209
  155.1 0.7 shard_map.54
  (15 shorter events, 1.8 us)
Async XLA Ops:
  0.0 0.9 copy-start.2
  0.9 0.7 copy-start.3
  1.6 0.7 copy-start.4
  2.2 21.0 %copy-start = (bf16[768,1024]{1,0:T(8,128)(2,1)S(1)}, bf16[768,1024]{1,0:T(8,128)(2,1)}, u32[]{:S(2)}) copy-start(bf16[768,1024]{1,0:T(8,128)(2,1)} %mine.7) | copy-start | bytes 4718596
  4.5 57.0 %all-to-all-start = ((bf16[64,5,8,128]{3,2,1,0:T(8,128)(2,1)}), bf16[64,5,8,128]{3,2,1,0:T(8,128)(2,1)}, u32[]{:S(2)}, u32[]{:S(2)}) async-start(bf16[64,5,8,128]{3,2,1,0:T(8,128)(2,1)} %shard_map.46), calls=%async_computation | async-start | bytes 1310720 | tf_op jit(solution)/shard_map/all_to_all | solution.py:209
  23.3 45.9 %collective-permute-start = (bf16[768,1024]{1,0:T(8,128)(2,1)S(1)}, bf16[768,1024]{1,0:T(8,128)(2,1)S(1)}, u32[]{:S(2)}, u32[]{:S(2)}) collective-permute-start(bf16[768,1024]{1,0:T(8,128)(2,1)S(1)} %copy-done), channel_id=1, source_target_pairs={{0,64},{64,0},{128,192},{192,128},{256,320},{320,256},{384,448},{4... | collective-permute-start | bytes 4718600 | tf_op jit(solution)/shard_map/ppermute | solution.py:229
  63.5 0.9 copy-start.1
  64.5 15.8 %all-to-all-start.1 = ((bf16[4,128,768]{2,1,0:T(8,128)(2,1)}), bf16[4,128,768]{2,1,0:T(8,128)(2,1)}, u32[]{:S(2)}, u32[]{:S(2)}) async-start(bf16[4,128,768]{2,1,0:T(8,128)(2,1)} %copy-done.1), calls=%async_computation.1 | async-start | bytes 1572864 | tf_op jit(solution)/shard_map/all_to_all | solution.py:209
  82.1 18.0 %collective-permute-start.1 = (s16[264,1024]{1,0:T(8,128)(2,1)S(1)}, s16[264,1024]{1,0:T(8,128)(2,1)S(1)}, u32[]{:S(2)}, u32[]{:S(2)}) collective-permute-start(s16[264,1024]{1,0:T(8,128)(2,1)S(1)} %shard_map.48), channel_id=1, source_target_pairs={{0,0},{1,64},{2,2},{3,66},{4,4},{5,68},{6,6},{7,70},{8,8},{9,72},{... | collective-permute-start | bytes 1622024 | tf_op jit(solution)/shard_map/ppermute | solution.py:249
  85.9 15.0 %collective-permute-start.2 = (s16[264,1024]{1,0:T(8,128)(2,1)S(1)}, s16[264,1024]{1,0:T(8,128)(2,1)S(1)}, u32[]{:S(2)}, u32[]{:S(2)}) collective-permute-start(s16[264,1024]{1,0:T(8,128)(2,1)S(1)} %shard_map.49), channel_id=1, source_target_pairs={{0,64},{1,0},{2,66},{3,2},{4,68},{5,4},{6,70},{7,6},{8,72},{9,8},{... | collective-permute-start | bytes 1622024 | tf_op jit(solution)/shard_map/ppermute | solution.py:249
  89.7 23.5 %collective-permute-start.3 = (s16[264,1024]{1,0:T(8,128)(2,1)S(1)}, s16[264,1024]{1,0:T(8,128)(2,1)S(1)}, u32[]{:S(2)}, u32[]{:S(2)}) collective-permute-start(s16[264,1024]{1,0:T(8,128)(2,1)S(1)} %shard_map.50), channel_id=1, source_target_pairs={{0,2},{1,66},{2,0},{3,64},{4,6},{5,70},{6,4},{7,68},{8,10},{9,74},... | collective-permute-start | bytes 1622024 | tf_op jit(solution)/shard_map/ppermute | solution.py:249
  93.6 22.4 %collective-permute-start.4 = (s16[264,1024]{1,0:T(8,128)(2,1)S(1)}, s16[264,1024]{1,0:T(8,128)(2,1)S(1)}, u32[]{:S(2)}, u32[]{:S(2)}) collective-permute-start(s16[264,1024]{1,0:T(8,128)(2,1)S(1)} %shard_map.51), channel_id=1, source_target_pairs={{0,66},{1,2},{2,64},{3,0},{4,70},{5,6},{6,68},{7,4},{8,74},{9,10},... | collective-permute-start | bytes 1622024 | tf_op jit(solution)/shard_map/ppermute | solution.py:249

commit v4 on v3

--- a/solution.py
+++ b/solution.py
@@ -37,56 +37,44 @@
     return values16.astype(jnp.int32).astype(jnp.float32)
 
 
-def pack(tile_dev, amp, block, index, out, keys, count):
-    owners, _, lanes = keys.shape
-    units = amp.shape[1] // UNIT
+def pack(tile_dev, amp, index, out, count):
+    owners = out.shape[0]
 
     def clear(o, _):
         count[o] = 0
         return 0
 
     lax.fori_loop(0, owners, clear, 0)
-    keys[...] = jnp.full(keys.shape, -1.0, jnp.float32)
     for r in range(amp.shape[0]):
-        tile = index[r]
-        owner = tile // tile_dev
+        owner = index[r] // tile_dev
         rank = count[owner]
         count[owner] = rank + 1
-        key = block[r] * tile_dev + (tile - owner * tile_dev)
-        for u in range(units):
-            out[owner, rank * units + u] = amp[r, u * UNIT : (u + 1) * UNIT, :]
-        keys[owner, pl.ds(rank, 1), :] = jnp.full((1, lanes), key, jnp.int32).astype(jnp.float32)
-    for o in range(owners):
-        out[o, CAP * units] = keys[o].astype(out.dtype)
-
-
-def place(tile_dev, got, out, held, row, key, sem):
-    sources, units, _, width = got.shape
-    units = (units - 1) // CAP
-    line = lax.broadcasted_iota(jnp.int32, (UNIT, width), 0)
-    lane = lax.broadcasted_iota(jnp.int32, (UNIT, width), 1)
-    slot = jnp.where(line < CAP, lane - line, -1)
-    marks = jnp.zeros((UNIT, width), jnp.float32)
-    for s in range(sources):
-        marks = jnp.where(slot == CAP * s, got[s, CAP * units].astype(jnp.float32), marks)
-    row[...] = jnp.sum(marks, axis=0, keepdims=True).astype(jnp.int32)
-    copy = pltpu.make_async_copy(row, key, sem)
-    copy.start()
-    copy.wait()
+        out[owner, rank] = amp[r]
+
+
+def place(tile_dev, got, key, out, held):
+    sources, _, occ, width = got.shape
     spare = NB * tile_dev
     for s in range(sources):
         for r in range(CAP):
-            k = key[0, s * CAP + r]
-            to = jnp.where(k < 0, spare, k)
-            for u in range(units):
-                held[to, u] = got[s, r * units + u]
+            k = key[s * CAP + r]
+            held[jnp.where(k < 0, spare, k)] = got[s, r]
     for b in range(NB):
         for t in range(tile_dev):
-            for u in range(units):
-                tile = held[b * tile_dev + t, u]
-                at = (b * units + u) * UNIT
-                for y in range(out.shape[0]):
-                    out[y, at : at + UNIT, t * width : (t + 1) * width] = tile
+            tile = held[b * tile_dev + t]
+            for y in range(out.shape[0]):
+                out[y, b * occ : (b + 1) * occ, t * width : (t + 1) * width] = tile
+
+
+def slot_keys(plan, first, count):
+    key = plan - first
+    at = lax.broadcasted_iota(jnp.int32, plan.shape, 1)
+    hit = (key >= 0) & (key < count)
+    low = jnp.min(jnp.where(hit, at, plan.shape[1]), axis=1, keepdims=True)
+    high = jnp.max(jnp.where(hit, at, -1), axis=1, keepdims=True)
+    one = jnp.max(jnp.where(hit & (at == low), key, -1), axis=1)
+    two = jnp.max(jnp.where(hit & (at == high) & (high > low), key, -1), axis=1)
+    return jnp.stack([one, two], axis=1).reshape(-1)
 
 
 def multiply(a, mine, theirs, which, out):
@@ -116,14 +104,14 @@
         block(theirs)
 
 
-def recoded(tiles, out, z):
+def recoded(tiles, out):
     largest = jnp.abs(tiles[0])
     for tile in tiles[1:]:
         largest = jnp.maximum(largest, jnp.abs(tile))
     code = code_of(largest)
     lines = code.shape[0]
     for t, tile in enumerate([*tiles, None]):
-        out[z, t * lines : (t + 1) * lines, :] = (
+        out[t * lines : (t + 1) * lines, :] = (
             code.astype(jnp.int32).astype(jnp.int16) if tile is None else coded(tile, code)
         )
 
@@ -160,21 +148,33 @@
                     total = term if total is None else total + term
                 tiles[z % lows] += [total[:, 128 * t : 128 * (t + 1)] for t in range(cols // 128)]
     for low in range(lows):
-        recoded(tiles[low], out, low)
-
-
-def add_low(got, out):
+        recoded(tiles[low], out.at[low])
+
+
+def add_low(which, got, own, *refs):
+    *outs, held = refs
+    highs = held.shape[0]
     tiles = decoded(got, UNIT)
-    count = len(tiles) // out.shape[0]
-    for high in range(out.shape[0]):
-        recoded(tiles[high * count : (high + 1) * count], out, high)
-
-
-def add_high(got, out):
+    count = len(tiles) // highs
+    for n, tile in enumerate(tiles):
+        held[n // count, n % count] = tile
+    own[...] = held[which[0]]
+    for k, out in enumerate(outs):
+        high = lax.rem(which[0] + (k + 1), highs)
+        recoded([held[high, n] for n in range(count)], out)
+
+
+def add_high(own, *refs):
+    *gots, out = refs
     lanes = out.shape[1] // 128
-    for n, tile in enumerate(decoded(got, UNIT)):
+    count = own.shape[0]
+    scales = [scale_of(got[count * UNIT :, :]) for got in gots]
+    for n in range(count):
+        total = own[n]
+        for got, scale in zip(gots, scales):
+            total = total + plain(got[n * UNIT : (n + 1) * UNIT, :]) * scale
         u, t = n // lanes, n % lanes
-        out[u * UNIT : (u + 1) * UNIT, 128 * t : 128 * (t + 1)] = tile
+        out[u * UNIT : (u + 1) * UNIT, 128 * t : 128 * (t + 1)] = total
 
 
 def call(body, out, ins, scratch=()):
@@ -189,7 +189,6 @@
     nz, ny = own // NX, grp // CORES
     highs, half = nz // LOWS, NX // CORES
     low_groups = [[(high * LOWS + low) * NX + x for low in range(LOWS)] for high in range(highs) for x in range(NX)]
-    high_groups = [[(high * LOWS + low) * NX + x for high in range(highs)] for low in range(LOWS) for x in range(NX)]
     y_groups = [[y * CORES + c for y in range(ny)] for c in range(CORES)]
     core_pairs = [(y * CORES + c, y * CORES + 1 - c) for y in range(ny) for c in range(CORES)]
 
@@ -220,27 +219,30 @@
     core = lax.axis_index("grp") % CORES
     x = lax.axis_index("own") % NX
 
+    def high_pairs(k):
+        far = LOWS * NX
+        return [(o, (o + k * far) % own) for o in range(own)]
+
     packed = call(
         lambda *refs: pack(tile_dev, *refs),
-        struct((own, CAP * units + 1, UNIT, width), dtype),
-        [VMEM, SMEM, SMEM],
-        [pltpu.VMEM((own, UNIT, width), jnp.float32), pltpu.SMEM((own,), jnp.int32)],
-    )(amplitudes, tile_block, tile_index)
+        struct((own, CAP, occ, width), dtype),
+        [VMEM, SMEM],
+        [pltpu.SMEM((own,), jnp.int32)],
+    )(amplitudes, tile_index)
     theirs = lax.ppermute(integrals, "grp", core_pairs)
+    got = exchange(packed)
+    keys = NB * tile_dev
+    owner = tile_index // tile_dev
+    plan = lax.all_gather(owner * keys + tile_block * tile_dev + (tile_index - owner * tile_dev), "own", axis=0)
     copies = call(
         lambda *refs: place(tile_dev, *refs),
         struct((ny, rows, tile_dev * width), dtype),
-        [VMEM],
-        [
-            pltpu.VMEM((NB * tile_dev + 1, units, UNIT, width), dtype),
-            pltpu.VMEM((1, width), jnp.int32),
-            pltpu.SMEM((1, width), jnp.int32),
-            pltpu.SemaphoreType.DMA,
-        ],
-    )(exchange(packed))
+        [VMEM, SMEM],
+        [pltpu.VMEM((keys + 1, occ, width), dtype)],
+    )(got, slot_keys(plan, lax.axis_index("own") * keys, keys))
     mine = exchange(copies, y_groups, "grp")
     gots = []
-    for r in range(half * CORES):
+    for r in (2, 3, 0, 1):
         a, to = target(r, x)
         which = jnp.stack([a, to ^ core]).astype(jnp.int32)
         sent = call(multiply, struct((parts * rows + 8, cols), jnp.int16), [VMEM, VMEM, VMEM, SMEM])(
@@ -252,10 +254,17 @@
         struct((LOWS, (highs * units * tiles + 1) * UNIT, 128), jnp.int16),
         [VMEM] * len(gots),
     )(*gots)
-    sent = call(add_low, struct((highs, (units * tiles + 1) * UNIT, 128), jnp.int16), [VMEM])(
-        exchange(sent, low_groups)
-    )
-    return call(add_high, struct((occ, cols), jnp.float32), [VMEM])(exchange(sent, high_groups))
+    count = units * tiles
+    part = struct(((count + 1) * UNIT, 128), jnp.int16)
+    high = jnp.reshape(lax.axis_index("own") // (LOWS * NX), (1,)).astype(jnp.int32)
+    kept, *sent = call(
+        add_low,
+        [struct((count, UNIT, 128), jnp.float32)] + [part] * (highs - 1),
+        [SMEM, VMEM],
+        [pltpu.VMEM((highs, count, UNIT, 128), jnp.float32)],
+    )(high, exchange(sent, low_groups))
+    sent = {k: lax.ppermute(sent[k - 1], "own", high_pairs(k)) for k in (2, 1, 3)}
+    return call(add_high, struct((occ, cols), jnp.float32), [VMEM] * highs)(kept, *sent.values())
 
 
 def solution(mesh):

time: 156 us -> 407 us (2.61); the launches traced: 156 us -> 400 us
  blocking collectives: 38 us -> 279 us
  starting transfers between devices: 37.6 us -> 68.3 us
  waiting for transfers between devices: 63.3 us -> 33.2 us
    unnamed x0 -> x1, blocking collectives: none -> 279 us
    all_to_all x2 -> x0, blocking collectives: 38 us -> none  [exchange(): lax.all_to_all(array, axis, 0, 0, axis_index_groups=groups, tiled=True)]
    all_to_all x2 -> x3, waiting for transfers between devices: 47.4 us -> 21.5 us  [exchange(): lax.all_to_all(array, axis, 0, 0, axis_index_groups=groups, tiled=True)]
    ppermute x0 -> x3, starting transfers between devices: none -> 24 us  [local(): lax.ppermute(sent[k - 1], 'own', high_pairs(k))]
    ppermute x4, waiting for transfers between devices: 15.9 us -> 8.87 us  [local(): gots.append(lax.ppermute(sent, ('grp', 'own'), round_pairs(r)))]
    all_to_all x2 -> x3, starting transfers between devices: 23.2 us -> 27.2 us  [exchange(): lax.all_to_all(array, axis, 0, 0, axis_index_groups=groups, tiled=True)]
  transfers between devices with their start and end apart: 7 -> 11, of which waited for: 5 -> 7; matrix products, arithmetic and copies ran while one was open for 0% -> 1% of each run, Pallas kernels for 5% -> 2%
where the time goes in v4:
time: 407 us; the launch traced here: 400 us
  blocking collectives  279 us (69%)
  starting transfers between devices  68.3 us (17%)
  waiting for transfers between devices  33.2 us (8%)
  Pallas kernels  13.2 us (3%)
  local copies, waits for them, and re-layouts  4.19 us (1%)
    unnamed x1, blocking collectives  279 us
    all_to_all x3, starting transfers between devices, exchange(): lax.all_to_all(array, axis, 0, 0, axis_index_groups=groups, tiled=True)  27.2 us
    ppermute x3, starting transfers between devices, local(): lax.ppermute(sent[k - 1], 'own', high_pairs(k))  24 us
    all_to_all x3, waiting for transfers between devices, exchange(): lax.all_to_all(array, axis, 0, 0, axis_index_groups=groups, tiled=True)  21.5 us
    ppermute x4, starting transfers between devices, local(): gots.append(lax.ppermute(sent, ('grp', 'own'), round_pairs(r)))  15.2 us
    ppermute x4, waiting for transfers between devices, local(): gots.append(lax.ppermute(sent, ('grp', 'own'), round_pairs(r)))  8.87 us
  transfers between devices with their start and end apart: 11, of which 7 were waited for; matrix products, arithmetic and copies ran while one was open for 1% of the time, Pallas kernels for 2%

profile of v4, /device:TPU:6, one launch (start us, length us, event | category | flops | bytes accessed | tf_op | source)
XLA Modules:
  0.0 400.2 jit_solution(17526724197620618629)
XLA Ops:
  1.7 2.1 shard_map.46
  3.8 18.8 %all-to-all-start = ((bf16[64,2,16,128]{3,2,1,0:T(8,128)(2,1)}), bf16[64,2,16,128]{3,2,1,0:T(8,128)(2,1)}, u32[]{:S(2)}, u32[]{:S(2)}) async-start(bf16[64,2,16,128]{3,2,1,0:T(8,128)(2,1)} %shard_map.46), calls=%async_computation | async-start | bytes 1048576 | tf_op jit(solution)/shard_map/all_to_all | solution.py:208
  22.6 1.9 collective-permute-start
  24.6 1.3 dynamic-slice
  26.6 279.5 %all-reduce = s32[3072]{0:T(1024)S(1)} all-reduce(s32[3072]{0:T(1024)S(1)} %add_dynamic-update-slice_fusion), channel_id=2, replica_groups=mesh['grp'=8,'own'=64] {'own'}, use_global_device_ids=true, to_apply=%add | all-reduce | flops 3072 | bytes 24576
  307.0 1.3 shard_map.47
  309.2 4.5 %all-to-all-start.1 = ((bf16[4,128,768]{2,1,0:T(8,128)(2,1)}), bf16[4,128,768]{2,1,0:T(8,128)(2,1)}, u32[]{:S(2)}, u32[]{:S(2)}) async-start(bf16[4,128,768]{2,1,0:T(8,128)(2,1)} %copy-done.1), calls=%async_computation.1 | async-start | bytes 1572864 | tf_op jit(solution)/shard_map/all_to_all | solution.py:208
  314.0 9.3 %all-to-all-done.1.a = bf16[4,128,768]{2,1,0:T(8,128)(2,1)} async-done(((bf16[4,128,768]{2,1,0:T(8,128)(2,1)}), bf16[4,128,768]{2,1,0:T(8,128)(2,1)}, u32[]{:S(2)}, u32[]{:S(2)}) %all-to-all-start.1) | async-done | bytes 786464 | tf_op jit(solution)/shard_map/all_to_all | solution.py:208
  323.3 1.8 shard_map.48
  325.1 1.9 collective-permute-start.1
  327.1 1.8 shard_map.49
  328.9 9.4 %collective-permute-start.2 = (s16[264,1024]{1,0:T(8,128)(2,1)S(1)}, s16[264,1024]{1,0:T(8,128)(2,1)S(1)}, u32[]{:S(2)}, u32[]{:S(2)}) collective-permute-start(s16[264,1024]{1,0:T(8,128)(2,1)S(1)} %shard_map.49), channel_id=1, source_target_pairs={{0,66},{1,2},{2,64},{3,0},{4,70},{5,6},{6,68},{7,4},{8,74},{9,10},... | collective-permute-start | bytes 1622024 | tf_op jit(solution)/shard_map/ppermute | solution.py:251
  338.3 1.8 shard_map.50
  340.2 1.9 collective-permute-start.3
  342.1 1.8 shard_map.51
  343.9 1.9 collective-permute-start.4
  345.9 7.4 %collective-permute-done.2.refs_1_ = s16[264,1024]{1,0:T(8,128)(2,1)S(1)} collective-permute-done((s16[264,1024]{1,0:T(8,128)(2,1)S(1)}, s16[264,1024]{1,0:T(8,128)(2,1)S(1)}, u32[]{:S(2)}, u32[]{:S(2)}) %collective-permute-start.2) | collective-permute-done | bytes 540704 | tf_op jit(solution)/shard_map/ppermute | solution.py:251
  354.7 1.6 shard_map.52
  356.3 3.9 all-to-all-start.2
  360.2 12.2 %all-to-all-done.2.got = s16[4,520,128]{2,1,0:T(8,128)(2,1)S(1)} async-done(((s16[4,520,128]{2,1,0:T(8,128)(2,1)}), s16[4,520,128]{2,1,0:T(8,128)(2,1)S(1)}, u32[]{:S(2)}, u32[]{:S(2)}) %all-to-all-start.2) | async-done | bytes 532512 | tf_op jit(solution)/shard_map/all_to_all | solution.py:208
  372.6 14.3 %collective-permute-start.5 = (s16[136,128]{1,0:T(8,128)(2,1)S(1)}, s16[136,128]{1,0:T(8,128)(2,1)S(1)}, u32[]{:S(2)}, u32[]{:S(2)}) collective-permute-start(s16[136,128]{1,0:T(8,128)(2,1)S(1)} %get-tuple-element.10), channel_id=1, source_target_pairs={{0,32},{1,33},{2,34},{3,35},{4,36},{5,37},{6,38},{7,39},{8,40},{9,... | collective-permute-start | bytes 104456 | tf_op jit(solution)/shard_map/ppermute | solution.py:266
  386.9 2.8 collective-permute-start.6
  389.8 6.9 %collective-permute-start.7 = (s16[136,128]{1,0:T(8,128)(2,1)S(1)}, s16[136,128]{1,0:T(8,128)(2,1)S(1)}, u32[]{:S(2)}, u32[]{:S(2)}) collective-permute-start(s16[136,128]{1,0:T(8,128)(2,1)S(1)} %get-tuple-element.12), channel_id=1, source_target_pairs={{0,48},{1,49},{2,50},{3,51},{4,52},{5,53},{6,54},{7,55},{8,56},{9,... | collective-permute-start | bytes 104456 | tf_op jit(solution)/shard_map/ppermute | solution.py:266
  396.8 2.7 collective-permute-done.7.refs_2_
  (36 shorter events, 6.3 us)
Async XLA Ops:
  0.0 22.6 %copy-start = (bf16[768,1024]{1,0:T(8,128)(2,1)S(1)}, bf16[768,1024]{1,0:T(8,128)(2,1)}, u32[]{:S(2)}) copy-start(bf16[768,1024]{1,0:T(8,128)(2,1)} %mine.7) | copy-start | bytes 4718596
  0.0 1.0 copy-start.2
  1.0 0.7 copy-start.3
  1.7 24.8 %copy-start.4 = (s32[48]{0:T(128)S(1)}, s32[48]{0:T(128)}, u32[]{:S(2)}) copy-start(s32[48]{0:T(128)} %refs_1_.1) | copy-start | bytes 580
  1.7 24.8 %copy-start.5 = (s32[48]{0:T(128)S(1)}, s32[48]{0:T(128)}, u32[]{:S(2)}) copy-start(s32[48]{0:T(128)} %param.6) | copy-start | bytes 580
  3.8 303.1 %all-to-all-start = ((bf16[64,2,16,128]{3,2,1,0:T(8,128)(2,1)}), bf16[64,2,16,128]{3,2,1,0:T(8,128)(2,1)}, u32[]{:S(2)}, u32[]{:S(2)}) async-start(bf16[64,2,16,128]{3,2,1,0:T(8,128)(2,1)} %shard_map.46), calls=%async_computation | async-start | bytes 1048576 | tf_op jit(solution)/shard_map/all_to_all | solution.py:208
  22.6 291.4 %collective-permute-start = (bf16[768,1024]{1,0:T(8,128)(2,1)S(1)}, bf16[768,1024]{1,0:T(8,128)(2,1)S(1)}, u32[]{:S(2)}, u32[]{:S(2)}) collective-permute-start(bf16[768,1024]{1,0:T(8,128)(2,1)S(1)} %copy-done), channel_id=1, source_target_pairs={{0,64},{64,0},{128,192},{192,128},{256,320},{320,256},{384,448},{4... | collective-permute-start | bytes 4718600 | tf_op jit(solution)/shard_map/ppermute | solution.py:232
  308.3 0.9 copy-start.1
  309.2 14.1 %all-to-all-start.1 = ((bf16[4,128,768]{2,1,0:T(8,128)(2,1)}), bf16[4,128,768]{2,1,0:T(8,128)(2,1)}, u32[]{:S(2)}, u32[]{:S(2)}) async-start(bf16[4,128,768]{2,1,0:T(8,128)(2,1)} %copy-done.1), calls=%async_computation.1 | async-start | bytes 1572864 | tf_op jit(solution)/shard_map/all_to_all | solution.py:208
  325.1 20.7 %collective-permute-start.1 = (s16[264,1024]{1,0:T(8,128)(2,1)S(1)}, s16[264,1024]{1,0:T(8,128)(2,1)S(1)}, u32[]{:S(2)}, u32[]{:S(2)}) collective-permute-start(s16[264,1024]{1,0:T(8,128)(2,1)S(1)} %shard_map.48), channel_id=1, source_target_pairs={{0,2},{1,66},{2,0},{3,64},{4,6},{5,70},{6,4},{7,68},{8,10},{9,74},... | collective-permute-start | bytes 1622024 | tf_op jit(solution)/shard_map/ppermute | solution.py:251
  328.9 24.4 %collective-permute-start.2 = (s16[264,1024]{1,0:T(8,128)(2,1)S(1)}, s16[264,1024]{1,0:T(8,128)(2,1)S(1)}, u32[]{:S(2)}, u32[]{:S(2)}) collective-permute-start(s16[264,1024]{1,0:T(8,128)(2,1)S(1)} %shard_map.49), channel_id=1, source_target_pairs={{0,66},{1,2},{2,64},{3,0},{4,70},{5,6},{6,68},{7,4},{8,74},{9,10},... | collective-permute-start | bytes 1622024 | tf_op jit(solution)/shard_map/ppermute | solution.py:251
  340.2 14.2 %collective-permute-start.3 = (s16[264,1024]{1,0:T(8,128)(2,1)S(1)}, s16[264,1024]{1,0:T(8,128)(2,1)S(1)}, u32[]{:S(2)}, u32[]{:S(2)}) collective-permute-start(s16[264,1024]{1,0:T(8,128)(2,1)S(1)} %shard_map.50), channel_id=1, source_target_pairs={{0,0},{1,64},{2,2},{3,66},{4,4},{5,68},{6,6},{7,70},{8,8},{9,72},{... | collective-permute-start | bytes 1622024 | tf_op jit(solution)/shard_map/ppermute | solution.py:251
  343.9 10.8 %collective-permute-start.4 = (s16[264,1024]{1,0:T(8,128)(2,1)S(1)}, s16[264,1024]{1,0:T(8,128)(2,1)S(1)}, u32[]{:S(2)}, u32[]{:S(2)}) collective-permute-start(s16[264,1024]{1,0:T(8,128)(2,1)S(1)} %shard_map.51), channel_id=1, source_target_pairs={{0,64},{1,0},{2,66},{3,2},{4,68},{5,4},{6,70},{7,6},{8,72},{9,8},{... | collective-permute-start | bytes 1622024 | tf_op jit(solution)/shard_map/ppermute | solution.py:251
  356.3 16.1 %all-to-all-start.2 = ((s16[4,520,128]{2,1,0:T(8,128)(2,1)}), s16[4,520,128]{2,1,0:T(8,128)(2,1)S(1)}, u32[]{:S(2)}, u32[]{:S(2)}) async-start(s16[4,520,128]{2,1,0:T(8,128)(2,1)} %shard_map.52), calls=%async_computation.2 | async-start | bytes 1064960 | tf_op jit(solution)/shard_map/all_to_all | solution.py:208
  372.6 24.1 %collective-permute-start.5 = (s16[136,128]{1,0:T(8,128)(2,1)S(1)}, s16[136,128]{1,0:T(8,128)(2,1)S(1)}, u32[]{:S(2)}, u32[]{:S(2)}) collective-permute-start(s16[136,128]{1,0:T(8,128)(2,1)S(1)} %get-tuple-element.10), channel_id=1, source_target_pairs={{0,32},{1,33},{2,34},{3,35},{4,36},{5,37},{6,38},{7,39},{8,40},{9,... | collective-permute-start | bytes 104456 | tf_op jit(solution)/shard_map/ppermute | solution.py:266
  386.9 9.9 %collective-permute-start.6 = (s16[136,128]{1,0:T(8,128)(2,1)S(1)}, s16[136,128]{1,0:T(8,128)(2,1)S(1)}, u32[]{:S(2)}, u32[]{:S(2)}) collective-permute-start(s16[136,128]{1,0:T(8,128)(2,1)S(1)} %get-tuple-element.11), channel_id=1, source_target_pairs={{0,16},{1,17},{2,18},{3,19},{4,20},{5,21},{6,22},{7,23},{8,24},{9,... | collective-permute-start | bytes 104456 | tf_op jit(solution)/shard_map/ppermute | solution.py:266
  389.8 9.7 %collective-permute-start.7 = (s16[136,128]{1,0:T(8,128)(2,1)S(1)}, s16[136,128]{1,0:T(8,128)(2,1)S(1)}, u32[]{:S(2)}, u32[]{:S(2)}) collective-permute-start(s16[136,128]{1,0:T(8,128)(2,1)S(1)} %get-tuple-element.12), channel_id=1, source_target_pairs={{0,48},{1,49},{2,50},{3,51},{4,52},{5,53},{6,54},{7,55},{8,56},{9,... | collective-permute-start | bytes 104456 | tf_op jit(solution)/shard_map/ppermute | solution.py:266

commit v5 on v3

--- a/solution.py
+++ b/solution.py
@@ -187,8 +187,13 @@
 def local(amplitudes, integrals, tile_block, tile_index):
     own, grp = lax.axis_size("own"), lax.axis_size("grp")
     nz, ny = own // NX, grp // CORES
-    highs, half = nz // LOWS, NX // CORES
-    low_groups = [[(high * LOWS + low) * NX + x for low in range(LOWS)] for high in range(highs) for x in range(NX)]
+    highs = nz // LOWS
+    low_groups = []
+    for g in range(grp):
+        shift = g % CORES * (LOWS // CORES)
+        for high in range(highs):
+            line = sorted(((high * LOWS + low + shift) % nz for low in range(LOWS)), key=lambda z: z % LOWS)
+            low_groups += [[g * own + z * NX + x for z in line] for x in range(NX)]
     high_groups = [[(high * LOWS + low) * NX + x for high in range(highs)] for low in range(LOWS) for x in range(NX)]
     y_groups = [[y * CORES + c for y in range(ny)] for c in range(CORES)]
     core_pairs = [(y * CORES + c, y * CORES + 1 - c) for y in range(ny) for c in range(CORES)]
@@ -240,7 +245,7 @@
     )(exchange(packed))
     mine = exchange(copies, y_groups, "grp")
     gots = []
-    for r in range(half * CORES):
+    for r in (2, 3, 0, 1):
         a, to = target(r, x)
         which = jnp.stack([a, to ^ core]).astype(jnp.int32)
         sent = call(multiply, struct((parts * rows + 8, cols), jnp.int16), [VMEM, VMEM, VMEM, SMEM])(
@@ -253,7 +258,7 @@
         [VMEM] * len(gots),
     )(*gots)
     sent = call(add_low, struct((highs, (units * tiles + 1) * UNIT, 128), jnp.int16), [VMEM])(
-        exchange(sent, low_groups)
+        exchange(sent, low_groups, ("grp", "own"))
     )
     return call(add_high, struct((occ, cols), jnp.float32), [VMEM])(exchange(sent, high_groups))
 

time: 156 us -> 147 us (0.942); the launches traced: 156 us -> 144 us
  waiting for transfers between devices: 63.3 us -> 56.8 us
  blocking collectives: 38 us -> 35.3 us
  starting transfers between devices: 37.6 us -> 35.4 us
    ppermute x4, waiting for transfers between devices: 15.9 us -> 9.44 us  [local(): gots.append(lax.ppermute(sent, ('grp', 'own'), round_pairs(r)))]
    all_to_all x2, blocking collectives: 38 us -> 35.3 us  [exchange(): lax.all_to_all(array, axis, 0, 0, axis_index_groups=groups, tiled=True)]
    ppermute x4, starting transfers between devices: 12.4 us -> 10.2 us  [local(): gots.append(lax.ppermute(sent, ('grp', 'own'), round_pairs(r)))]
  transfers between devices with their start and end apart: 7 -> 7, of which waited for: 5 -> 4; matrix products, arithmetic and copies ran while one was open for 0% -> 0% of each run, Pallas kernels for 5% -> 5%
where the time goes in v5:
time: 147 us; the launch traced here: 144 us
  waiting for transfers between devices  56.8 us (39%)
  starting transfers between devices  35.4 us (24%)
  blocking collectives  35.3 us (24%)
  Pallas kernels  13.2 us (9%)
  local copies, waits for them, and re-layouts  3.15 us (2%)
    all_to_all x2, waiting for transfers between devices, exchange(): lax.all_to_all(array, axis, 0, 0, axis_index_groups=groups, tiled=True)  47.4 us
    all_to_all x2, blocking collectives, exchange(): lax.all_to_all(array, axis, 0, 0, axis_index_groups=groups, tiled=True)  35.3 us
    all_to_all x2, starting transfers between devices, exchange(): lax.all_to_all(array, axis, 0, 0, axis_index_groups=groups, tiled=True)  23.2 us
    ppermute x4, starting transfers between devices, local(): gots.append(lax.ppermute(sent, ('grp', 'own'), round_pairs(r)))  10.2 us
    ppermute x4, waiting for transfers between devices, local(): gots.append(lax.ppermute(sent, ('grp', 'own'), round_pairs(r)))  9.44 us
    pallas_call x4, Pallas kernels, local(): call(multiply, struct((parts * rows + 8, cols), jnp.int16), [VMEM, VMEM,...  7.32 us
    unnamed x10, local copies, waits for them, and re-layouts  3.15 us
  transfers between devices with their start and end apart: 7, of which 4 were waited for; matrix products, arithmetic and copies ran while one was open for 0% of the time, Pallas kernels for 5%

profile of v5, /device:TPU:6, one launch (start us, length us, event | category | flops | bytes accessed | tf_op | source)
XLA Modules:
  0.0 144.3 jit_solution(4943900428941245575)
XLA Ops:
  0.0 0.9 copy-done.2
  0.9 0.7 copy-done.3
  2.2 2.3 %shard_map.46 = bf16[64,5,8,128]{3,2,1,0:T(8,128)(2,1)} custom-call(bf16[48,16,128]{2,1,0:T(8,128)(2,1)S(1)} %copy-done.2, s32[48]{0:T(128)S(1)} %copy-done.3, s32[48]{0:T(128)S(1)} %copy-done.4), custom_call_target="tpu_custom_call" | custom-call | tf_op jit(solution)/shard_map/pallas_call | solution.py:228
  4.5 18.7 %all-to-all-start = ((bf16[64,5,8,128]{3,2,1,0:T(8,128)(2,1)}), bf16[64,5,8,128]{3,2,1,0:T(8,128)(2,1)}, u32[]{:S(2)}, u32[]{:S(2)}) async-start(bf16[64,5,8,128]{3,2,1,0:T(8,128)(2,1)} %shard_map.46), calls=%async_computation | async-start | bytes 1310720 | tf_op jit(solution)/shard_map/all_to_all | solution.py:214
  23.3 1.9 %collective-permute-start = (bf16[768,1024]{1,0:T(8,128)(2,1)S(1)}, bf16[768,1024]{1,0:T(8,128)(2,1)S(1)}, u32[]{:S(2)}, u32[]{:S(2)}) collective-permute-start(bf16[768,1024]{1,0:T(8,128)(2,1)S(1)} %copy-done), channel_id=1, source_target_pairs={{0,64},{64,0},{128,192},{192,128},{256,320},{320,256},{384,448},{4... | collective-permute-start | bytes 4718600 | tf_op jit(solution)/shard_map/ppermute | solution.py:234
  25.2 36.4 %all-to-all-done.refs_0_ = bf16[64,5,8,128]{3,2,1,0:T(8,128)(2,1)} async-done(((bf16[64,5,8,128]{3,2,1,0:T(8,128)(2,1)}), bf16[64,5,8,128]{3,2,1,0:T(8,128)(2,1)}, u32[]{:S(2)}, u32[]{:S(2)}) %all-to-all-start) | async-done | bytes 655392 | tf_op jit(solution)/shard_map/all_to_all | solution.py:214
  61.6 2.0 %shard_map.47 = bf16[4,128,768]{2,1,0:T(8,128)(2,1)S(1)} custom-call(bf16[64,5,8,128]{3,2,1,0:T(8,128)(2,1)} %all-to-all-done.refs_0_), custom_call_target="tpu_custom_call" | custom-call | tf_op jit(solution)/shard_map/pallas_call | solution.py:235
  63.5 0.9 copy-done.1
  64.4 4.5 %all-to-all-start.1 = ((bf16[4,128,768]{2,1,0:T(8,128)(2,1)}), bf16[4,128,768]{2,1,0:T(8,128)(2,1)}, u32[]{:S(2)}, u32[]{:S(2)}) async-start(bf16[4,128,768]{2,1,0:T(8,128)(2,1)} %copy-done.1), calls=%async_computation.1 | async-start | bytes 1572864 | tf_op jit(solution)/shard_map/all_to_all | solution.py:214
  69.2 11.1 %all-to-all-done.1.a = bf16[4,128,768]{2,1,0:T(8,128)(2,1)} async-done(((bf16[4,128,768]{2,1,0:T(8,128)(2,1)}), bf16[4,128,768]{2,1,0:T(8,128)(2,1)}, u32[]{:S(2)}, u32[]{:S(2)}) %all-to-all-start.1) | async-done | bytes 786464 | tf_op jit(solution)/shard_map/all_to_all | solution.py:214
  80.3 1.8 %shard_map.48 = s16[264,1024]{1,0:T(8,128)(2,1)S(1)} custom-call(bf16[4,128,768]{2,1,0:T(8,128)(2,1)} %all-to-all-done.1.a, bf16[768,1024]{1,0:T(8,128)(2,1)S(1)} %copy-done, bf16[768,1024]{1,0:T(8,128)(2,1)S(1)} %collective-permute-done.theirs, s32[2]{0:T(128)S(1)} %pad_add_fusion.1.which), custom_call_target="tpu_custom_call" | custom-call | tf_op jit(solution)/shard_map/pallas_call | solution.py:251
  82.1 1.9 %collective-permute-start.1 = (s16[264,1024]{1,0:T(8,128)(2,1)S(1)}, s16[264,1024]{1,0:T(8,128)(2,1)S(1)}, u32[]{:S(2)}, u32[]{:S(2)}) collective-permute-start(s16[264,1024]{1,0:T(8,128)(2,1)S(1)} %shard_map.48), channel_id=1, source_target_pairs={{0,2},{1,66},{2,0},{3,64},{4,6},{5,70},{6,4},{7,68},{8,10},{9,74},... | collective-permute-start | bytes 1622024 | tf_op jit(solution)/shard_map/ppermute | solution.py:254
  84.0 1.8 %shard_map.49 = s16[264,1024]{1,0:T(8,128)(2,1)S(1)} custom-call(bf16[4,128,768]{2,1,0:T(8,128)(2,1)} %all-to-all-done.1.a, bf16[768,1024]{1,0:T(8,128)(2,1)S(1)} %copy-done, bf16[768,1024]{1,0:T(8,128)(2,1)S(1)} %collective-permute-done.theirs, s32[2]{0:T(128)S(1)} %pad_add_fusion.2.which), custom_call_target="tpu_custom_call" | custom-call | tf_op jit(solution)/shard_map/pallas_call | solution.py:251
  85.9 3.7 %collective-permute-start.2 = (s16[264,1024]{1,0:T(8,128)(2,1)S(1)}, s16[264,1024]{1,0:T(8,128)(2,1)S(1)}, u32[]{:S(2)}, u32[]{:S(2)}) collective-permute-start(s16[264,1024]{1,0:T(8,128)(2,1)S(1)} %shard_map.49), channel_id=1, source_target_pairs={{0,66},{1,2},{2,64},{3,0},{4,70},{5,6},{6,68},{7,4},{8,74},{9,10},... | collective-permute-start | bytes 1622024 | tf_op jit(solution)/shard_map/ppermute | solution.py:254
  89.5 1.8 %shard_map.50 = s16[264,1024]{1,0:T(8,128)(2,1)S(1)} custom-call(bf16[4,128,768]{2,1,0:T(8,128)(2,1)} %all-to-all-done.1.a, bf16[768,1024]{1,0:T(8,128)(2,1)S(1)} %copy-done, bf16[768,1024]{1,0:T(8,128)(2,1)S(1)} %collective-permute-done.theirs, s32[2]{0:T(128)S(1)} %pad_add_fusion.which), custom_call_target="tpu_custom_call" | custom-call | tf_op jit(solution)/shard_map/pallas_call | solution.py:251
  91.4 1.9 %collective-permute-start.3 = (s16[264,1024]{1,0:T(8,128)(2,1)S(1)}, s16[264,1024]{1,0:T(8,128)(2,1)S(1)}, u32[]{:S(2)}, u32[]{:S(2)}) collective-permute-start(s16[264,1024]{1,0:T(8,128)(2,1)S(1)} %shard_map.50), channel_id=1, source_target_pairs={{0,0},{1,64},{2,2},{3,66},{4,4},{5,68},{6,6},{7,70},{8,8},{9,72},{... | collective-permute-start | bytes 1622024 | tf_op jit(solution)/shard_map/ppermute | solution.py:254
  93.3 1.8 %shard_map.51 = s16[264,1024]{1,0:T(8,128)(2,1)S(1)} custom-call(bf16[4,128,768]{2,1,0:T(8,128)(2,1)} %all-to-all-done.1.a, bf16[768,1024]{1,0:T(8,128)(2,1)S(1)} %copy-done, bf16[768,1024]{1,0:T(8,128)(2,1)S(1)} %collective-permute-done.theirs, s32[2]{0:T(128)S(1)} %pad_add_fusion.3.which), custom_call_target="tpu_custom_call" | custom-call | tf_op jit(solution)/shard_map/pallas_call | solution.py:251
  95.1 2.7 %collective-permute-start.4 = (s16[264,1024]{1,0:T(8,128)(2,1)S(1)}, s16[264,1024]{1,0:T(8,128)(2,1)S(1)}, u32[]{:S(2)}, u32[]{:S(2)}) collective-permute-start(s16[264,1024]{1,0:T(8,128)(2,1)S(1)} %shard_map.51), channel_id=1, source_target_pairs={{0,64},{1,0},{2,66},{3,2},{4,68},{5,4},{6,70},{7,6},{8,72},{9,8},{... | collective-permute-start | bytes 1622024 | tf_op jit(solution)/shard_map/ppermute | solution.py:254
  97.9 4.9 %collective-permute-done.1.refs_0_ = s16[264,1024]{1,0:T(8,128)(2,1)S(1)} collective-permute-done((s16[264,1024]{1,0:T(8,128)(2,1)S(1)}, s16[264,1024]{1,0:T(8,128)(2,1)S(1)}, u32[]{:S(2)}, u32[]{:S(2)}) %collective-permute-start.1) | collective-permute-done | bytes 540704 | tf_op jit(solution)/shard_map/ppermute | solution.py:254
  102.8 4.5 %collective-permute-done.2.refs_1_ = s16[264,1024]{1,0:T(8,128)(2,1)S(1)} collective-permute-done((s16[264,1024]{1,0:T(8,128)(2,1)S(1)}, s16[264,1024]{1,0:T(8,128)(2,1)S(1)}, u32[]{:S(2)}, u32[]{:S(2)}) %collective-permute-start.2) | collective-permute-done | bytes 540704 | tf_op jit(solution)/shard_map/ppermute | solution.py:254
  107.3 0.8 shard_map.52
  108.1 16.6 %all_to_all.20.got = s16[4,520,128]{2,1,0:T(8,128)(2,1)S(1)} all-to-all(s16[4,520,128]{2,1,0:T(8,128)(2,1)S(1)} %shard_map.52), channel_id=1, replica_groups={{0,4,8,12},{1,5,9,13},{2,6,10,14},{3,7,11,15},{16,20,24,28},{17,21,25,2..., dimensions={0} | all-to-all | bytes 1064960 | tf_op jit(solution)/shard_map/all_to_all | solution.py:214
  124.9 18.7 %all_to_all.21.got = s16[4,136,128]{2,1,0:T(8,128)(2,1)S(1)} all-to-all(s16[4,136,128]{2,1,0:T(8,128)(2,1)S(1)} %shard_map.53), channel_id=1, replica_groups={{0,16,32,48},{1,17,33,49},{2,18,34,50},{3,19,35,51},{4,20,36,52},{5,21,..., dimensions={0} | all-to-all | bytes 278528 | tf_op jit(solution)/shard_map/all_to_all | solution.py:214
  143.7 0.7 shard_map.54
  (15 shorter events, 1.2 us)
Async XLA Ops:
  0.0 0.9 copy-start.2
  0.9 0.7 copy-start.3
  1.6 0.7 copy-start.4
  2.2 21.0 %copy-start = (bf16[768,1024]{1,0:T(8,128)(2,1)S(1)}, bf16[768,1024]{1,0:T(8,128)(2,1)}, u32[]{:S(2)}) copy-start(bf16[768,1024]{1,0:T(8,128)(2,1)} %mine.7) | copy-start | bytes 4718596
  4.5 57.0 %all-to-all-start = ((bf16[64,5,8,128]{3,2,1,0:T(8,128)(2,1)}), bf16[64,5,8,128]{3,2,1,0:T(8,128)(2,1)}, u32[]{:S(2)}, u32[]{:S(2)}) async-start(bf16[64,5,8,128]{3,2,1,0:T(8,128)(2,1)} %shard_map.46), calls=%async_computation | async-start | bytes 1310720 | tf_op jit(solution)/shard_map/all_to_all | solution.py:214
  23.3 45.9 %collective-permute-start = (bf16[768,1024]{1,0:T(8,128)(2,1)S(1)}, bf16[768,1024]{1,0:T(8,128)(2,1)S(1)}, u32[]{:S(2)}, u32[]{:S(2)}) collective-permute-start(bf16[768,1024]{1,0:T(8,128)(2,1)S(1)} %copy-done), channel_id=1, source_target_pairs={{0,64},{64,0},{128,192},{192,128},{256,320},{320,256},{384,448},{4... | collective-permute-start | bytes 4718600 | tf_op jit(solution)/shard_map/ppermute | solution.py:234
  63.5 0.9 copy-start.1
  64.4 15.8 %all-to-all-start.1 = ((bf16[4,128,768]{2,1,0:T(8,128)(2,1)}), bf16[4,128,768]{2,1,0:T(8,128)(2,1)}, u32[]{:S(2)}, u32[]{:S(2)}) async-start(bf16[4,128,768]{2,1,0:T(8,128)(2,1)} %copy-done.1), calls=%async_computation.1 | async-start | bytes 1572864 | tf_op jit(solution)/shard_map/all_to_all | solution.py:214
  82.1 20.7 %collective-permute-start.1 = (s16[264,1024]{1,0:T(8,128)(2,1)S(1)}, s16[264,1024]{1,0:T(8,128)(2,1)S(1)}, u32[]{:S(2)}, u32[]{:S(2)}) collective-permute-start(s16[264,1024]{1,0:T(8,128)(2,1)S(1)} %shard_map.48), channel_id=1, source_target_pairs={{0,2},{1,66},{2,0},{3,64},{4,6},{5,70},{6,4},{7,68},{8,10},{9,74},... | collective-permute-start | bytes 1622024 | tf_op jit(solution)/shard_map/ppermute | solution.py:254
  85.9 21.4 %collective-permute-start.2 = (s16[264,1024]{1,0:T(8,128)(2,1)S(1)}, s16[264,1024]{1,0:T(8,128)(2,1)S(1)}, u32[]{:S(2)}, u32[]{:S(2)}) collective-permute-start(s16[264,1024]{1,0:T(8,128)(2,1)S(1)} %shard_map.49), channel_id=1, source_target_pairs={{0,66},{1,2},{2,64},{3,0},{4,70},{5,6},{6,68},{7,4},{8,74},{9,10},... | collective-permute-start | bytes 1622024 | tf_op jit(solution)/shard_map/ppermute | solution.py:254
  91.4 16.0 %collective-permute-start.3 = (s16[264,1024]{1,0:T(8,128)(2,1)S(1)}, s16[264,1024]{1,0:T(8,128)(2,1)S(1)}, u32[]{:S(2)}, u32[]{:S(2)}) collective-permute-start(s16[264,1024]{1,0:T(8,128)(2,1)S(1)} %shard_map.50), channel_id=1, source_target_pairs={{0,0},{1,64},{2,2},{3,66},{4,4},{5,68},{6,6},{7,70},{8,8},{9,72},{... | collective-permute-start | bytes 1622024 | tf_op jit(solution)/shard_map/ppermute | solution.py:254
  95.1 12.2 %collective-permute-start.4 = (s16[264,1024]{1,0:T(8,128)(2,1)S(1)}, s16[264,1024]{1,0:T(8,128)(2,1)S(1)}, u32[]{:S(2)}, u32[]{:S(2)}) collective-permute-start(s16[264,1024]{1,0:T(8,128)(2,1)S(1)} %shard_map.51), channel_id=1, source_target_pairs={{0,64},{1,0},{2,66},{3,2},{4,68},{5,4},{6,70},{7,6},{8,72},{9,8},{... | collective-permute-start | bytes 1622024 | tf_op jit(solution)/shard_map/ppermute | solution.py:254

commit v6 on v3

v6 whole, which is shorter than its diff:
```python
import jax
import jax.numpy as jnp
from jax import lax
from jax.experimental import pallas as pl
from jax.experimental.pallas import tpu as pltpu
from jax.sharding import PartitionSpec as P

NB = 8
CAP = 2
NX = 4
UNIT = 8
CORES = 2
PAIR = 2
TOP = 32767.0
STEPS = 64.0
TINY = 1e-30
VMEM = pl.BlockSpec(memory_space=pltpu.VMEM)
SMEM = pl.BlockSpec(memory_space=pltpu.SMEM)
PARAMS = pltpu.CompilerParams(vmem_limit_bytes=40 << 20)


def code_of(largest):
    return jnp.ceil(jnp.log2(jnp.maximum(largest, TINY)) * STEPS)


def coded(values, code):
    scaled = values * (jnp.exp2(code * (-1.0 / STEPS)) * (TOP - 1.0))
    return jnp.round(scaled).astype(jnp.int32).astype(jnp.int16)


def scale_of(code16):
    code = code16.astype(jnp.int32).astype(jnp.float32)
    return jnp.exp2(code * (1.0 / STEPS)) * (1.0 / (TOP - 1.0))


def plain(values16):
    return values16.astype(jnp.int32).astype(jnp.float32)


def pack(tile_dev, amp, block, index, out, rows, blocks, tiles, keys, count, sems):
    owners, _, lanes = keys.shape
    units = rows.shape[1] // UNIT
    pairs = ((index, tiles), (block, blocks), (amp, rows))
    copies = [pltpu.make_async_copy(a, b, sems.at[n]) for n, (a, b) in enumerate(pairs)]
    for copy in copies:
        copy.start()

    def clear(o, _):
        count[o] = 0
        return 0

    lax.fori_loop(0, owners, clear, 0)
    keys[...] = jnp.full(keys.shape, -1.0, jnp.float32)
    for copy in copies:
        copy.wait()
    for r in range(rows.shape[0]):
        tile = tiles[r]
        owner = tile // tile_dev
        rank = count[owner]
        count[owner] = rank + 1
        key = blocks[r] * tile_dev + (tile - owner * tile_dev)
        for u in range(units):
            out[owner, rank * units + u] = rows[r, u * UNIT : (u + 1) * UNIT, :]
        keys[owner, pl.ds(rank, 1), :] = jnp.full((1, lanes), key, jnp.int32).astype(jnp.float32)
    for o in range(owners):
        out[o, CAP * units] = keys[o].astype(out.dtype)


def place(tile_dev, got, out, held, dense, row, key, sems):
    sources, units, _, width = got.shape
    units = (units - 1) // CAP
    line = lax.broadcasted_iota(jnp.int32, (UNIT, width), 0)
    lane = lax.broadcasted_iota(jnp.int32, (UNIT, width), 1)
    slot = jnp.where(line < CAP, lane - line, -1)
    marks = jnp.zeros((UNIT, width), jnp.float32)
    for s in range(sources):
        marks = jnp.where(slot == CAP * s, got[s, CAP * units].astype(jnp.float32), marks)
    row[...] = jnp.sum(marks, axis=0, keepdims=True).astype(jnp.int32)
    targets = out.shape[0]
    copy = pltpu.make_async_copy(row, key, sems.at[targets])
    copy.start()
    copy.wait()
    spare = NB * tile_dev
    for s in range(sources):
        for r in range(CAP):
            k = key[0, s * CAP + r]
            to = jnp.where(k < 0, spare, k)
            for u in range(units):
                held[to, u] = got[s, r * units + u]
    for b in range(NB):
        for t in range(tile_dev):
            for u in range(units):
                at = (b * units + u) * UNIT
                dense[at : at + UNIT, t * width : (t + 1) * width] = held[b * tile_dev + t, u]
    copies = [pltpu.make_async_copy(dense, out.at[y], sems.at[y]) for y in range(targets)]
    for copy in copies:
        copy.start()
    for copy in copies:
        copy.wait()


def multiply(a, mine, theirs, which, *outs):
    rows, cols = a.shape[1], outs[0].shape[1]

    def block(v, slice_at):
        p = jnp.dot(a[slice_at], v[...], preferred_element_type=jnp.float32).reshape(rows // 8, 8, cols)
        code = code_of(jnp.max(jnp.abs(p), axis=0))
        return coded(p, code[None]).reshape(rows, cols), code.astype(jnp.int32).astype(jnp.int16)

    def put(out, values, code):
        out[:rows, :] = values
        out[rows:, :] = code

    for n in range(len(outs) // CORES):
        first, second = outs[n * CORES : (n + 1) * CORES]
        for v, near in ((mine, 0), (theirs, 1)):
            values, code = block(v, which[n])

            @pl.when(which[CORES] == near)
            def _(first=first, values=values, code=code):
                put(first, values, code)

            @pl.when(which[CORES] != near)
            def _(second=second, values=values, code=code):
                put(second, values, code)


def recoded(tiles, out, z):
    largest = jnp.abs(tiles[0])
    for tile in tiles[1:]:
        largest = jnp.maximum(largest, jnp.abs(tile))
    code = code_of(largest)
    lines = code.shape[0]
    for t, tile in enumerate([*tiles, None]):
        out[z, t * lines : (t + 1) * lines, :] = (
            code.astype(jnp.int32).astype(jnp.int16) if tile is None else coded(tile, code)
        )


def decoded(got, lines):
    sources, count = got.shape[0], got.shape[1] // lines - 1
    scales = [scale_of(got[s, count * lines :, :]) for s in range(sources)]
    tiles = []
    for t in range(count):
        total = None
        for s in range(sources):
            term = plain(got[s, t * lines : (t + 1) * lines, :]) * scales[s]
            total = term if total is None else total + term
        tiles.append(total)
    return tiles


def add_x(*refs):
    *gots, out = refs
    rows, cols = gots[0].shape[0] - 8, gots[0].shape[1]
    occ = rows // NB
    scales = [scale_of(got[rows:, :]) for got in gots]
    for b in range(NB):
        tiles = []
        for u in range(occ // UNIT):
            total = None
            at = b * occ + u * UNIT
            for got, scale in zip(gots, scales):
                term = plain(got[at : at + UNIT, :]) * scale
                total = term if total is None else total + term
            tiles += [total[:, 128 * t : 128 * (t + 1)] for t in range(cols // 128)]
        recoded(tiles, out, b)


def add_z(got, out):
    lanes = out.shape[1] // 128
    for n, tile in enumerate(decoded(got, UNIT)):
        u, t = n // lanes, n % lanes
        out[u * UNIT : (u + 1) * UNIT, 128 * t : 128 * (t + 1)] = tile


def call(body, out, ins, scratch=(), place_of=VMEM):
    specs = [place_of] * len(out) if isinstance(out, list) else place_of
    return pl.pallas_call(
        body, out_shape=out, in_specs=ins, out_specs=specs, scratch_shapes=list(scratch), compiler_params=PARAMS
    )


def local(amplitudes, integrals, tile_block, tile_index):
    own, grp = lax.axis_size("own"), lax.axis_size("grp")
    nz, ny = own // NX, grp // CORES
    z_groups = [[z * NX + x for z in range(p, nz, PAIR)] for p in range(PAIR) for x in range(NX)]
    y_groups = [[y * CORES + c for y in range(ny)] for c in range(CORES)]
    core_pairs = [(y * CORES + c, y * CORES + 1 - c) for y in range(ny) for c in range(CORES)]

    def target(near, r, x, z):
        return (1 - near) ^ (x // CORES), (r // CORES) ^ (z % PAIR), (r % CORES) ^ (x % CORES)

    def round_pairs(near, r):
        pairs = []
        for g in range(grp):
            for o in range(own):
                y, c, z, x = g // CORES, g % CORES, o // NX, o % NX
                a, parity, to = target(near, r, x, z)
                if parity != z % PAIR:
                    z = (z + 1 if z % PAIR == c else z - 1) % nz
                pairs.append((g * own + o, (y * CORES + to) * own + z * NX + a * CORES + c))
        return pairs

    def exchange(array, groups=None, axis="own"):
        return lax.all_to_all(array, axis, 0, 0, axis_index_groups=groups, tiled=True)

    _, occ, width = amplitudes.shape
    units = occ // UNIT
    tile_dev = integrals.shape[0] // width
    cols = integrals.shape[1]
    rows = NB * occ
    tiles = cols // 128
    dtype = amplitudes.dtype
    struct = jax.ShapeDtypeStruct
    core = lax.axis_index("grp") % CORES
    x = lax.axis_index("own") % NX
    z = lax.axis_index("own") // NX
    anywhere = pl.BlockSpec(memory_space=pl.ANY)

    packed = call(
        lambda *refs: pack(tile_dev, *refs),
        struct((own, CAP * units + 1, UNIT, width), dtype),
        [pl.BlockSpec(memory_space=pltpu.HBM)] * 3,
        [
            pltpu.VMEM(amplitudes.shape, dtype),
            pltpu.SMEM(tile_block.shape, jnp.int32),
            pltpu.SMEM(tile_index.shape, jnp.int32),
            pltpu.VMEM((own, UNIT, width), jnp.float32),
            pltpu.SMEM((own,), jnp.int32),
            pltpu.SemaphoreType.DMA((3,)),
        ],
    )(amplitudes, tile_block, tile_index)
    theirs = lax.ppermute(integrals, "grp", core_pairs)
    copies = call(
        lambda *refs: place(tile_dev, *refs),
        struct((ny, rows, tile_dev * width), dtype),
        [VMEM],
        [
            pltpu.VMEM((NB * tile_dev + 1, units, UNIT, width), dtype),
            pltpu.VMEM((rows, tile_dev * width), dtype),
            pltpu.VMEM((1, width), jnp.int32),
            pltpu.SMEM((1, width), jnp.int32),
            pltpu.SemaphoreType.DMA((ny + 1,)),
        ],
        anywhere,
    )(exchange(packed))
    mine = exchange(copies, y_groups, "grp")
    gots = []
    for near in range(NX // CORES):
        rounds = [target(near, r, x, z) for r in range(PAIR * CORES)]
        which = [a + (NX // CORES) * parity for a, parity, _ in rounds[::CORES]] + [rounds[0][2] ^ core]
        sent = call(
            multiply, [struct((rows + 8, cols), jnp.int16)] * len(rounds), [VMEM, VMEM, VMEM, SMEM]
        )(mine, integrals, theirs, jnp.stack(which).astype(jnp.int32))
        order = sorted(range(len(rounds)), reverse=True)
        gots += [lax.ppermute(sent[r], ("grp", "own"), round_pairs(near, r)) for r in order]
    sent = call(add_x, struct((NB, (units * tiles + 1) * UNIT, 128), jnp.int16), [VMEM] * len(gots))(*gots)
    return call(add_z, struct((occ, cols), jnp.float32), [VMEM])(exchange(sent, z_groups))


def solution(mesh):
    return jax.shard_map(
        local,
        mesh=mesh,
        in_specs=(P("own", "grp", None), P("own", "grp"), P("own"), P("own")),
        out_specs=P("own", "grp"),
        check_vma=False,
    )
```

time: 156 us -> 154 us (0.987)
  the two profiles are of different devices: /device:TPU:6 before, /device:TPU:1 now
where the time goes in v6:
time: 154 us; the launch traced here: 153 us
  starting transfers between devices  60.9 us (40%)
  waiting for transfers between devices  53.5 us (35%)
  blocking collectives  24.6 us (16%)
  Pallas kernels  11.6 us (8%)
  local copies, waits for them, and re-layouts  2.24 us (1%)
    all_to_all x2, waiting for transfers between devices, exchange(): lax.all_to_all(array, axis, 0, 0, axis_index_groups=groups, tiled=True)  40.3 us
    ppermute x8, starting transfers between devices, local(): lax.ppermute(sent[r], ('grp', 'own'), round_pairs(near, r))  34.8 us
    all_to_all x1, blocking collectives, exchange(): lax.all_to_all(array, axis, 0, 0, axis_index_groups=groups, tiled=True)  24.6 us
    all_to_all x2, starting transfers between devices, exchange(): lax.all_to_all(array, axis, 0, 0, axis_index_groups=groups, tiled=True)  23.3 us
    ppermute x8, waiting for transfers between devices, local(): lax.ppermute(sent[r], ('grp', 'own'), round_pairs(near, r))  13.2 us
    pallas_call x2, Pallas kernels, local(): call(multiply, [struct((rows + 8, cols), jnp.int16)] * len(rounds), [VMEM...  6.42 us
  transfers between devices with their start and end apart: 11, of which 5 were waited for; matrix products, arithmetic and copies ran while one was open for 0% of the time, Pallas kernels for 3%

profile of v6, /device:TPU:1, one launch (start us, length us, event | category | flops | bytes accessed | tf_op | source)
XLA Modules:
  0.0 153.2 jit_solution(2454441400673225246)
XLA Ops:
  0.0 0.9 copy-done.1
  2.2 2.0 %shard_map.46 = bf16[64,5,8,128]{3,2,1,0:T(8,128)(2,1)} custom-call(bf16[48,16,128]{2,1,0:T(8,128)(2,1)S(1)} %copy-done.1, s32[48]{0:T(128)S(1)} %copy-done.2, s32[48]{0:T(128)S(1)} %copy-done.3), custom_call_target="tpu_custom_call" | custom-call | tf_op jit(solution)/shard_map/pallas_call | solution.py:221
  4.2 19.1 %all-to-all-start = ((bf16[64,5,8,128]{3,2,1,0:T(8,128)(2,1)}), bf16[64,5,8,128]{3,2,1,0:T(8,128)(2,1)S(1)}, u32[]{:S(2)}, u32[]{:S(2)}) async-start(bf16[64,5,8,128]{3,2,1,0:T(8,128)(2,1)} %shard_map.46), calls=%async_computation | async-start | bytes 1310720 | tf_op jit(solution)/shard_map/all_to_all | solution.py:206
  23.4 2.9 %collective-permute-start = (bf16[768,1024]{1,0:T(8,128)(2,1)S(1)}, bf16[768,1024]{1,0:T(8,128)(2,1)}, u32[]{:S(2)}, u32[]{:S(2)}) collective-permute-start(bf16[768,1024]{1,0:T(8,128)(2,1)S(1)} %copy-done), channel_id=1, source_target_pairs={{0,64},{64,0},{128,192},{192,128},{256,320},{320,256},{384,448},{4... | collective-permute-start | bytes 4718600 | tf_op jit(solution)/shard_map/ppermute | solution.py:234
  26.2 32.0 %all-to-all-done.refs_0_ = bf16[64,5,8,128]{3,2,1,0:T(8,128)(2,1)S(1)} async-done(((bf16[64,5,8,128]{3,2,1,0:T(8,128)(2,1)}), bf16[64,5,8,128]{3,2,1,0:T(8,128)(2,1)S(1)}, u32[]{:S(2)}, u32[]{:S(2)}) %all-to-all-start) | async-done | bytes 655392 | tf_op jit(solution)/shard_map/all_to_all | solution.py:206
  58.3 1.7 %shard_map.47 = bf16[4,128,768]{2,1,0:T(8,128)(2,1)} custom-call(bf16[64,5,8,128]{3,2,1,0:T(8,128)(2,1)S(1)} %all-to-all-done.refs_0_), custom_call_target="tpu_custom_call" | custom-call | tf_op jit(solution)/shard_map/pallas_call | solution.py:235
  60.0 4.2 %all-to-all-start.1 = ((bf16[4,128,768]{2,1,0:T(8,128)(2,1)}), bf16[4,128,768]{2,1,0:T(8,128)(2,1)S(1)}, u32[]{:S(2)}, u32[]{:S(2)}) async-start(bf16[4,128,768]{2,1,0:T(8,128)(2,1)} %shard_map.47), calls=%async_computation.1 | async-start | bytes 1572864 | tf_op jit(solution)/shard_map/all_to_all | solution.py:206
  64.3 8.3 %all-to-all-done.1.a = bf16[4,128,768]{2,1,0:T(8,128)(2,1)S(1)} async-done(((bf16[4,128,768]{2,1,0:T(8,128)(2,1)}), bf16[4,128,768]{2,1,0:T(8,128)(2,1)S(1)}, u32[]{:S(2)}, u32[]{:S(2)}) %all-to-all-start.1) | async-done | bytes 786464 | tf_op jit(solution)/shard_map/all_to_all | solution.py:206
  72.5 3.2 %shard_map.49 = (s16[136,1024]{1,0:T(8,128)(2,1)S(1)}, s16[136,1024]{1,0:T(8,128)(2,1)S(1)}, s16[136,1024]{1,0:T(8,128)(2,1)S(1)}, s16[136,1024]{1,0:T(8,128)(2,1)S(1)}) custom-call(bf16[4,128,768]{2,1,0:T(8,128)(2,1)S(1)} %all-to-all-done.1.a, bf16[768,1024]{1,0:T(8,128)(2,1)S(1)} %copy-done, bf16[768,1024]{1,0:T(8,128)(2,1)} %collective-permute-done.theirs, ...), custom_call_target="tpu_custom_call" | custom-call | tf_op jit(solution)/shard_map/pallas_call | solution.py:253
  75.7 1.9 %collective-permute-start.5 = (s16[136,1024]{1,0:T(8,128)(2,1)S(1)}, s16[136,1024]{1,0:T(8,128)(2,1)S(1)}, u32[]{:S(2)}, u32[]{:S(2)}) collective-permute-start(s16[136,1024]{1,0:T(8,128)(2,1)S(1)} %get-tuple-element.17), channel_id=1, source_target_pairs={{0,68},{1,4},{2,70},{3,6},{4,64},{5,0},{6,66},{7,2},{8,76},{9,12},... | collective-permute-start | bytes 835592 | tf_op jit(solution)/shard_map/ppermute | solution.py:257
  77.7 12.3 %collective-permute-start.6 = (s16[136,1024]{1,0:T(8,128)(2,1)S(1)}, s16[136,1024]{1,0:T(8,128)(2,1)S(1)}, u32[]{:S(2)}, u32[]{:S(2)}) collective-permute-start(s16[136,1024]{1,0:T(8,128)(2,1)S(1)} %get-tuple-element.18), channel_id=1, source_target_pairs={{0,4},{1,68},{2,6},{3,70},{4,0},{5,64},{6,2},{7,66},{8,12},{9,76},... | collective-permute-start | bytes 835592 | tf_op jit(solution)/shard_map/ppermute | solution.py:257
  89.9 1.9 %collective-permute-start.7 = (s16[136,1024]{1,0:T(8,128)(2,1)S(1)}, s16[136,1024]{1,0:T(8,128)(2,1)S(1)}, u32[]{:S(2)}, u32[]{:S(2)}) collective-permute-start(s16[136,1024]{1,0:T(8,128)(2,1)S(1)} %get-tuple-element.19), channel_id=1, source_target_pairs={{0,64},{1,0},{2,66},{3,2},{4,68},{5,4},{6,70},{7,6},{8,72},{9,8},{... | collective-permute-start | bytes 835592 | tf_op jit(solution)/shard_map/ppermute | solution.py:257
  91.9 1.9 %collective-permute-start.8 = (s16[136,1024]{1,0:T(8,128)(2,1)S(1)}, s16[136,1024]{1,0:T(8,128)(2,1)S(1)}, u32[]{:S(2)}, u32[]{:S(2)}) collective-permute-start(s16[136,1024]{1,0:T(8,128)(2,1)S(1)} %get-tuple-element.20), channel_id=1, source_target_pairs={{0,0},{1,64},{2,2},{3,66},{4,4},{5,68},{6,6},{7,70},{8,8},{9,72},{... | collective-permute-start | bytes 835592 | tf_op jit(solution)/shard_map/ppermute | solution.py:257
  93.8 3.2 %shard_map.48 = (s16[136,1024]{1,0:T(8,128)(2,1)S(1)}, s16[136,1024]{1,0:T(8,128)(2,1)S(1)}, s16[136,1024]{1,0:T(8,128)(2,1)S(1)}, s16[136,1024]{1,0:T(8,128)(2,1)S(1)}) custom-call(bf16[4,128,768]{2,1,0:T(8,128)(2,1)S(1)} %all-to-all-done.1.a, bf16[768,1024]{1,0:T(8,128)(2,1)S(1)} %copy-done, bf16[768,1024]{1,0:T(8,128)(2,1)} %collective-permute-done.theirs, ...), custom_call_target="tpu_custom_call" | custom-call | tf_op jit(solution)/shard_map/pallas_call | solution.py:253
  97.0 2.7 %collective-permute-start.1 = (s16[136,1024]{1,0:T(8,128)(2,1)S(1)}, s16[136,1024]{1,0:T(8,128)(2,1)S(1)}, u32[]{:S(2)}, u32[]{:S(2)}) collective-permute-start(s16[136,1024]{1,0:T(8,128)(2,1)S(1)} %get-tuple-element.13), channel_id=1, source_target_pairs={{0,70},{1,6},{2,68},{3,4},{4,66},{5,2},{6,64},{7,0},{8,78},{9,14},... | collective-permute-start | bytes 835592 | tf_op jit(solution)/shard_map/ppermute | solution.py:257
  99.7 4.9 %collective-permute-start.2 = (s16[136,1024]{1,0:T(8,128)(2,1)S(1)}, s16[136,1024]{1,0:T(8,128)(2,1)S(1)}, u32[]{:S(2)}, u32[]{:S(2)}) collective-permute-start(s16[136,1024]{1,0:T(8,128)(2,1)S(1)} %get-tuple-element.14), channel_id=1, source_target_pairs={{0,6},{1,70},{2,4},{3,68},{4,2},{5,66},{6,0},{7,64},{8,14},{9,78},... | collective-permute-start | bytes 835592 | tf_op jit(solution)/shard_map/ppermute | solution.py:257
  104.6 7.3 %collective-permute-start.3 = (s16[136,1024]{1,0:T(8,128)(2,1)S(1)}, s16[136,1024]{1,0:T(8,128)(2,1)S(1)}, u32[]{:S(2)}, u32[]{:S(2)}) collective-permute-start(s16[136,1024]{1,0:T(8,128)(2,1)S(1)} %get-tuple-element.15), channel_id=1, source_target_pairs={{0,66},{1,2},{2,64},{3,0},{4,70},{5,6},{6,68},{7,4},{8,74},{9,10},... | collective-permute-start | bytes 835592 | tf_op jit(solution)/shard_map/ppermute | solution.py:257
  111.9 1.9 %collective-permute-start.4 = (s16[136,1024]{1,0:T(8,128)(2,1)S(1)}, s16[136,1024]{1,0:T(8,128)(2,1)S(1)}, u32[]{:S(2)}, u32[]{:S(2)}) collective-permute-start(s16[136,1024]{1,0:T(8,128)(2,1)S(1)} %get-tuple-element.16), channel_id=1, source_target_pairs={{0,2},{1,66},{2,0},{3,64},{4,6},{5,70},{6,4},{7,68},{8,10},{9,74},... | collective-permute-start | bytes 835592 | tf_op jit(solution)/shard_map/ppermute | solution.py:257
  113.8 0.9 collective-permute-done.2.refs_1_
  114.7 9.0 %collective-permute-done.3.refs_2_ = s16[136,1024]{1,0:T(8,128)(2,1)S(1)} collective-permute-done((s16[136,1024]{1,0:T(8,128)(2,1)S(1)}, s16[136,1024]{1,0:T(8,128)(2,1)S(1)}, u32[]{:S(2)}, u32[]{:S(2)}) %collective-permute-start.3) | collective-permute-done | bytes 278560 | tf_op jit(solution)/shard_map/ppermute | solution.py:257
  123.7 3.3 %collective-permute-done.4.refs_3_ = s16[136,1024]{1,0:T(8,128)(2,1)S(1)} collective-permute-done((s16[136,1024]{1,0:T(8,128)(2,1)S(1)}, s16[136,1024]{1,0:T(8,128)(2,1)S(1)}, u32[]{:S(2)}, u32[]{:S(2)}) %collective-permute-start.4) | collective-permute-done | bytes 278560 | tf_op jit(solution)/shard_map/ppermute | solution.py:257
  127.0 0.8 shard_map.50
  127.8 24.6 %all_to_all.15.got = s16[8,136,128]{2,1,0:T(8,128)(2,1)S(1)} all-to-all(s16[8,136,128]{2,1,0:T(8,128)(2,1)S(1)} %shard_map.50), channel_id=1, replica_groups={{0,8,16,24,32,40,48,56},{1,9,17,25,33,41,49,57},{2,10,18,26,34,42,50,58..., dimensions={0} | all-to-all | bytes 557056 | tf_op jit(solution)/shard_map/all_to_all | solution.py:206
  152.4 0.7 shard_map.51
  (14 shorter events, 1.4 us)
Async XLA Ops:
  0.0 0.9 copy-start.1
  0.9 0.7 copy-start.2
  1.6 0.7 copy-start.3
  2.2 21.1 %copy-start = (bf16[768,1024]{1,0:T(8,128)(2,1)S(1)}, bf16[768,1024]{1,0:T(8,128)(2,1)}, u32[]{:S(2)}) copy-start(bf16[768,1024]{1,0:T(8,128)(2,1)} %mine.3) | copy-start | bytes 4718596
  4.2 54.0 %all-to-all-start = ((bf16[64,5,8,128]{3,2,1,0:T(8,128)(2,1)}), bf16[64,5,8,128]{3,2,1,0:T(8,128)(2,1)S(1)}, u32[]{:S(2)}, u32[]{:S(2)}) async-start(bf16[64,5,8,128]{3,2,1,0:T(8,128)(2,1)} %shard_map.46), calls=%async_computation | async-start | bytes 1310720 | tf_op jit(solution)/shard_map/all_to_all | solution.py:206
  23.4 40.9 %collective-permute-start = (bf16[768,1024]{1,0:T(8,128)(2,1)S(1)}, bf16[768,1024]{1,0:T(8,128)(2,1)}, u32[]{:S(2)}, u32[]{:S(2)}) collective-permute-start(bf16[768,1024]{1,0:T(8,128)(2,1)S(1)} %copy-done), channel_id=1, source_target_pairs={{0,64},{64,0},{128,192},{192,128},{256,320},{320,256},{384,448},{4... | collective-permute-start | bytes 4718600 | tf_op jit(solution)/shard_map/ppermute | solution.py:234
  60.0 12.5 %all-to-all-start.1 = ((bf16[4,128,768]{2,1,0:T(8,128)(2,1)}), bf16[4,128,768]{2,1,0:T(8,128)(2,1)S(1)}, u32[]{:S(2)}, u32[]{:S(2)}) async-start(bf16[4,128,768]{2,1,0:T(8,128)(2,1)} %shard_map.47), calls=%async_computation.1 | async-start | bytes 1572864 | tf_op jit(solution)/shard_map/all_to_all | solution.py:206
  75.7 24.0 %collective-permute-start.5 = (s16[136,1024]{1,0:T(8,128)(2,1)S(1)}, s16[136,1024]{1,0:T(8,128)(2,1)S(1)}, u32[]{:S(2)}, u32[]{:S(2)}) collective-permute-start(s16[136,1024]{1,0:T(8,128)(2,1)S(1)} %get-tuple-element.17), channel_id=1, source_target_pairs={{0,68},{1,4},{2,70},{3,6},{4,64},{5,0},{6,66},{7,2},{8,76},{9,12},... | collective-permute-start | bytes 835592 | tf_op jit(solution)/shard_map/ppermute | solution.py:257
  77.7 26.9 %collective-permute-start.6 = (s16[136,1024]{1,0:T(8,128)(2,1)S(1)}, s16[136,1024]{1,0:T(8,128)(2,1)S(1)}, u32[]{:S(2)}, u32[]{:S(2)}) collective-permute-start(s16[136,1024]{1,0:T(8,128)(2,1)S(1)} %get-tuple-element.18), channel_id=1, source_target_pairs={{0,4},{1,68},{2,6},{3,70},{4,0},{5,64},{6,2},{7,66},{8,12},{9,76},... | collective-permute-start | bytes 835592 | tf_op jit(solution)/shard_map/ppermute | solution.py:257
  89.9 21.9 %collective-permute-start.7 = (s16[136,1024]{1,0:T(8,128)(2,1)S(1)}, s16[136,1024]{1,0:T(8,128)(2,1)S(1)}, u32[]{:S(2)}, u32[]{:S(2)}) collective-permute-start(s16[136,1024]{1,0:T(8,128)(2,1)S(1)} %get-tuple-element.19), channel_id=1, source_target_pairs={{0,64},{1,0},{2,66},{3,2},{4,68},{5,4},{6,70},{7,6},{8,72},{9,8},{... | collective-permute-start | bytes 835592 | tf_op jit(solution)/shard_map/ppermute | solution.py:257
  91.9 22.0 %collective-permute-start.8 = (s16[136,1024]{1,0:T(8,128)(2,1)S(1)}, s16[136,1024]{1,0:T(8,128)(2,1)S(1)}, u32[]{:S(2)}, u32[]{:S(2)}) collective-permute-start(s16[136,1024]{1,0:T(8,128)(2,1)S(1)} %get-tuple-element.20), channel_id=1, source_target_pairs={{0,0},{1,64},{2,2},{3,66},{4,4},{5,68},{6,6},{7,70},{8,8},{9,72},{... | collective-permute-start | bytes 835592 | tf_op jit(solution)/shard_map/ppermute | solution.py:257
  97.0 16.8 %collective-permute-start.1 = (s16[136,1024]{1,0:T(8,128)(2,1)S(1)}, s16[136,1024]{1,0:T(8,128)(2,1)S(1)}, u32[]{:S(2)}, u32[]{:S(2)}) collective-permute-start(s16[136,1024]{1,0:T(8,128)(2,1)S(1)} %get-tuple-element.13), channel_id=1, source_target_pairs={{0,70},{1,6},{2,68},{3,4},{4,66},{5,2},{6,64},{7,0},{8,78},{9,14},... | collective-permute-start | bytes 835592 | tf_op jit(solution)/shard_map/ppermute | solution.py:257
  99.7 15.0 %collective-permute-start.2 = (s16[136,1024]{1,0:T(8,128)(2,1)S(1)}, s16[136,1024]{1,0:T(8,128)(2,1)S(1)}, u32[]{:S(2)}, u32[]{:S(2)}) collective-permute-start(s16[136,1024]{1,0:T(8,128)(2,1)S(1)} %get-tuple-element.14), channel_id=1, source_target_pairs={{0,6},{1,70},{2,4},{3,68},{4,2},{5,66},{6,0},{7,64},{8,14},{9,78},... | collective-permute-start | bytes 835592 | tf_op jit(solution)/shard_map/ppermute | solution.py:257
  104.6 19.1 %collective-permute-start.3 = (s16[136,1024]{1,0:T(8,128)(2,1)S(1)}, s16[136,1024]{1,0:T(8,128)(2,1)S(1)}, u32[]{:S(2)}, u32[]{:S(2)}) collective-permute-start(s16[136,1024]{1,0:T(8,128)(2,1)S(1)} %get-tuple-element.15), channel_id=1, source_target_pairs={{0,66},{1,2},{2,64},{3,0},{4,70},{5,6},{6,68},{7,4},{8,74},{9,10},... | collective-permute-start | bytes 835592 | tf_op jit(solution)/shard_map/ppermute | solution.py:257
  111.9 15.1 %collective-permute-start.4 = (s16[136,1024]{1,0:T(8,128)(2,1)S(1)}, s16[136,1024]{1,0:T(8,128)(2,1)S(1)}, u32[]{:S(2)}, u32[]{:S(2)}) collective-permute-start(s16[136,1024]{1,0:T(8,128)(2,1)S(1)} %get-tuple-element.16), channel_id=1, source_target_pairs={{0,2},{1,66},{2,0},{3,64},{4,6},{5,70},{6,4},{7,68},{8,10},{9,74},... | collective-permute-start | bytes 835592 | tf_op jit(solution)/shard_map/ppermute | solution.py:257

commit v7 on v5

--- a/solution.py
+++ b/solution.py
@@ -11,12 +11,14 @@
 UNIT = 8
 CORES = 2
 LOWS = 4
+LINES = 2
 TOP = 32767.0
 STEPS = 64.0
 TINY = 1e-30
 VMEM = pl.BlockSpec(memory_space=pltpu.VMEM)
 SMEM = pl.BlockSpec(memory_space=pltpu.SMEM)
-PARAMS = pltpu.CompilerParams(vmem_limit_bytes=40 << 20)
+GRANT = 40 << 20
+WHOLE = 64 << 20
 
 
 def code_of(largest):
@@ -37,9 +39,13 @@
     return values16.astype(jnp.int32).astype(jnp.float32)
 
 
-def pack(tile_dev, amp, block, index, out, keys, count):
-    owners, _, lanes = keys.shape
-    units = amp.shape[1] // UNIT
+def pack(tile_dev, amp, block, index, out, rows, blocks, tiles, keys, count, sems):
+    owners, lanes = keys.shape[0] // LINES, keys.shape[1]
+    units = rows.shape[1]
+    pairs = ((index, tiles), (block, blocks), (amp, rows))
+    copies = [pltpu.make_async_copy(a, b, sems.at[n]) for n, (a, b) in enumerate(pairs)]
+    for copy in copies:
+        copy.start()
 
     def clear(o, _):
         count[o] = 0
@@ -47,56 +53,62 @@
 
     lax.fori_loop(0, owners, clear, 0)
     keys[...] = jnp.full(keys.shape, -1.0, jnp.float32)
-    for r in range(amp.shape[0]):
-        tile = index[r]
+    for copy in copies:
+        copy.wait()
+    for r in range(rows.shape[0]):
+        tile = tiles[r]
         owner = tile // tile_dev
         rank = count[owner]
         count[owner] = rank + 1
-        key = block[r] * tile_dev + (tile - owner * tile_dev)
-        for u in range(units):
-            out[owner, rank * units + u] = amp[r, u * UNIT : (u + 1) * UNIT, :]
-        keys[owner, pl.ds(rank, 1), :] = jnp.full((1, lanes), key, jnp.int32).astype(jnp.float32)
+        key = blocks[r] * tile_dev + (tile - owner * tile_dev)
+        out[owner, pl.ds(rank * units, units)] = rows[r]
+        line = owner * LINES + rank
+        keys[pl.ds(line, 1), :] = jnp.full((1, lanes), key, jnp.int32).astype(jnp.float32)
     for o in range(owners):
-        out[o, CAP * units] = keys[o].astype(out.dtype)
-
-
-def place(tile_dev, got, out, held, row, key, sem):
-    sources, units, _, width = got.shape
+        out[o, CAP * units] = keys[o * LINES : (o + 1) * LINES, :].astype(out.dtype)
+
+
+def place(tile_dev, got, out, held, row, key, sems):
+    sources, units, lines, width = got.shape
     units = (units - 1) // CAP
-    line = lax.broadcasted_iota(jnp.int32, (UNIT, width), 0)
-    lane = lax.broadcasted_iota(jnp.int32, (UNIT, width), 1)
+    line = lax.broadcasted_iota(jnp.int32, (lines, width), 0)
+    lane = lax.broadcasted_iota(jnp.int32, (lines, width), 1)
     slot = jnp.where(line < CAP, lane - line, -1)
-    marks = jnp.zeros((UNIT, width), jnp.float32)
+    marks = jnp.zeros((lines, width), jnp.float32)
     for s in range(sources):
         marks = jnp.where(slot == CAP * s, got[s, CAP * units].astype(jnp.float32), marks)
     row[...] = jnp.sum(marks, axis=0, keepdims=True).astype(jnp.int32)
-    copy = pltpu.make_async_copy(row, key, sem)
+    targets, keys = out.shape[0], out.shape[1]
+    copy = pltpu.make_async_copy(row, key, sems.at[targets])
     copy.start()
     copy.wait()
-    spare = NB * tile_dev
     for s in range(sources):
         for r in range(CAP):
             k = key[0, s * CAP + r]
-            to = jnp.where(k < 0, spare, k)
-            for u in range(units):
-                held[to, u] = got[s, r * units + u]
-    for b in range(NB):
-        for t in range(tile_dev):
-            for u in range(units):
-                tile = held[b * tile_dev + t, u]
-                at = (b * units + u) * UNIT
-                for y in range(out.shape[0]):
-                    out[y, at : at + UNIT, t * width : (t + 1) * width] = tile
-
-
-def multiply(a, mine, theirs, which, out):
-    rows, cols = a.shape[1], out.shape[1]
+            held[jnp.where(k < 0, keys, k)] = got[s, r * units : (r + 1) * units]
+    copies = [pltpu.make_async_copy(held.at[pl.ds(0, keys)], out.at[y], sems.at[y]) for y in range(targets)]
+    for copy in copies:
+        copy.start()
+    for copy in copies:
+        copy.wait()
+
+
+def multiply(tile_dev, a, mine, theirs, which, out, left):
+    rows, width, cols = NB * a.shape[2], a.shape[3], out.shape[1]
+    occ = a.shape[2]
     half = NX // CORES
+    parts = a.shape[0] // half
+    for h in range(parts):
+        for b in range(NB):
+            for t in range(tile_dev):
+                at = h * rows + b * occ
+                left[at : at + occ, t * width : (t + 1) * width] = a[which[0] + half * h, b * tile_dev + t]
 
     def block(v):
         sums = [
-            jnp.dot(a[which[0] + half * h], v[...], preferred_element_type=jnp.float32).reshape(rows // 8, 8, cols)
-            for h in range(a.shape[0] // half)
+            jnp.dot(left[h * rows : (h + 1) * rows, :], v[...], preferred_element_type=jnp.float32)
+            .reshape(rows // 8, 8, cols)
+            for h in range(parts)
         ]
         largest = None
         for p in sums:
@@ -177,10 +189,15 @@
         out[u * UNIT : (u + 1) * UNIT, 128 * t : 128 * (t + 1)] = tile
 
 
-def call(body, out, ins, scratch=()):
-    specs = [VMEM] * len(out) if isinstance(out, list) else VMEM
+def call(body, out, ins, scratch=(), place_of=VMEM, grant=GRANT):
+    specs = [place_of] * len(out) if isinstance(out, list) else place_of
     return pl.pallas_call(
-        body, out_shape=out, in_specs=ins, out_specs=specs, scratch_shapes=list(scratch), compiler_params=PARAMS
+        body,
+        out_shape=out,
+        in_specs=ins,
+        out_specs=specs,
+        scratch_shapes=list(scratch),
+        compiler_params=pltpu.CompilerParams(vmem_limit_bytes=grant),
     )
 
 
@@ -225,32 +242,48 @@
     core = lax.axis_index("grp") % CORES
     x = lax.axis_index("own") % NX
 
+    anywhere = pl.BlockSpec(memory_space=pl.ANY)
+    lines = occ // LINES
+    keys = NB * tile_dev
     packed = call(
         lambda *refs: pack(tile_dev, *refs),
-        struct((own, CAP * units + 1, UNIT, width), dtype),
-        [VMEM, SMEM, SMEM],
-        [pltpu.VMEM((own, UNIT, width), jnp.float32), pltpu.SMEM((own,), jnp.int32)],
-    )(amplitudes, tile_block, tile_index)
+        struct((own, CAP * lines + 1, LINES, width), dtype),
+        [anywhere, anywhere, anywhere],
+        [
+            pltpu.VMEM((amplitudes.shape[0], lines, LINES, width), dtype),
+            pltpu.SMEM(tile_block.shape, jnp.int32),
+            pltpu.SMEM(tile_index.shape, jnp.int32),
+            pltpu.VMEM((own * LINES, width), jnp.float32),
+            pltpu.SMEM((own,), jnp.int32),
+            pltpu.SemaphoreType.DMA((3,)),
+        ],
+        grant=WHOLE,
+    )(amplitudes.reshape(-1, lines, LINES, width), tile_block, tile_index)
     theirs = lax.ppermute(integrals, "grp", core_pairs)
     copies = call(
         lambda *refs: place(tile_dev, *refs),
-        struct((ny, rows, tile_dev * width), dtype),
+        struct((ny, keys, lines, LINES, width), dtype),
         [VMEM],
         [
-            pltpu.VMEM((NB * tile_dev + 1, units, UNIT, width), dtype),
+            pltpu.VMEM((keys + 1, lines, LINES, width), dtype),
             pltpu.VMEM((1, width), jnp.int32),
             pltpu.SMEM((1, width), jnp.int32),
-            pltpu.SemaphoreType.DMA,
+            pltpu.SemaphoreType.DMA((ny + 1,)),
         ],
+        anywhere,
+        WHOLE,
     )(exchange(packed))
-    mine = exchange(copies, y_groups, "grp")
+    mine = exchange(copies, y_groups, "grp").reshape(ny, keys, occ, width)
     gots = []
     for r in (2, 3, 0, 1):
         a, to = target(r, x)
         which = jnp.stack([a, to ^ core]).astype(jnp.int32)
-        sent = call(multiply, struct((parts * rows + 8, cols), jnp.int16), [VMEM, VMEM, VMEM, SMEM])(
-            mine, integrals, theirs, which
-        )
+        sent = call(
+            lambda *refs: multiply(tile_dev, *refs),
+            struct((parts * rows + 8, cols), jnp.int16),
+            [VMEM, VMEM, VMEM, SMEM],
+            [pltpu.VMEM((parts * rows, tile_dev * width), dtype)],
+        )(mine, integrals, theirs, which)
         gots.append(lax.ppermute(sent, ("grp", "own"), round_pairs(r)))
     sent = call(
         lambda *refs: add_x(rows, *refs),

time: 147 us -> 141 us (0.959)
  waiting for transfers between devices: 56.8 us -> 51.5 us
  local copies, waits for them, and re-layouts: 3.15 us -> 0.01 us
  Pallas kernels: 13.2 us -> 15.3 us
    all_to_all x2, waiting for transfers between devices: 47.4 us -> 43.4 us  [exchange(): lax.all_to_all(array, axis, 0, 0, axis_index_groups=groups, tiled=True)]
    unnamed x10 -> x2, local copies, waits for them, and re-layouts: 3.15 us -> 0.01 us
    pallas_call x6, Pallas kernels: 11.6 us -> 13.6 us  [the longest x4 8.7 us: local(): call(lambda *refs: multiply(tile_dev, *refs), struct((parts * rows + 8, c...]
  transfers between devices with their start and end apart: 7 -> 7, of which waited for: 4 -> 4; matrix products, arithmetic and copies ran while one was open for 0% -> 0% of each run, Pallas kernels for 5% -> 7%
where the time goes in v7:
time: 141 us; the launch traced here: 139 us
  waiting for transfers between devices  51.5 us (37%)
  blocking collectives  35.9 us (25%)
  starting transfers between devices  35.5 us (25%)
  Pallas kernels  15.3 us (11%)
    all_to_all x2, waiting for transfers between devices, exchange(): lax.all_to_all(array, axis, 0, 0, axis_index_groups=groups, tiled=True)  43.4 us
    all_to_all x2, blocking collectives, exchange(): lax.all_to_all(array, axis, 0, 0, axis_index_groups=groups, tiled=True)  35.9 us
    all_to_all x2, starting transfers between devices, exchange(): lax.all_to_all(array, axis, 0, 0, axis_index_groups=groups, tiled=True)  23.4 us
    ppermute x4, starting transfers between devices, local(): gots.append(lax.ppermute(sent, ('grp', 'own'), round_pairs(r)))  10.2 us
    pallas_call x4, Pallas kernels, local(): call(lambda *refs: multiply(tile_dev, *refs), struct((parts * rows + 8, c...  8.7 us
    ppermute x4, waiting for transfers between devices, local(): gots.append(lax.ppermute(sent, ('grp', 'own'), round_pairs(r)))  8.09 us
  transfers between devices with their start and end apart: 7, of which 4 were waited for; matrix products, arithmetic and copies ran while one was open for 0% of the time, Pallas kernels for 7%

profile of v7, /device:TPU:6, one launch (start us, length us, event | category | flops | bytes accessed | tf_op | source)
XLA Modules:
  0.0 138.6 jit_solution(14282022009100051066)
XLA Ops:
  0.0 2.2 %shard_map.46 = bf16[64,17,2,128]{3,2,1,0:T(2,128)(2,1)} custom-call(bf16[48,8,2,128]{3,2,1,0:T(2,128)(2,1)} %bitcast.10, s32[48]{0:T(128)} %refs_1_.5, s32[48]{0:T(128)} %refs_2_.1), custom_call_target="tpu_custom_call" | custom-call | tf_op jit(solution)/shard_map/pallas_call | solution.py:248
  2.2 18.8 %all-to-all-start = ((bf16[64,17,2,128]{3,2,1,0:T(2,128)(2,1)}), bf16[64,17,2,128]{3,2,1,0:T(2,128)(2,1)}, u32[]{:S(2)}, u32[]{:S(2)}) async-start(bf16[64,17,2,128]{3,2,1,0:T(2,128)(2,1)} %shard_map.46), calls=%async_computation | async-start | bytes 1114112 | tf_op jit(solution)/shard_map/all_to_all | solution.py:231
  21.0 1.9 %collective-permute-start = (bf16[768,1024]{1,0:T(8,128)(2,1)}, bf16[768,1024]{1,0:T(8,128)(2,1)}, u32[]{:S(2)}, u32[]{:S(2)}) collective-permute-start(bf16[768,1024]{1,0:T(8,128)(2,1)} %refs_1_.9), channel_id=1, source_target_pairs={{0,64},{64,0},{128,192},{192,128},{256,320},{320,256},{384,448},{4... | collective-permute-start | bytes 4718600 | tf_op jit(solution)/shard_map/ppermute | solution.py:262
  22.9 32.1 %all-to-all-done.refs_0_ = bf16[64,17,2,128]{3,2,1,0:T(2,128)(2,1)} async-done(((bf16[64,17,2,128]{3,2,1,0:T(2,128)(2,1)}), bf16[64,17,2,128]{3,2,1,0:T(2,128)(2,1)}, u32[]{:S(2)}, u32[]{:S(2)}) %all-to-all-start) | async-done | bytes 557088 | tf_op jit(solution)/shard_map/all_to_all | solution.py:231
  55.0 2.7 %shard_map.47 = bf16[4,48,8,2,128]{4,3,2,1,0:T(2,128)(2,1)} custom-call(bf16[64,17,2,128]{3,2,1,0:T(2,128)(2,1)} %all-to-all-done.refs_0_), custom_call_target="tpu_custom_call" | custom-call | tf_op jit(solution)/shard_map/pallas_call | solution.py:263
  57.8 4.6 %all-to-all-start.1 = ((bf16[4,48,8,2,128]{4,3,2,1,0:T(2,128)(2,1)}), bf16[4,48,8,2,128]{4,3,2,1,0:T(2,128)(2,1)S(1)}, u32[]{:S(2)}, u32[]{:S(2)}) async-start(bf16[4,48,8,2,128]{4,3,2,1,0:T(2,128)(2,1)} %shard_map.47), calls=%async_computation.1 | async-start | bytes 1572864 | tf_op jit(solution)/shard_map/all_to_all | solution.py:231
  62.4 0.1 pad_add_fusion.2.refs_3_
  62.6 0.1 pad_add_fusion.refs_3_
  62.7 11.3 %all-to-all-done.1 = bf16[4,48,8,2,128]{4,3,2,1,0:T(2,128)(2,1)S(1)} async-done(((bf16[4,48,8,2,128]{4,3,2,1,0:T(2,128)(2,1)}), bf16[4,48,8,2,128]{4,3,2,1,0:T(2,128)(2,1)S(1)}, u32[]{:S(2)}, u32[]{:S(2)}) %all-to-all-start.1) | async-done | bytes 786464 | tf_op jit(solution)/shard_map/all_to_all | solution.py:231
  74.0 2.2 %shard_map.48 = s16[264,1024]{1,0:T(8,128)(2,1)S(1)} custom-call(bf16[4,48,16,128]{3,2,1,0:T(8,128)(2,1)S(1)} %bitcast.6, bf16[768,1024]{1,0:T(8,128)(2,1)S(1)} %copy-done, bf16[768,1024]{1,0:T(8,128)(2,1)} %collective-permute-done.refs_2_, s32[2]{0:T(128)S(1)} %pad_add_fusion.1.refs_3_), custom_call_target="tpu_custom_call" | custom-call | tf_op jit(solution)/shard_map/pallas_call | solution.py:281
  76.2 1.9 %collective-permute-start.1 = (s16[264,1024]{1,0:T(8,128)(2,1)S(1)}, s16[264,1024]{1,0:T(8,128)(2,1)S(1)}, u32[]{:S(2)}, u32[]{:S(2)}) collective-permute-start(s16[264,1024]{1,0:T(8,128)(2,1)S(1)} %shard_map.48), channel_id=1, source_target_pairs={{0,2},{1,66},{2,0},{3,64},{4,6},{5,70},{6,4},{7,68},{8,10},{9,74},... | collective-permute-start | bytes 1622024 | tf_op jit(solution)/shard_map/ppermute | solution.py:287
  78.1 2.2 %shard_map.49 = s16[264,1024]{1,0:T(8,128)(2,1)S(1)} custom-call(bf16[4,48,16,128]{3,2,1,0:T(8,128)(2,1)S(1)} %bitcast.7, bf16[768,1024]{1,0:T(8,128)(2,1)S(1)} %copy-done, bf16[768,1024]{1,0:T(8,128)(2,1)} %collective-permute-done.refs_2_, s32[2]{0:T(128)S(1)} %pad_add_fusion.2.refs_3_), custom_call_target="tpu_custom_call" | custom-call | tf_op jit(solution)/shard_map/pallas_call | solution.py:281
  80.3 3.3 %collective-permute-start.2 = (s16[264,1024]{1,0:T(8,128)(2,1)S(1)}, s16[264,1024]{1,0:T(8,128)(2,1)S(1)}, u32[]{:S(2)}, u32[]{:S(2)}) collective-permute-start(s16[264,1024]{1,0:T(8,128)(2,1)S(1)} %shard_map.49), channel_id=1, source_target_pairs={{0,66},{1,2},{2,64},{3,0},{4,70},{5,6},{6,68},{7,4},{8,74},{9,10},... | collective-permute-start | bytes 1622024 | tf_op jit(solution)/shard_map/ppermute | solution.py:287
  83.6 2.2 %shard_map.50 = s16[264,1024]{1,0:T(8,128)(2,1)S(1)} custom-call(bf16[4,48,16,128]{3,2,1,0:T(8,128)(2,1)S(1)} %bitcast.8, bf16[768,1024]{1,0:T(8,128)(2,1)S(1)} %copy-done, bf16[768,1024]{1,0:T(8,128)(2,1)} %collective-permute-done.refs_2_, s32[2]{0:T(128)S(1)} %pad_add_fusion.refs_3_), custom_call_target="tpu_custom_call" | custom-call | tf_op jit(solution)/shard_map/pallas_call | solution.py:281
  85.8 1.9 %collective-permute-start.3 = (s16[264,1024]{1,0:T(8,128)(2,1)S(1)}, s16[264,1024]{1,0:T(8,128)(2,1)S(1)}, u32[]{:S(2)}, u32[]{:S(2)}) collective-permute-start(s16[264,1024]{1,0:T(8,128)(2,1)S(1)} %shard_map.50), channel_id=1, source_target_pairs={{0,0},{1,64},{2,2},{3,66},{4,4},{5,68},{6,6},{7,70},{8,8},{9,72},{... | collective-permute-start | bytes 1622024 | tf_op jit(solution)/shard_map/ppermute | solution.py:287
  87.7 2.2 %shard_map.51 = s16[264,1024]{1,0:T(8,128)(2,1)S(1)} custom-call(bf16[4,48,16,128]{3,2,1,0:T(8,128)(2,1)S(1)} %bitcast.9, bf16[768,1024]{1,0:T(8,128)(2,1)S(1)} %copy-done, bf16[768,1024]{1,0:T(8,128)(2,1)} %collective-permute-done.refs_2_, s32[2]{0:T(128)S(1)} %pad_add_fusion.3.refs_3_), custom_call_target="tpu_custom_call" | custom-call | tf_op jit(solution)/shard_map/pallas_call | solution.py:281
  89.9 3.1 %collective-permute-start.4 = (s16[264,1024]{1,0:T(8,128)(2,1)S(1)}, s16[264,1024]{1,0:T(8,128)(2,1)S(1)}, u32[]{:S(2)}, u32[]{:S(2)}) collective-permute-start(s16[264,1024]{1,0:T(8,128)(2,1)S(1)} %shard_map.51), channel_id=1, source_target_pairs={{0,64},{1,0},{2,66},{3,2},{4,68},{5,4},{6,70},{7,6},{8,72},{9,8},{... | collective-permute-start | bytes 1622024 | tf_op jit(solution)/shard_map/ppermute | solution.py:287
  93.0 4.2 %collective-permute-done.1.refs_0_ = s16[264,1024]{1,0:T(8,128)(2,1)S(1)} collective-permute-done((s16[264,1024]{1,0:T(8,128)(2,1)S(1)}, s16[264,1024]{1,0:T(8,128)(2,1)S(1)}, u32[]{:S(2)}, u32[]{:S(2)}) %collective-permute-start.1) | collective-permute-done | bytes 540704 | tf_op jit(solution)/shard_map/ppermute | solution.py:287
  97.2 3.9 %collective-permute-done.2.refs_1_ = s16[264,1024]{1,0:T(8,128)(2,1)S(1)} collective-permute-done((s16[264,1024]{1,0:T(8,128)(2,1)S(1)}, s16[264,1024]{1,0:T(8,128)(2,1)S(1)}, u32[]{:S(2)}, u32[]{:S(2)}) %collective-permute-start.2) | collective-permute-done | bytes 540704 | tf_op jit(solution)/shard_map/ppermute | solution.py:287
  101.1 0.8 shard_map.52
  101.9 17.3 %all_to_all.20.got = s16[4,520,128]{2,1,0:T(8,128)(2,1)S(1)} all-to-all(s16[4,520,128]{2,1,0:T(8,128)(2,1)S(1)} %shard_map.52), channel_id=1, replica_groups={{0,4,8,12},{1,5,9,13},{2,6,10,14},{3,7,11,15},{16,20,24,28},{17,21,25,2..., dimensions={0} | all-to-all | bytes 1064960 | tf_op jit(solution)/shard_map/all_to_all | solution.py:231
  119.2 0.2 shard_map.53
  119.4 18.5 %all_to_all.21.got = s16[4,136,128]{2,1,0:T(8,128)(2,1)S(1)} all-to-all(s16[4,136,128]{2,1,0:T(8,128)(2,1)S(1)} %shard_map.53), channel_id=1, replica_groups={{0,16,32,48},{1,17,33,49},{2,18,34,50},{3,19,35,51},{4,20,36,52},{5,21,..., dimensions={0} | all-to-all | bytes 278528 | tf_op jit(solution)/shard_map/all_to_all | solution.py:231
  137.9 0.7 shard_map.54
  (7 shorter events, 0.2 us)
Async XLA Ops:
  2.2 52.8 %all-to-all-start = ((bf16[64,17,2,128]{3,2,1,0:T(2,128)(2,1)}), bf16[64,17,2,128]{3,2,1,0:T(2,128)(2,1)}, u32[]{:S(2)}, u32[]{:S(2)}) async-start(bf16[64,17,2,128]{3,2,1,0:T(2,128)(2,1)} %shard_map.46), calls=%async_computation | async-start | bytes 1114112 | tf_op jit(solution)/shard_map/all_to_all | solution.py:231
  21.0 41.7 %collective-permute-start = (bf16[768,1024]{1,0:T(8,128)(2,1)}, bf16[768,1024]{1,0:T(8,128)(2,1)}, u32[]{:S(2)}, u32[]{:S(2)}) collective-permute-start(bf16[768,1024]{1,0:T(8,128)(2,1)} %refs_1_.9), channel_id=1, source_target_pairs={{0,64},{64,0},{128,192},{192,128},{256,320},{320,256},{384,448},{4... | collective-permute-start | bytes 4718600 | tf_op jit(solution)/shard_map/ppermute | solution.py:262
  57.8 16.2 %copy-start = (bf16[768,1024]{1,0:T(8,128)(2,1)S(1)}, bf16[768,1024]{1,0:T(8,128)(2,1)}, u32[]{:S(2)}) copy-start(bf16[768,1024]{1,0:T(8,128)(2,1)} %refs_1_.9) | copy-start | bytes 4718596
  57.8 16.2 %all-to-all-start.1 = ((bf16[4,48,8,2,128]{4,3,2,1,0:T(2,128)(2,1)}), bf16[4,48,8,2,128]{4,3,2,1,0:T(2,128)(2,1)S(1)}, u32[]{:S(2)}, u32[]{:S(2)}) async-start(bf16[4,48,8,2,128]{4,3,2,1,0:T(2,128)(2,1)} %shard_map.47), calls=%async_computation.1 | async-start | bytes 1572864 | tf_op jit(solution)/shard_map/all_to_all | solution.py:231
  76.2 21.0 %collective-permute-start.1 = (s16[264,1024]{1,0:T(8,128)(2,1)S(1)}, s16[264,1024]{1,0:T(8,128)(2,1)S(1)}, u32[]{:S(2)}, u32[]{:S(2)}) collective-permute-start(s16[264,1024]{1,0:T(8,128)(2,1)S(1)} %shard_map.48), channel_id=1, source_target_pairs={{0,2},{1,66},{2,0},{3,64},{4,6},{5,70},{6,4},{7,68},{8,10},{9,74},... | collective-permute-start | bytes 1622024 | tf_op jit(solution)/shard_map/ppermute | solution.py:287
  80.3 20.8 %collective-permute-start.2 = (s16[264,1024]{1,0:T(8,128)(2,1)S(1)}, s16[264,1024]{1,0:T(8,128)(2,1)S(1)}, u32[]{:S(2)}, u32[]{:S(2)}) collective-permute-start(s16[264,1024]{1,0:T(8,128)(2,1)S(1)} %shard_map.49), channel_id=1, source_target_pairs={{0,66},{1,2},{2,64},{3,0},{4,70},{5,6},{6,68},{7,4},{8,74},{9,10},... | collective-permute-start | bytes 1622024 | tf_op jit(solution)/shard_map/ppermute | solution.py:287
  85.8 15.3 %collective-permute-start.3 = (s16[264,1024]{1,0:T(8,128)(2,1)S(1)}, s16[264,1024]{1,0:T(8,128)(2,1)S(1)}, u32[]{:S(2)}, u32[]{:S(2)}) collective-permute-start(s16[264,1024]{1,0:T(8,128)(2,1)S(1)} %shard_map.50), channel_id=1, source_target_pairs={{0,0},{1,64},{2,2},{3,66},{4,4},{5,68},{6,6},{7,70},{8,8},{9,72},{... | collective-permute-start | bytes 1622024 | tf_op jit(solution)/shard_map/ppermute | solution.py:287
  89.9 11.2 %collective-permute-start.4 = (s16[264,1024]{1,0:T(8,128)(2,1)S(1)}, s16[264,1024]{1,0:T(8,128)(2,1)S(1)}, u32[]{:S(2)}, u32[]{:S(2)}) collective-permute-start(s16[264,1024]{1,0:T(8,128)(2,1)S(1)} %shard_map.51), channel_id=1, source_target_pairs={{0,64},{1,0},{2,66},{3,2},{4,68},{5,4},{6,70},{7,6},{8,72},{9,8},{... | collective-permute-start | bytes 1622024 | tf_op jit(solution)/shard_map/ppermute | solution.py:287

commit v8 on v7

--- a/solution.py
+++ b/solution.py
@@ -53,22 +53,26 @@
 
     lax.fori_loop(0, owners, clear, 0)
     keys[...] = jnp.full(keys.shape, -1.0, jnp.float32)
-    for copy in copies:
+    for copy in copies[:2]:
         copy.wait()
+    slots = []
     for r in range(rows.shape[0]):
         tile = tiles[r]
         owner = tile // tile_dev
         rank = count[owner]
         count[owner] = rank + 1
         key = blocks[r] * tile_dev + (tile - owner * tile_dev)
-        out[owner, pl.ds(rank * units, units)] = rows[r]
+        slots.append((owner, rank))
         line = owner * LINES + rank
         keys[pl.ds(line, 1), :] = jnp.full((1, lanes), key, jnp.int32).astype(jnp.float32)
     for o in range(owners):
         out[o, CAP * units] = keys[o * LINES : (o + 1) * LINES, :].astype(out.dtype)
-
-
-def place(tile_dev, got, out, held, row, key, sems):
+    copies[2].wait()
+    for r, (owner, rank) in enumerate(slots):
+        out[owner, pl.ds(rank * units, units)] = rows[r]
+
+
+def place(tile_dev, got, out, held, row, key, slot_of, sems):
     sources, units, lines, width = got.shape
     units = (units - 1) // CAP
     line = lax.broadcasted_iota(jnp.int32, (lines, width), 0)
@@ -82,19 +86,23 @@
     copy = pltpu.make_async_copy(row, key, sems.at[targets])
     copy.start()
     copy.wait()
-    for s in range(sources):
-        for r in range(CAP):
-            k = key[0, s * CAP + r]
-            held[jnp.where(k < 0, keys, k)] = got[s, r * units : (r + 1) * units]
-    copies = [pltpu.make_async_copy(held.at[pl.ds(0, keys)], out.at[y], sems.at[y]) for y in range(targets)]
+    for k in range(keys):
+        slot_of[k] = 0
+    for n in range(sources * CAP):
+        k = key[0, n]
+        slot_of[jnp.where(k < 0, keys, k)] = n
+    for k in range(keys):
+        n = slot_of[k]
+        held[k] = got[n // CAP, pl.ds(n % CAP * units, units)]
+    copies = [pltpu.make_async_copy(held, out.at[y], sems.at[y]) for y in range(targets)]
     for copy in copies:
         copy.start()
     for copy in copies:
         copy.wait()
 
 
-def multiply(tile_dev, a, mine, theirs, which, out, left):
-    rows, width, cols = NB * a.shape[2], a.shape[3], out.shape[1]
+def multiply(tile_dev, a, mine, theirs, which, first, second, left):
+    rows, width, cols = NB * a.shape[2], a.shape[3], first.shape[1]
     occ = a.shape[2]
     half = NX // CORES
     parts = a.shape[0] // half
@@ -104,7 +112,7 @@
                 at = h * rows + b * occ
                 left[at : at + occ, t * width : (t + 1) * width] = a[which[0] + half * h, b * tile_dev + t]
 
-    def block(v):
+    def block(v, out):
         sums = [
             jnp.dot(left[h * rows : (h + 1) * rows, :], v[...], preferred_element_type=jnp.float32)
             .reshape(rows // 8, 8, cols)
@@ -121,11 +129,13 @@
 
     @pl.when(which[1] == 0)
     def _():
-        block(mine)
+        block(mine, first)
+        block(theirs, second)
 
     @pl.when(which[1] != 0)
     def _():
-        block(theirs)
+        block(theirs, first)
+        block(mine, second)
 
 
 def recoded(tiles, out, z):
@@ -265,9 +275,10 @@
         struct((ny, keys, lines, LINES, width), dtype),
         [VMEM],
         [
-            pltpu.VMEM((keys + 1, lines, LINES, width), dtype),
+            pltpu.VMEM((keys, lines, LINES, width), dtype),
             pltpu.VMEM((1, width), jnp.int32),
             pltpu.SMEM((1, width), jnp.int32),
+            pltpu.SMEM((keys + 1,), jnp.int32),
             pltpu.SemaphoreType.DMA((ny + 1,)),
         ],
         anywhere,
@@ -275,16 +286,16 @@
     )(exchange(packed))
     mine = exchange(copies, y_groups, "grp").reshape(ny, keys, occ, width)
     gots = []
-    for r in (2, 3, 0, 1):
-        a, to = target(r, x)
+    for half in reversed(range(NX // CORES)):
+        a, to = target(half * CORES, x)
         which = jnp.stack([a, to ^ core]).astype(jnp.int32)
         sent = call(
             lambda *refs: multiply(tile_dev, *refs),
-            struct((parts * rows + 8, cols), jnp.int16),
+            [struct((parts * rows + 8, cols), jnp.int16)] * CORES,
             [VMEM, VMEM, VMEM, SMEM],
             [pltpu.VMEM((parts * rows, tile_dev * width), dtype)],
         )(mine, integrals, theirs, which)
-        gots.append(lax.ppermute(sent, ("grp", "own"), round_pairs(r)))
+        gots += [lax.ppermute(sent[r], ("grp", "own"), round_pairs(half * CORES + r)) for r in range(CORES)]
     sent = call(
         lambda *refs: add_x(rows, *refs),
         struct((LOWS, (highs * units * tiles + 1) * UNIT, 128), jnp.int16),

time: 141 us -> 148 us (1.050)
  waiting for transfers between devices: 51.5 us -> 61.2 us
  Pallas kernels: 15.3 us -> 12.3 us
  starting transfers between devices: 35.5 us -> 37.7 us
    ppermute x4, waiting for transfers between devices: 8.09 us -> 17.5 us  [local(): lax.ppermute(sent[r], ('grp', 'own'), round_pairs(half * CORES + r))]
    pallas_call x4 -> x2, Pallas kernels: 8.7 us -> 5.44 us  [local(): call(lambda *refs: multiply(tile_dev, *refs), [struct((parts * rows + 8,...]
    ppermute x4, starting transfers between devices: 10.2 us -> 12.4 us  [local(): lax.ppermute(sent[r], ('grp', 'own'), round_pairs(half * CORES + r))]
  transfers between devices with their start and end apart: 7 -> 7, of which waited for: 4 -> 5; matrix products, arithmetic and copies ran while one was open for 0% -> 0% of each run, Pallas kernels for 7% -> 4%
where the time goes in v8:
time: 148 us; the launch traced here: 147 us
  waiting for transfers between devices  61.2 us (41%)
  starting transfers between devices  37.7 us (25%)
  blocking collectives  35.2 us (24%)
  Pallas kernels  12.3 us (8%)
    all_to_all x2, waiting for transfers between devices, exchange(): lax.all_to_all(array, axis, 0, 0, axis_index_groups=groups, tiled=True)  43.6 us
    all_to_all x2, blocking collectives, exchange(): lax.all_to_all(array, axis, 0, 0, axis_index_groups=groups, tiled=True)  35.2 us
    all_to_all x2, starting transfers between devices, exchange(): lax.all_to_all(array, axis, 0, 0, axis_index_groups=groups, tiled=True)  23.4 us
    ppermute x4, waiting for transfers between devices, local(): lax.ppermute(sent[r], ('grp', 'own'), round_pairs(half * CORES + r))  17.5 us
    ppermute x4, starting transfers between devices, local(): lax.ppermute(sent[r], ('grp', 'own'), round_pairs(half * CORES + r))  12.4 us
    pallas_call x2, Pallas kernels, local(): call(lambda *refs: multiply(tile_dev, *refs), [struct((parts * rows + 8,...  5.44 us
    pallas_call x1, Pallas kernels, local(): call(lambda *refs: place(tile_dev, *refs), struct((ny, keys, lines, LINES...  3.09 us
  transfers between devices with their start and end apart: 7, of which 5 were waited for; matrix products, arithmetic and copies ran while one was open for 0% of the time, Pallas kernels for 4%

profile of v8, /device:TPU:6, one launch (start us, length us, event | category | flops | bytes accessed | tf_op | source)
XLA Modules:
  0.0 146.5 jit_solution(3307034141183383857)
XLA Ops:
  0.0 2.1 %shard_map.46 = bf16[64,17,2,128]{3,2,1,0:T(2,128)(2,1)} custom-call(bf16[48,8,2,128]{3,2,1,0:T(2,128)(2,1)} %bitcast.7, s32[48]{0:T(128)} %refs_1_.3, s32[48]{0:T(128)} %refs_2_.1), custom_call_target="tpu_custom_call" | custom-call | tf_op jit(solution)/shard_map/pallas_call | solution.py:258
  2.1 18.8 %all-to-all-start = ((bf16[64,17,2,128]{3,2,1,0:T(2,128)(2,1)}), bf16[64,17,2,128]{3,2,1,0:T(2,128)(2,1)}, u32[]{:S(2)}, u32[]{:S(2)}) async-start(bf16[64,17,2,128]{3,2,1,0:T(2,128)(2,1)} %shard_map.46), calls=%async_computation | async-start | bytes 1114112 | tf_op jit(solution)/shard_map/all_to_all | solution.py:241
  20.9 1.9 %collective-permute-start = (bf16[768,1024]{1,0:T(8,128)(2,1)}, bf16[768,1024]{1,0:T(8,128)(2,1)}, u32[]{:S(2)}, u32[]{:S(2)}) collective-permute-start(bf16[768,1024]{1,0:T(8,128)(2,1)} %refs_1_.5), channel_id=1, source_target_pairs={{0,64},{64,0},{128,192},{192,128},{256,320},{320,256},{384,448},{4... | collective-permute-start | bytes 4718600 | tf_op jit(solution)/shard_map/ppermute | solution.py:272
  22.8 32.1 %all-to-all-done.refs_0_ = bf16[64,17,2,128]{3,2,1,0:T(2,128)(2,1)} async-done(((bf16[64,17,2,128]{3,2,1,0:T(2,128)(2,1)}), bf16[64,17,2,128]{3,2,1,0:T(2,128)(2,1)}, u32[]{:S(2)}, u32[]{:S(2)}) %all-to-all-start) | async-done | bytes 557088 | tf_op jit(solution)/shard_map/all_to_all | solution.py:241
  54.9 3.1 %shard_map.47 = bf16[4,48,8,2,128]{4,3,2,1,0:T(2,128)(2,1)} custom-call(bf16[64,17,2,128]{3,2,1,0:T(2,128)(2,1)} %all-to-all-done.refs_0_), custom_call_target="tpu_custom_call" | custom-call | tf_op jit(solution)/shard_map/pallas_call | solution.py:273
  58.0 0.0 copy-start
  58.0 4.6 %all-to-all-start.1 = ((bf16[4,48,8,2,128]{4,3,2,1,0:T(2,128)(2,1)}), bf16[4,48,8,2,128]{4,3,2,1,0:T(2,128)(2,1)S(1)}, u32[]{:S(2)}, u32[]{:S(2)}) async-start(bf16[4,48,8,2,128]{4,3,2,1,0:T(2,128)(2,1)} %shard_map.47), calls=%async_computation.1 | async-start | bytes 1572864 | tf_op jit(solution)/shard_map/all_to_all | solution.py:241
  62.7 0.1 pad_add_fusion
  62.7 0.0 collective-permute-done.refs_2_
  62.7 11.5 %all-to-all-done.1 = bf16[4,48,8,2,128]{4,3,2,1,0:T(2,128)(2,1)S(1)} async-done(((bf16[4,48,8,2,128]{4,3,2,1,0:T(2,128)(2,1)}), bf16[4,48,8,2,128]{4,3,2,1,0:T(2,128)(2,1)S(1)}, u32[]{:S(2)}, u32[]{:S(2)}) %all-to-all-start.1) | async-done | bytes 786464 | tf_op jit(solution)/shard_map/all_to_all | solution.py:241
  74.2 2.7 %shard_map.49 = (s16[264,1024]{1,0:T(8,128)(2,1)S(1)}, s16[264,1024]{1,0:T(8,128)(2,1)S(1)}) custom-call(bf16[4,48,16,128]{3,2,1,0:T(8,128)(2,1)S(1)} %bitcast.5, bf16[768,1024]{1,0:T(8,128)(2,1)S(1)} %copy-done, bf16[768,1024]{1,0:T(8,128)(2,1)} %collective-permute-done.refs_2_, s32[2]{0:T(128)S(1)} %get-tuple-element.14.refs_3_), custom_call_target="tpu_custom_call" | custom-call | tf_op jit(solution)/shard_map/pallas_call | solution.py:292
  77.0 1.9 %collective-permute-start.3 = (s16[264,1024]{1,0:T(8,128)(2,1)S(1)}, s16[264,1024]{1,0:T(8,128)(2,1)S(1)}, u32[]{:S(2)}, u32[]{:S(2)}) collective-permute-start(s16[264,1024]{1,0:T(8,128)(2,1)S(1)} %get-tuple-element.11), channel_id=1, source_target_pairs={{0,0},{1,64},{2,2},{3,66},{4,4},{5,68},{6,6},{7,70},{8,8},{9,72},{... | collective-permute-start | bytes 1622024 | tf_op jit(solution)/shard_map/ppermute | solution.py:298
  78.9 1.9 %collective-permute-start.4 = (s16[264,1024]{1,0:T(8,128)(2,1)S(1)}, s16[264,1024]{1,0:T(8,128)(2,1)S(1)}, u32[]{:S(2)}, u32[]{:S(2)}) collective-permute-start(s16[264,1024]{1,0:T(8,128)(2,1)S(1)} %get-tuple-element.12), channel_id=1, source_target_pairs={{0,64},{1,0},{2,66},{3,2},{4,68},{5,4},{6,70},{7,6},{8,72},{9,8},{... | collective-permute-start | bytes 1622024 | tf_op jit(solution)/shard_map/ppermute | solution.py:298
  80.8 2.7 %shard_map.48 = (s16[264,1024]{1,0:T(8,128)(2,1)S(1)}, s16[264,1024]{1,0:T(8,128)(2,1)S(1)}) custom-call(bf16[4,48,16,128]{3,2,1,0:T(8,128)(2,1)S(1)} %bitcast.6, bf16[768,1024]{1,0:T(8,128)(2,1)S(1)} %copy-done, bf16[768,1024]{1,0:T(8,128)(2,1)} %collective-permute-done.refs_2_, s32[2]{0:T(128)S(1)} %get-tuple-element.13.refs_3_), custom_call_target="tpu_custom_call" | custom-call | tf_op jit(solution)/shard_map/pallas_call | solution.py:292
  83.5 1.9 %collective-permute-start.1 = (s16[264,1024]{1,0:T(8,128)(2,1)S(1)}, s16[264,1024]{1,0:T(8,128)(2,1)S(1)}, u32[]{:S(2)}, u32[]{:S(2)}) collective-permute-start(s16[264,1024]{1,0:T(8,128)(2,1)S(1)} %get-tuple-element.9), channel_id=1, source_target_pairs={{0,2},{1,66},{2,0},{3,64},{4,6},{5,70},{6,4},{7,68},{8,10},{9,74},... | collective-permute-start | bytes 1622024 | tf_op jit(solution)/shard_map/ppermute | solution.py:298
  85.5 6.7 %collective-permute-start.2 = (s16[264,1024]{1,0:T(8,128)(2,1)S(1)}, s16[264,1024]{1,0:T(8,128)(2,1)S(1)}, u32[]{:S(2)}, u32[]{:S(2)}) collective-permute-start(s16[264,1024]{1,0:T(8,128)(2,1)S(1)} %get-tuple-element.10), channel_id=1, source_target_pairs={{0,66},{1,2},{2,64},{3,0},{4,70},{5,6},{6,68},{7,4},{8,74},{9,10},... | collective-permute-start | bytes 1622024 | tf_op jit(solution)/shard_map/ppermute | solution.py:298
  92.2 4.5 %collective-permute-done.4.refs_3_ = s16[264,1024]{1,0:T(8,128)(2,1)S(1)} collective-permute-done((s16[264,1024]{1,0:T(8,128)(2,1)S(1)}, s16[264,1024]{1,0:T(8,128)(2,1)S(1)}, u32[]{:S(2)}, u32[]{:S(2)}) %collective-permute-start.4) | collective-permute-done | bytes 540704 | tf_op jit(solution)/shard_map/ppermute | solution.py:298
  96.7 10.4 %collective-permute-done.1.refs_0_ = s16[264,1024]{1,0:T(8,128)(2,1)S(1)} collective-permute-done((s16[264,1024]{1,0:T(8,128)(2,1)S(1)}, s16[264,1024]{1,0:T(8,128)(2,1)S(1)}, u32[]{:S(2)}, u32[]{:S(2)}) %collective-permute-start.1) | collective-permute-done | bytes 540704 | tf_op jit(solution)/shard_map/ppermute | solution.py:298
  107.0 2.7 %collective-permute-done.2.refs_1_ = s16[264,1024]{1,0:T(8,128)(2,1)S(1)} collective-permute-done((s16[264,1024]{1,0:T(8,128)(2,1)S(1)}, s16[264,1024]{1,0:T(8,128)(2,1)S(1)}, u32[]{:S(2)}, u32[]{:S(2)}) %collective-permute-start.2) | collective-permute-done | bytes 540704 | tf_op jit(solution)/shard_map/ppermute | solution.py:298
  109.7 0.8 shard_map.50
  110.5 16.9 %all_to_all.20.got = s16[4,520,128]{2,1,0:T(8,128)(2,1)S(1)} all-to-all(s16[4,520,128]{2,1,0:T(8,128)(2,1)S(1)} %shard_map.50), channel_id=1, replica_groups={{0,4,8,12},{1,5,9,13},{2,6,10,14},{3,7,11,15},{16,20,24,28},{17,21,25,2..., dimensions={0} | all-to-all | bytes 1064960 | tf_op jit(solution)/shard_map/all_to_all | solution.py:241
  127.4 0.2 shard_map.51
  127.6 18.2 %all_to_all.21.got = s16[4,136,128]{2,1,0:T(8,128)(2,1)S(1)} all-to-all(s16[4,136,128]{2,1,0:T(8,128)(2,1)S(1)} %shard_map.51), channel_id=1, replica_groups={{0,16,32,48},{1,17,33,49},{2,18,34,50},{3,19,35,51},{4,20,36,52},{5,21,..., dimensions={0} | all-to-all | bytes 278528 | tf_op jit(solution)/shard_map/all_to_all | solution.py:241
  145.9 0.7 shard_map.52
  (2 shorter events, 0.0 us)
Async XLA Ops:
  2.1 52.8 %all-to-all-start = ((bf16[64,17,2,128]{3,2,1,0:T(2,128)(2,1)}), bf16[64,17,2,128]{3,2,1,0:T(2,128)(2,1)}, u32[]{:S(2)}, u32[]{:S(2)}) async-start(bf16[64,17,2,128]{3,2,1,0:T(2,128)(2,1)} %shard_map.46), calls=%async_computation | async-start | bytes 1114112 | tf_op jit(solution)/shard_map/all_to_all | solution.py:241
  20.9 41.9 %collective-permute-start = (bf16[768,1024]{1,0:T(8,128)(2,1)}, bf16[768,1024]{1,0:T(8,128)(2,1)}, u32[]{:S(2)}, u32[]{:S(2)}) collective-permute-start(bf16[768,1024]{1,0:T(8,128)(2,1)} %refs_1_.5), channel_id=1, source_target_pairs={{0,64},{64,0},{128,192},{192,128},{256,320},{320,256},{384,448},{4... | collective-permute-start | bytes 4718600 | tf_op jit(solution)/shard_map/ppermute | solution.py:272
  58.0 16.2 %copy-start = (bf16[768,1024]{1,0:T(8,128)(2,1)S(1)}, bf16[768,1024]{1,0:T(8,128)(2,1)}, u32[]{:S(2)}) copy-start(bf16[768,1024]{1,0:T(8,128)(2,1)} %refs_1_.5) | copy-start | bytes 4718596
  58.0 16.2 %all-to-all-start.1 = ((bf16[4,48,8,2,128]{4,3,2,1,0:T(2,128)(2,1)}), bf16[4,48,8,2,128]{4,3,2,1,0:T(2,128)(2,1)S(1)}, u32[]{:S(2)}, u32[]{:S(2)}) async-start(bf16[4,48,8,2,128]{4,3,2,1,0:T(2,128)(2,1)} %shard_map.47), calls=%async_computation.1 | async-start | bytes 1572864 | tf_op jit(solution)/shard_map/all_to_all | solution.py:241
  77.0 15.2 %collective-permute-start.3 = (s16[264,1024]{1,0:T(8,128)(2,1)S(1)}, s16[264,1024]{1,0:T(8,128)(2,1)S(1)}, u32[]{:S(2)}, u32[]{:S(2)}) collective-permute-start(s16[264,1024]{1,0:T(8,128)(2,1)S(1)} %get-tuple-element.11), channel_id=1, source_target_pairs={{0,0},{1,64},{2,2},{3,66},{4,4},{5,68},{6,6},{7,70},{8,8},{9,72},{... | collective-permute-start | bytes 1622024 | tf_op jit(solution)/shard_map/ppermute | solution.py:298
  78.9 17.8 %collective-permute-start.4 = (s16[264,1024]{1,0:T(8,128)(2,1)S(1)}, s16[264,1024]{1,0:T(8,128)(2,1)S(1)}, u32[]{:S(2)}, u32[]{:S(2)}) collective-permute-start(s16[264,1024]{1,0:T(8,128)(2,1)S(1)} %get-tuple-element.12), channel_id=1, source_target_pairs={{0,64},{1,0},{2,66},{3,2},{4,68},{5,4},{6,70},{7,6},{8,72},{9,8},{... | collective-permute-start | bytes 1622024 | tf_op jit(solution)/shard_map/ppermute | solution.py:298
  83.5 23.5 %collective-permute-start.1 = (s16[264,1024]{1,0:T(8,128)(2,1)S(1)}, s16[264,1024]{1,0:T(8,128)(2,1)S(1)}, u32[]{:S(2)}, u32[]{:S(2)}) collective-permute-start(s16[264,1024]{1,0:T(8,128)(2,1)S(1)} %get-tuple-element.9), channel_id=1, source_target_pairs={{0,2},{1,66},{2,0},{3,64},{4,6},{5,70},{6,4},{7,68},{8,10},{9,74},... | collective-permute-start | bytes 1622024 | tf_op jit(solution)/shard_map/ppermute | solution.py:298
  85.5 24.2 %collective-permute-start.2 = (s16[264,1024]{1,0:T(8,128)(2,1)S(1)}, s16[264,1024]{1,0:T(8,128)(2,1)S(1)}, u32[]{:S(2)}, u32[]{:S(2)}) collective-permute-start(s16[264,1024]{1,0:T(8,128)(2,1)S(1)} %get-tuple-element.10), channel_id=1, source_target_pairs={{0,66},{1,2},{2,64},{3,0},{4,70},{5,6},{6,68},{7,4},{8,74},{9,10},... | collective-permute-start | bytes 1622024 | tf_op jit(solution)/shard_map/ppermute | solution.py:298

commit v9 on v7

--- a/solution.py
+++ b/solution.py
@@ -78,31 +78,33 @@
     for s in range(sources):
         marks = jnp.where(slot == CAP * s, got[s, CAP * units].astype(jnp.float32), marks)
     row[...] = jnp.sum(marks, axis=0, keepdims=True).astype(jnp.int32)
-    targets, keys = out.shape[0], out.shape[1]
-    copy = pltpu.make_async_copy(row, key, sems.at[targets])
+    keys = out.shape[0]
+    copy = pltpu.make_async_copy(row, key, sems.at[0])
     copy.start()
     copy.wait()
     for s in range(sources):
         for r in range(CAP):
             k = key[0, s * CAP + r]
             held[jnp.where(k < 0, keys, k)] = got[s, r * units : (r + 1) * units]
-    copies = [pltpu.make_async_copy(held.at[pl.ds(0, keys)], out.at[y], sems.at[y]) for y in range(targets)]
-    for copy in copies:
-        copy.start()
-    for copy in copies:
-        copy.wait()
-
-
-def multiply(tile_dev, a, mine, theirs, which, out, left):
-    rows, width, cols = NB * a.shape[2], a.shape[3], out.shape[1]
-    occ = a.shape[2]
-    half = NX // CORES
-    parts = a.shape[0] // half
+    copy = pltpu.make_async_copy(held.at[pl.ds(0, keys)], out, sems.at[1])
+    copy.start()
+    copy.wait()
+
+
+def multiply(tile_dev, *refs):
+    *slices, mine, theirs, which, out, left = refs
+    _, occ, width = slices[0].shape
+    rows, cols = NB * occ, out.shape[1]
+    parts = left.shape[0] // rows
     for h in range(parts):
-        for b in range(NB):
-            for t in range(tile_dev):
-                at = h * rows + b * occ
-                left[at : at + occ, t * width : (t + 1) * width] = a[which[0] + half * h, b * tile_dev + t]
+        for back, a in enumerate(slices):
+
+            @pl.when(which[2 + h] == back)
+            def _(h=h, a=a):
+                for b in range(NB):
+                    for t in range(tile_dev):
+                        at = h * rows + b * occ
+                        left[at : at + occ, t * width : (t + 1) * width] = a[b * tile_dev + t]
 
     def block(v):
         sums = [
@@ -212,7 +214,6 @@
             line = sorted(((high * LOWS + low + shift) % nz for low in range(LOWS)), key=lambda z: z % LOWS)
             low_groups += [[g * own + z * NX + x for z in line] for x in range(NX)]
     high_groups = [[(high * LOWS + low) * NX + x for high in range(highs)] for low in range(LOWS) for x in range(NX)]
-    y_groups = [[y * CORES + c for y in range(ny)] for c in range(CORES)]
     core_pairs = [(y * CORES + c, y * CORES + 1 - c) for y in range(ny) for c in range(CORES)]
 
     def target(r, x):
@@ -226,6 +227,9 @@
                 a, to = target(r, x)
                 pairs.append((g * own + o, (y * CORES + to) * own + z * NX + a * CORES + c))
         return pairs
+
+    def y_pairs(k):
+        return [(g, (g + k * CORES) % grp) for g in range(grp)]
 
     def exchange(array, groups=None, axis="own"):
         return lax.all_to_all(array, axis, 0, 0, axis_index_groups=groups, tiled=True)
@@ -240,6 +244,7 @@
     dtype = amplitudes.dtype
     struct = jax.ShapeDtypeStruct
     core = lax.axis_index("grp") % CORES
+    y = lax.axis_index("grp") // CORES
     x = lax.axis_index("own") % NX
 
     anywhere = pl.BlockSpec(memory_space=pl.ANY)
@@ -260,30 +265,33 @@
         grant=WHOLE,
     )(amplitudes.reshape(-1, lines, LINES, width), tile_block, tile_index)
     theirs = lax.ppermute(integrals, "grp", core_pairs)
-    copies = call(
+    placed = call(
         lambda *refs: place(tile_dev, *refs),
-        struct((ny, keys, lines, LINES, width), dtype),
+        struct((keys, lines, LINES, width), dtype),
         [VMEM],
         [
             pltpu.VMEM((keys + 1, lines, LINES, width), dtype),
             pltpu.VMEM((1, width), jnp.int32),
             pltpu.SMEM((1, width), jnp.int32),
-            pltpu.SemaphoreType.DMA((ny + 1,)),
+            pltpu.SemaphoreType.DMA((2,)),
         ],
         anywhere,
         WHOLE,
     )(exchange(packed))
-    mine = exchange(copies, y_groups, "grp").reshape(ny, keys, occ, width)
+    far_first = sorted(range(1, ny), key=lambda k: k % CORES)
+    slices = {k: lax.ppermute(placed, "grp", y_pairs(k)) for k in far_first}
+    slices = [s.reshape(keys, occ, width) for s in (placed, *(slices[k] for k in range(1, ny)))]
     gots = []
     for r in (2, 3, 0, 1):
         a, to = target(r, x)
-        which = jnp.stack([a, to ^ core]).astype(jnp.int32)
+        back = [(y - a - NX // CORES * h) % ny for h in range(parts)]
+        which = jnp.stack([a, to ^ core, *back]).astype(jnp.int32)
         sent = call(
             lambda *refs: multiply(tile_dev, *refs),
             struct((parts * rows + 8, cols), jnp.int16),
-            [VMEM, VMEM, VMEM, SMEM],
+            [VMEM] * (ny + 2) + [SMEM],
             [pltpu.VMEM((parts * rows, tile_dev * width), dtype)],
-        )(mine, integrals, theirs, which)
+        )(*slices, integrals, theirs, which)
         gots.append(lax.ppermute(sent, ("grp", "own"), round_pairs(r)))
     sent = call(
         lambda *refs: add_x(rows, *refs),

time: 141 us -> 146 us (1.035)
  starting transfers between devices: 35.5 us -> 41.3 us
  waiting for transfers between devices: 51.5 us -> 46.8 us
  local copies, waits for them, and re-layouts: 0.01 us -> 2.95 us
    all_to_all x2 -> x1, waiting for transfers between devices: 43.4 us -> 30.8 us  [exchange(): lax.all_to_all(array, axis, 0, 0, axis_index_groups=groups, tiled=True)]
    ppermute x0 -> x3, starting transfers between devices: none -> 10.3 us  [local(): slices = {k: lax.ppermute(placed, 'grp', y_pairs(k)) for k in far_first}]
    ppermute x0 -> x3, waiting for transfers between devices: none -> 7.88 us  [local(): slices = {k: lax.ppermute(placed, 'grp', y_pairs(k)) for k in far_first}]
    all_to_all x2 -> x1, starting transfers between devices: 23.4 us -> 18.8 us  [exchange(): lax.all_to_all(array, axis, 0, 0, axis_index_groups=groups, tiled=True)]
    unnamed x2 -> x8, local copies, waits for them, and re-layouts: 0.01 us -> 2.95 us
  transfers between devices with their start and end apart: 7 -> 9, of which waited for: 4 -> 6; matrix products, arithmetic and copies ran while one was open for 0% -> 1% of each run, Pallas kernels for 7% -> 6%
where the time goes in v9:
time: 146 us; the launch traced here: 144 us
  waiting for transfers between devices  46.8 us (32%)
  starting transfers between devices  41.3 us (28%)
  blocking collectives  35.7 us (24%)
  Pallas kernels  15.3 us (10%)
  local copies, waits for them, and re-layouts  2.95 us (2%)
    all_to_all x2, blocking collectives, exchange(): lax.all_to_all(array, axis, 0, 0, axis_index_groups=groups, tiled=True)  35.7 us
    all_to_all x1, waiting for transfers between devices, exchange(): lax.all_to_all(array, axis, 0, 0, axis_index_groups=groups, tiled=True)  30.8 us
    all_to_all x1, starting transfers between devices, exchange(): lax.all_to_all(array, axis, 0, 0, axis_index_groups=groups, tiled=True)  18.8 us
    ppermute x3, starting transfers between devices, local(): slices = {k: lax.ppermute(placed, 'grp', y_pairs(k)) for k in far_first}  10.3 us
    ppermute x4, starting transfers between devices, local(): gots.append(lax.ppermute(sent, ('grp', 'own'), round_pairs(r)))  10.2 us
    pallas_call x4, Pallas kernels, local(): call(lambda *refs: multiply(tile_dev, *refs), struct((parts * rows + 8, c...  8.92 us
    ppermute x4, waiting for transfers between devices, local(): gots.append(lax.ppermute(sent, ('grp', 'own'), round_pairs(r)))  8.07 us
    ppermute x3, waiting for transfers between devices, local(): slices = {k: lax.ppermute(placed, 'grp', y_pairs(k)) for k in far_first}  7.88 us
  transfers between devices with their start and end apart: 9, of which 6 were waited for; matrix products, arithmetic and copies ran while one was open for 1% of the time, Pallas kernels for 6%

profile of v9, /device:TPU:6, one launch (start us, length us, event | category | flops | bytes accessed | tf_op | source)
XLA Modules:
  0.0 143.6 jit_solution(4642116384137835785)
XLA Ops:
  0.0 2.2 %shard_map.46 = bf16[64,17,2,128]{3,2,1,0:T(2,128)(2,1)} custom-call(bf16[48,8,2,128]{3,2,1,0:T(2,128)(2,1)} %bitcast.29, s32[48]{0:T(128)} %refs_1_.1, s32[48]{0:T(128)} %refs_2_.1), custom_call_target="tpu_custom_call" | custom-call | tf_op jit(solution)/shard_map/pallas_call | solution.py:253
  2.2 18.8 %all-to-all-start = ((bf16[64,17,2,128]{3,2,1,0:T(2,128)(2,1)}), bf16[64,17,2,128]{3,2,1,0:T(2,128)(2,1)}, u32[]{:S(2)}, u32[]{:S(2)}) async-start(bf16[64,17,2,128]{3,2,1,0:T(2,128)(2,1)} %shard_map.46), calls=%async_computation | async-start | bytes 1114112 | tf_op jit(solution)/shard_map/all_to_all | solution.py:235
  21.0 1.9 %collective-permute-start.3 = (bf16[768,1024]{1,0:T(8,128)(2,1)}, bf16[768,1024]{1,0:T(8,128)(2,1)}, u32[]{:S(2)}, u32[]{:S(2)}) collective-permute-start(bf16[768,1024]{1,0:T(8,128)(2,1)} %refs_4_.7), channel_id=1, source_target_pairs={{0,64},{64,0},{128,192},{192,128},{256,320},{320,256},{384,448},{4... | collective-permute-start | bytes 4718600 | tf_op jit(solution)/shard_map/ppermute | solution.py:267
  24.2 30.8 %all-to-all-done.refs_0_ = bf16[64,17,2,128]{3,2,1,0:T(2,128)(2,1)} async-done(((bf16[64,17,2,128]{3,2,1,0:T(2,128)(2,1)}), bf16[64,17,2,128]{3,2,1,0:T(2,128)(2,1)}, u32[]{:S(2)}, u32[]{:S(2)}) %all-to-all-start) | async-done | bytes 557088 | tf_op jit(solution)/shard_map/all_to_all | solution.py:235
  55.1 2.5 %shard_map.47 = bf16[48,8,2,128]{3,2,1,0:T(2,128)(2,1)} custom-call(bf16[64,17,2,128]{3,2,1,0:T(2,128)(2,1)} %all-to-all-done.refs_0_), custom_call_target="tpu_custom_call" | custom-call | tf_op jit(solution)/shard_map/pallas_call | solution.py:268
  57.6 4.9 %collective-permute-start.2 = (bf16[48,8,2,128]{3,2,1,0:T(2,128)(2,1)}, bf16[48,8,2,128]{3,2,1,0:T(2,128)(2,1)S(1)}, u32[]{:S(2)}, u32[]{:S(2)}) collective-permute-start(bf16[48,8,2,128]{3,2,1,0:T(2,128)(2,1)} %shard_map.47), channel_id=1, source_target_pairs={{0,384},{64,448},{128,0},{192,64},{256,128},{320,192},{384,256},{4... | collective-permute-start | bytes 589832 | tf_op jit(solution)/shard_map/ppermute | solution.py:282
  62.5 2.5 %collective-permute-start.1 = (bf16[48,8,2,128]{3,2,1,0:T(2,128)(2,1)}, bf16[48,8,2,128]{3,2,1,0:T(2,128)(2,1)S(1)}, u32[]{:S(2)}, u32[]{:S(2)}) collective-permute-start(bf16[48,8,2,128]{3,2,1,0:T(2,128)(2,1)} %shard_map.47), channel_id=1, source_target_pairs={{0,256},{64,320},{128,384},{192,448},{256,0},{320,64},{384,128},{4... | collective-permute-start | bytes 589832 | tf_op jit(solution)/shard_map/ppermute | solution.py:282
  65.0 2.9 %collective-permute-start = (bf16[48,8,2,128]{3,2,1,0:T(2,128)(2,1)}, bf16[48,8,2,128]{3,2,1,0:T(2,128)(2,1)S(1)}, u32[]{:S(2)}, u32[]{:S(2)}) collective-permute-start(bf16[48,8,2,128]{3,2,1,0:T(2,128)(2,1)} %shard_map.47), channel_id=1, source_target_pairs={{0,128},{64,192},{128,256},{192,320},{256,384},{320,448},{384,0},{... | collective-permute-start | bytes 589832 | tf_op jit(solution)/shard_map/ppermute | solution.py:282
  68.1 2.4 %collective-permute-done.2 = bf16[48,8,2,128]{3,2,1,0:T(2,128)(2,1)S(1)} collective-permute-done((bf16[48,8,2,128]{3,2,1,0:T(2,128)(2,1)}, bf16[48,8,2,128]{3,2,1,0:T(2,128)(2,1)S(1)}, u32[]{:S(2)}, u32[]{:S(2)}) %collective-permute-start.2) | collective-permute-done | bytes 196640 | tf_op jit(solution)/shard_map/ppermute | solution.py:282
  70.5 3.4 %collective-permute-done.1 = bf16[48,8,2,128]{3,2,1,0:T(2,128)(2,1)S(1)} collective-permute-done((bf16[48,8,2,128]{3,2,1,0:T(2,128)(2,1)}, bf16[48,8,2,128]{3,2,1,0:T(2,128)(2,1)S(1)}, u32[]{:S(2)}, u32[]{:S(2)}) %collective-permute-start.1) | collective-permute-done | bytes 196640 | tf_op jit(solution)/shard_map/ppermute | solution.py:282
  73.9 2.1 %collective-permute-done = bf16[48,8,2,128]{3,2,1,0:T(2,128)(2,1)S(1)} collective-permute-done((bf16[48,8,2,128]{3,2,1,0:T(2,128)(2,1)}, bf16[48,8,2,128]{3,2,1,0:T(2,128)(2,1)S(1)}, u32[]{:S(2)}, u32[]{:S(2)}) %collective-permute-start) | collective-permute-done | bytes 196640 | tf_op jit(solution)/shard_map/ppermute | solution.py:282
  76.0 1.4 copy-done
  78.9 2.2 %shard_map.48 = s16[264,1024]{1,0:T(8,128)(2,1)S(1)} custom-call(bf16[48,16,128]{2,1,0:T(8,128)(2,1)S(1)} %bitcast.13, bf16[48,16,128]{2,1,0:T(8,128)(2,1)S(1)} %bitcast.25, bf16[48,16,128]{2,1,0:T(8,128)(2,1)S(1)} %bitcast.21, bf16[48,16,128]{2,1,0:T(8,128)(2,1)S(1)} %bitcast.17, bf16[768,1024]{1,0:T(8,128)(2,1)S(1)} %copy-done, ...), custom_call_target="tpu_custom_call" | custom-call | tf_op jit(solution)/shard_map/pallas_call | solution.py:289
  81.1 1.9 %collective-permute-start.4 = (s16[264,1024]{1,0:T(8,128)(2,1)S(1)}, s16[264,1024]{1,0:T(8,128)(2,1)S(1)}, u32[]{:S(2)}, u32[]{:S(2)}) collective-permute-start(s16[264,1024]{1,0:T(8,128)(2,1)S(1)} %shard_map.48), channel_id=1, source_target_pairs={{0,2},{1,66},{2,0},{3,64},{4,6},{5,70},{6,4},{7,68},{8,10},{9,74},... | collective-permute-start | bytes 1622024 | tf_op jit(solution)/shard_map/ppermute | solution.py:295
  83.1 2.2 %shard_map.49 = s16[264,1024]{1,0:T(8,128)(2,1)S(1)} custom-call(bf16[48,16,128]{2,1,0:T(8,128)(2,1)S(1)} %bitcast.14, bf16[48,16,128]{2,1,0:T(8,128)(2,1)S(1)} %bitcast.26, bf16[48,16,128]{2,1,0:T(8,128)(2,1)S(1)} %bitcast.22, bf16[48,16,128]{2,1,0:T(8,128)(2,1)S(1)} %bitcast.18, bf16[768,1024]{1,0:T(8,128)(2,1)S(1)} %copy-done, ...), custom_call_target="tpu_custom_call" | custom-call | tf_op jit(solution)/shard_map/pallas_call | solution.py:289
  85.3 3.5 %collective-permute-start.5 = (s16[264,1024]{1,0:T(8,128)(2,1)S(1)}, s16[264,1024]{1,0:T(8,128)(2,1)S(1)}, u32[]{:S(2)}, u32[]{:S(2)}) collective-permute-start(s16[264,1024]{1,0:T(8,128)(2,1)S(1)} %shard_map.49), channel_id=1, source_target_pairs={{0,66},{1,2},{2,64},{3,0},{4,70},{5,6},{6,68},{7,4},{8,74},{9,10},... | collective-permute-start | bytes 1622024 | tf_op jit(solution)/shard_map/ppermute | solution.py:295
  88.8 2.2 %shard_map.50 = s16[264,1024]{1,0:T(8,128)(2,1)S(1)} custom-call(bf16[48,16,128]{2,1,0:T(8,128)(2,1)S(1)} %bitcast.15, bf16[48,16,128]{2,1,0:T(8,128)(2,1)S(1)} %bitcast.27, bf16[48,16,128]{2,1,0:T(8,128)(2,1)S(1)} %bitcast.23, bf16[48,16,128]{2,1,0:T(8,128)(2,1)S(1)} %bitcast.19, bf16[768,1024]{1,0:T(8,128)(2,1)S(1)} %copy-done, ...), custom_call_target="tpu_custom_call" | custom-call | tf_op jit(solution)/shard_map/pallas_call | solution.py:289
  91.1 1.9 %collective-permute-start.6 = (s16[264,1024]{1,0:T(8,128)(2,1)S(1)}, s16[264,1024]{1,0:T(8,128)(2,1)S(1)}, u32[]{:S(2)}, u32[]{:S(2)}) collective-permute-start(s16[264,1024]{1,0:T(8,128)(2,1)S(1)} %shard_map.50), channel_id=1, source_target_pairs={{0,0},{1,64},{2,2},{3,66},{4,4},{5,68},{6,6},{7,70},{8,8},{9,72},{... | collective-permute-start | bytes 1622024 | tf_op jit(solution)/shard_map/ppermute | solution.py:295
  93.0 2.2 %shard_map.51 = s16[264,1024]{1,0:T(8,128)(2,1)S(1)} custom-call(bf16[48,16,128]{2,1,0:T(8,128)(2,1)S(1)} %bitcast.16, bf16[48,16,128]{2,1,0:T(8,128)(2,1)S(1)} %bitcast.28, bf16[48,16,128]{2,1,0:T(8,128)(2,1)S(1)} %bitcast.24, bf16[48,16,128]{2,1,0:T(8,128)(2,1)S(1)} %bitcast.20, bf16[768,1024]{1,0:T(8,128)(2,1)S(1)} %copy-done, ...), custom_call_target="tpu_custom_call" | custom-call | tf_op jit(solution)/shard_map/pallas_call | solution.py:289
  95.2 2.9 %collective-permute-start.7 = (s16[264,1024]{1,0:T(8,128)(2,1)S(1)}, s16[264,1024]{1,0:T(8,128)(2,1)S(1)}, u32[]{:S(2)}, u32[]{:S(2)}) collective-permute-start(s16[264,1024]{1,0:T(8,128)(2,1)S(1)} %shard_map.51), channel_id=1, source_target_pairs={{0,64},{1,0},{2,66},{3,2},{4,68},{5,4},{6,70},{7,6},{8,72},{9,8},{... | collective-permute-start | bytes 1622024 | tf_op jit(solution)/shard_map/ppermute | solution.py:295
  98.1 5.3 %collective-permute-done.4.refs_0_ = s16[264,1024]{1,0:T(8,128)(2,1)S(1)} collective-permute-done((s16[264,1024]{1,0:T(8,128)(2,1)S(1)}, s16[264,1024]{1,0:T(8,128)(2,1)S(1)}, u32[]{:S(2)}, u32[]{:S(2)}) %collective-permute-start.4) | collective-permute-done | bytes 540704 | tf_op jit(solution)/shard_map/ppermute | solution.py:295
  103.4 2.8 %collective-permute-done.5.refs_1_ = s16[264,1024]{1,0:T(8,128)(2,1)S(1)} collective-permute-done((s16[264,1024]{1,0:T(8,128)(2,1)S(1)}, s16[264,1024]{1,0:T(8,128)(2,1)S(1)}, u32[]{:S(2)}, u32[]{:S(2)}) %collective-permute-start.5) | collective-permute-done | bytes 540704 | tf_op jit(solution)/shard_map/ppermute | solution.py:295
  107.0 17.3 %all_to_all.15.got = s16[4,520,128]{2,1,0:T(8,128)(2,1)S(1)} all-to-all(s16[4,520,128]{2,1,0:T(8,128)(2,1)S(1)} %shard_map.52), channel_id=1, replica_groups={{0,4,8,12},{1,5,9,13},{2,6,10,14},{3,7,11,15},{16,20,24,28},{17,21,25,2..., dimensions={0} | all-to-all | bytes 1064960 | tf_op jit(solution)/shard_map/all_to_all | solution.py:235
  124.5 18.4 %all_to_all.16.got = s16[4,136,128]{2,1,0:T(8,128)(2,1)S(1)} all-to-all(s16[4,136,128]{2,1,0:T(8,128)(2,1)S(1)} %shard_map.53), channel_id=1, replica_groups={{0,16,32,48},{1,17,33,49},{2,18,34,50},{3,19,35,51},{4,20,36,52},{5,21,..., dimensions={0} | all-to-all | bytes 278528 | tf_op jit(solution)/shard_map/all_to_all | solution.py:235
  (17 shorter events, 4.5 us)
Async XLA Ops:
  2.2 52.8 %all-to-all-start = ((bf16[64,17,2,128]{3,2,1,0:T(2,128)(2,1)}), bf16[64,17,2,128]{3,2,1,0:T(2,128)(2,1)}, u32[]{:S(2)}, u32[]{:S(2)}) async-start(bf16[64,17,2,128]{3,2,1,0:T(2,128)(2,1)} %shard_map.46), calls=%async_computation | async-start | bytes 1114112 | tf_op jit(solution)/shard_map/all_to_all | solution.py:235
  21.0 47.1 %collective-permute-start.3 = (bf16[768,1024]{1,0:T(8,128)(2,1)}, bf16[768,1024]{1,0:T(8,128)(2,1)}, u32[]{:S(2)}, u32[]{:S(2)}) collective-permute-start(bf16[768,1024]{1,0:T(8,128)(2,1)} %refs_4_.7), channel_id=1, source_target_pairs={{0,64},{64,0},{128,192},{192,128},{256,320},{320,256},{384,448},{4... | collective-permute-start | bytes 4718600 | tf_op jit(solution)/shard_map/ppermute | solution.py:267
  57.6 12.9 %collective-permute-start.2 = (bf16[48,8,2,128]{3,2,1,0:T(2,128)(2,1)}, bf16[48,8,2,128]{3,2,1,0:T(2,128)(2,1)S(1)}, u32[]{:S(2)}, u32[]{:S(2)}) collective-permute-start(bf16[48,8,2,128]{3,2,1,0:T(2,128)(2,1)} %shard_map.47), channel_id=1, source_target_pairs={{0,384},{64,448},{128,0},{192,64},{256,128},{320,192},{384,256},{4... | collective-permute-start | bytes 589832 | tf_op jit(solution)/shard_map/ppermute | solution.py:282
  62.5 11.4 %collective-permute-start.1 = (bf16[48,8,2,128]{3,2,1,0:T(2,128)(2,1)}, bf16[48,8,2,128]{3,2,1,0:T(2,128)(2,1)S(1)}, u32[]{:S(2)}, u32[]{:S(2)}) collective-permute-start(bf16[48,8,2,128]{3,2,1,0:T(2,128)(2,1)} %shard_map.47), channel_id=1, source_target_pairs={{0,256},{64,320},{128,384},{192,448},{256,0},{320,64},{384,128},{4... | collective-permute-start | bytes 589832 | tf_op jit(solution)/shard_map/ppermute | solution.py:282
  65.0 10.9 %collective-permute-start = (bf16[48,8,2,128]{3,2,1,0:T(2,128)(2,1)}, bf16[48,8,2,128]{3,2,1,0:T(2,128)(2,1)S(1)}, u32[]{:S(2)}, u32[]{:S(2)}) collective-permute-start(bf16[48,8,2,128]{3,2,1,0:T(2,128)(2,1)} %shard_map.47), channel_id=1, source_target_pairs={{0,128},{64,192},{128,256},{192,320},{256,384},{320,448},{384,0},{... | collective-permute-start | bytes 589832 | tf_op jit(solution)/shard_map/ppermute | solution.py:282
  76.0 1.4 copy-start
  77.4 0.9 copy-start.1
  78.3 0.6 copy-start.3
  78.9 4.2 %copy-start.2 = (s32[4]{0:T(128)S(1)}, s32[4]{0:T(128)}, u32[]{:S(2)}) copy-start(s32[4]{0:T(128)} %add_add_fusion.1.refs_6_) | copy-start | bytes 52
  81.1 22.3 %collective-permute-start.4 = (s16[264,1024]{1,0:T(8,128)(2,1)S(1)}, s16[264,1024]{1,0:T(8,128)(2,1)S(1)}, u32[]{:S(2)}, u32[]{:S(2)}) collective-permute-start(s16[264,1024]{1,0:T(8,128)(2,1)S(1)} %shard_map.48), channel_id=1, source_target_pairs={{0,2},{1,66},{2,0},{3,64},{4,6},{5,70},{6,4},{7,68},{8,10},{9,74},... | collective-permute-start | bytes 1622024 | tf_op jit(solution)/shard_map/ppermute | solution.py:295
  85.3 20.9 %collective-permute-start.5 = (s16[264,1024]{1,0:T(8,128)(2,1)S(1)}, s16[264,1024]{1,0:T(8,128)(2,1)S(1)}, u32[]{:S(2)}, u32[]{:S(2)}) collective-permute-start(s16[264,1024]{1,0:T(8,128)(2,1)S(1)} %shard_map.49), channel_id=1, source_target_pairs={{0,66},{1,2},{2,64},{3,0},{4,70},{5,6},{6,68},{7,4},{8,74},{9,10},... | collective-permute-start | bytes 1622024 | tf_op jit(solution)/shard_map/ppermute | solution.py:295
  91.1 15.2 %collective-permute-start.6 = (s16[264,1024]{1,0:T(8,128)(2,1)S(1)}, s16[264,1024]{1,0:T(8,128)(2,1)S(1)}, u32[]{:S(2)}, u32[]{:S(2)}) collective-permute-start(s16[264,1024]{1,0:T(8,128)(2,1)S(1)} %shard_map.50), channel_id=1, source_target_pairs={{0,0},{1,64},{2,2},{3,66},{4,4},{5,68},{6,6},{7,70},{8,8},{9,72},{... | collective-permute-start | bytes 1622024 | tf_op jit(solution)/shard_map/ppermute | solution.py:295
  95.2 11.0 %collective-permute-start.7 = (s16[264,1024]{1,0:T(8,128)(2,1)S(1)}, s16[264,1024]{1,0:T(8,128)(2,1)S(1)}, u32[]{:S(2)}, u32[]{:S(2)}) collective-permute-start(s16[264,1024]{1,0:T(8,128)(2,1)S(1)} %shard_map.51), channel_id=1, source_target_pairs={{0,64},{1,0},{2,66},{3,2},{4,68},{5,4},{6,70},{7,6},{8,72},{9,8},{... | collective-permute-start | bytes 1622024 | tf_op jit(solution)/shard_map/ppermute | solution.py:295

commit v10 on v7

--- a/solution.py
+++ b/solution.py
@@ -10,7 +10,7 @@
 NX = 4
 UNIT = 8
 CORES = 2
-LOWS = 4
+PAIR = 2
 LINES = 2
 TOP = 32767.0
 STEPS = 64.0
@@ -153,36 +153,38 @@
     return tiles
 
 
-def add_x(rows, *refs):
-    *gots, out = refs
-    parts = (gots[0].shape[0] - 8) // rows
+def add_x(which, *refs):
+    *gots, kept, out, held = refs
+    parts, blocks = held.shape[0], held.shape[1]
+    rows = (gots[0].shape[0] - 8) // parts
     cols = gots[0].shape[1]
-    occ = rows // NB
-    lows = out.shape[0]
+    occ = rows // blocks
+    lanes = cols // 128
     scales = [scale_of(got[parts * rows :, :]) for got in gots]
-    tiles = [[] for _ in range(lows)]
-    for b in range(NB):
-        for h in range(parts):
-            z = parts * b + h
+    for h in range(parts):
+        for b in range(blocks):
             for u in range(occ // UNIT):
                 total = None
                 at = h * rows + b * occ + u * UNIT
                 for got, scale in zip(gots, scales):
                     term = plain(got[at : at + UNIT, :]) * scale
                     total = term if total is None else total + term
-                tiles[z % lows] += [total[:, 128 * t : 128 * (t + 1)] for t in range(cols // 128)]
-    for low in range(lows):
-        recoded(tiles[low], out, low)
-
-
-def add_low(got, out):
-    tiles = decoded(got, UNIT)
-    count = len(tiles) // out.shape[0]
-    for high in range(out.shape[0]):
-        recoded(tiles[high * count : (high + 1) * count], out, high)
-
-
-def add_high(got, out):
+                for t in range(lanes):
+                    held[h, b, u * lanes + t] = total[:, 128 * t : 128 * (t + 1)]
+    other = 1 - which[0]
+    for b in range(blocks):
+        recoded([held[other, b, n] for n in range(held.shape[2])], out, b)
+    kept[...] = held[which[0]]
+
+
+def add_pair(kept, got, out):
+    count = kept.shape[1]
+    for b in range(kept.shape[0]):
+        scale = scale_of(got[b, count * UNIT :, :])
+        recoded([kept[b, n] + plain(got[b, n * UNIT : (n + 1) * UNIT, :]) * scale for n in range(count)], out, b)
+
+
+def add_z(got, out):
     lanes = out.shape[1] // 128
     for n, tile in enumerate(decoded(got, UNIT)):
         u, t = n // lanes, n % lanes
@@ -204,14 +206,13 @@
 def local(amplitudes, integrals, tile_block, tile_index):
     own, grp = lax.axis_size("own"), lax.axis_size("grp")
     nz, ny = own // NX, grp // CORES
-    highs = nz // LOWS
-    low_groups = []
+    z_groups = [[z * NX + x for z in range(p, nz, PAIR)] for p in range(PAIR) for x in range(NX)]
+    z_pairs = []
     for g in range(grp):
-        shift = g % CORES * (LOWS // CORES)
-        for high in range(highs):
-            line = sorted(((high * LOWS + low + shift) % nz for low in range(LOWS)), key=lambda z: z % LOWS)
-            low_groups += [[g * own + z * NX + x for z in line] for x in range(NX)]
-    high_groups = [[(high * LOWS + low) * NX + x for high in range(highs)] for low in range(LOWS) for x in range(NX)]
+        for o in range(own):
+            z = o // NX
+            partner = (z + 1 if z % PAIR == g % CORES else z - 1) % nz
+            z_pairs.append((g * own + o, g * own + partner * NX + o % NX))
     y_groups = [[y * CORES + c for y in range(ny)] for c in range(CORES)]
     core_pairs = [(y * CORES + c, y * CORES + 1 - c) for y in range(ny) for c in range(CORES)]
 
@@ -285,15 +286,17 @@
             [pltpu.VMEM((parts * rows, tile_dev * width), dtype)],
         )(mine, integrals, theirs, which)
         gots.append(lax.ppermute(sent, ("grp", "own"), round_pairs(r)))
-    sent = call(
-        lambda *refs: add_x(rows, *refs),
-        struct((LOWS, (highs * units * tiles + 1) * UNIT, 128), jnp.int16),
-        [VMEM] * len(gots),
-    )(*gots)
-    sent = call(add_low, struct((highs, (units * tiles + 1) * UNIT, 128), jnp.int16), [VMEM])(
-        exchange(sent, low_groups, ("grp", "own"))
-    )
-    return call(add_high, struct((occ, cols), jnp.float32), [VMEM])(exchange(sent, high_groups))
+    parity = jnp.reshape(lax.axis_index("own") // NX % PAIR, (1,)).astype(jnp.int32)
+    count = units * tiles
+    coded_sums = struct((NB, (count + 1) * UNIT, 128), jnp.int16)
+    kept, sent = call(
+        add_x,
+        [struct((NB, count, UNIT, 128), jnp.float32), coded_sums],
+        [SMEM] + [VMEM] * len(gots),
+        [pltpu.VMEM((PAIR, NB, count, UNIT, 128), jnp.float32)],
+    )(parity, *gots)
+    sent = call(add_pair, coded_sums, [VMEM, VMEM])(kept, lax.ppermute(sent, ("grp", "own"), z_pairs))
+    return call(add_z, struct((occ, cols), jnp.float32), [VMEM])(exchange(sent, z_groups))
 
 
 def solution(mesh):

time: 141 us -> 143 us (1.014); the launches traced: 139 us -> 142 us
  blocking collectives: 35.9 us -> 23.8 us
  starting transfers between devices: 35.5 us -> 42.5 us
  waiting for transfers between devices: 51.5 us -> 57.1 us
  Pallas kernels: 15.3 us -> 18.3 us
    all_to_all x2 -> x1, blocking collectives: 35.9 us -> 23.8 us  [exchange(): lax.all_to_all(array, axis, 0, 0, axis_index_groups=groups, tiled=True)]
    ppermute x0 -> x1, waiting for transfers between devices: none -> 6.51 us  [local(): lax.ppermute(sent, ('grp', 'own'), z_pairs)]
    ppermute x4, starting transfers between devices: 10.2 us -> 15.3 us  [local(): gots.append(lax.ppermute(sent, ('grp', 'own'), round_pairs(r)))]
    ppermute x0 -> x1, starting transfers between devices: none -> 1.92 us  [local(): lax.ppermute(sent, ('grp', 'own'), z_pairs)]
    pallas_call x4, Pallas kernels: 8.7 us -> 10.3 us  [local(): call(lambda *refs: multiply(tile_dev, *refs), struct((parts * rows + 8, c...]
  transfers between devices with their start and end apart: 7 -> 8, of which waited for: 4 -> 5; matrix products, arithmetic and copies ran while one was open for 0% -> 0% of each run, Pallas kernels for 7% -> 8%
where the time goes in v10:
time: 143 us; the launch traced here: 142 us
  waiting for transfers between devices  57.1 us (40%)
  starting transfers between devices  42.5 us (30%)
  blocking collectives  23.8 us (17%)
  Pallas kernels  18.3 us (13%)
    all_to_all x2, waiting for transfers between devices, exchange(): lax.all_to_all(array, axis, 0, 0, axis_index_groups=groups, tiled=True)  43.4 us
    all_to_all x1, blocking collectives, exchange(): lax.all_to_all(array, axis, 0, 0, axis_index_groups=groups, tiled=True)  23.8 us
    all_to_all x2, starting transfers between devices, exchange(): lax.all_to_all(array, axis, 0, 0, axis_index_groups=groups, tiled=True)  23.4 us
    ppermute x4, starting transfers between devices, local(): gots.append(lax.ppermute(sent, ('grp', 'own'), round_pairs(r)))  15.3 us
    pallas_call x4, Pallas kernels, local(): call(lambda *refs: multiply(tile_dev, *refs), struct((parts * rows + 8, c...  10.3 us
    ppermute x4, waiting for transfers between devices, local(): gots.append(lax.ppermute(sent, ('grp', 'own'), round_pairs(r)))  7.13 us
    ppermute x1, waiting for transfers between devices, local(): lax.ppermute(sent, ('grp', 'own'), z_pairs)  6.51 us
  transfers between devices with their start and end apart: 8, of which 5 were waited for; matrix products, arithmetic and copies ran while one was open for 0% of the time, Pallas kernels for 8%

profile of v10, /device:TPU:6, one launch (start us, length us, event | category | flops | bytes accessed | tf_op | source)
XLA Modules:
  0.0 142.1 jit_solution(9555422670839775610)
XLA Ops:
  0.0 2.2 %shard_map.46 = bf16[64,17,2,128]{3,2,1,0:T(2,128)(2,1)} custom-call(bf16[48,8,2,128]{3,2,1,0:T(2,128)(2,1)} %bitcast.11, s32[48]{0:T(128)} %refs_1_.5, s32[48]{0:T(128)} %refs_2_.1), custom_call_target="tpu_custom_call" | custom-call | tf_op jit(solution)/shard_map/pallas_call | solution.py:249
  2.2 18.8 %all-to-all-start = ((bf16[64,17,2,128]{3,2,1,0:T(2,128)(2,1)}), bf16[64,17,2,128]{3,2,1,0:T(2,128)(2,1)}, u32[]{:S(2)}, u32[]{:S(2)}) async-start(bf16[64,17,2,128]{3,2,1,0:T(2,128)(2,1)} %shard_map.46), calls=%async_computation | async-start | bytes 1114112 | tf_op jit(solution)/shard_map/all_to_all | solution.py:232
  21.0 1.9 %collective-permute-start = (bf16[768,1024]{1,0:T(8,128)(2,1)}, bf16[768,1024]{1,0:T(8,128)(2,1)}, u32[]{:S(2)}, u32[]{:S(2)}) collective-permute-start(bf16[768,1024]{1,0:T(8,128)(2,1)} %refs_1_.9), channel_id=1, source_target_pairs={{0,64},{64,0},{128,192},{192,128},{256,320},{320,256},{384,448},{4... | collective-permute-start | bytes 4718600 | tf_op jit(solution)/shard_map/ppermute | solution.py:263
  22.9 32.1 %all-to-all-done.refs_0_ = bf16[64,17,2,128]{3,2,1,0:T(2,128)(2,1)} async-done(((bf16[64,17,2,128]{3,2,1,0:T(2,128)(2,1)}), bf16[64,17,2,128]{3,2,1,0:T(2,128)(2,1)}, u32[]{:S(2)}, u32[]{:S(2)}) %all-to-all-start) | async-done | bytes 557088 | tf_op jit(solution)/shard_map/all_to_all | solution.py:232
  55.1 2.7 %shard_map.47 = bf16[4,48,8,2,128]{4,3,2,1,0:T(2,128)(2,1)} custom-call(bf16[64,17,2,128]{3,2,1,0:T(2,128)(2,1)} %all-to-all-done.refs_0_), custom_call_target="tpu_custom_call" | custom-call | tf_op jit(solution)/shard_map/pallas_call | solution.py:264
  57.8 4.6 %all-to-all-start.1 = ((bf16[4,48,8,2,128]{4,3,2,1,0:T(2,128)(2,1)}), bf16[4,48,8,2,128]{4,3,2,1,0:T(2,128)(2,1)S(1)}, u32[]{:S(2)}, u32[]{:S(2)}) async-start(bf16[4,48,8,2,128]{4,3,2,1,0:T(2,128)(2,1)} %shard_map.47), calls=%async_computation.1 | async-start | bytes 1572864 | tf_op jit(solution)/shard_map/all_to_all | solution.py:232
  62.4 0.1 pad_add_fusion.2.refs_3_
  62.7 11.3 %all-to-all-done.1 = bf16[4,48,8,2,128]{4,3,2,1,0:T(2,128)(2,1)S(1)} async-done(((bf16[4,48,8,2,128]{4,3,2,1,0:T(2,128)(2,1)}), bf16[4,48,8,2,128]{4,3,2,1,0:T(2,128)(2,1)S(1)}, u32[]{:S(2)}, u32[]{:S(2)}) %all-to-all-start.1) | async-done | bytes 786464 | tf_op jit(solution)/shard_map/all_to_all | solution.py:232
  74.0 2.2 %shard_map.48 = s16[264,1024]{1,0:T(8,128)(2,1)S(1)} custom-call(bf16[4,48,16,128]{3,2,1,0:T(8,128)(2,1)S(1)} %bitcast.7, bf16[768,1024]{1,0:T(8,128)(2,1)S(1)} %copy-done, bf16[768,1024]{1,0:T(8,128)(2,1)} %collective-permute-done.refs_2_, s32[2]{0:T(128)S(1)} %pad_add_fusion.1.refs_3_), custom_call_target="tpu_custom_call" | custom-call | tf_op jit(solution)/shard_map/pallas_call | solution.py:282
  76.2 1.9 %collective-permute-start.1 = (s16[264,1024]{1,0:T(8,128)(2,1)S(1)}, s16[264,1024]{1,0:T(8,128)(2,1)}, u32[]{:S(2)}, u32[]{:S(2)}) collective-permute-start(s16[264,1024]{1,0:T(8,128)(2,1)S(1)} %shard_map.48), channel_id=1, source_target_pairs={{0,2},{1,66},{2,0},{3,64},{4,6},{5,70},{6,4},{7,68},{8,10},{9,74},... | collective-permute-start | bytes 1622024 | tf_op jit(solution)/shard_map/ppermute | solution.py:288
  78.1 2.2 %shard_map.49 = s16[264,1024]{1,0:T(8,128)(2,1)S(1)} custom-call(bf16[4,48,16,128]{3,2,1,0:T(8,128)(2,1)S(1)} %bitcast.8, bf16[768,1024]{1,0:T(8,128)(2,1)S(1)} %copy-done, bf16[768,1024]{1,0:T(8,128)(2,1)} %collective-permute-done.refs_2_, s32[2]{0:T(128)S(1)} %pad_add_fusion.2.refs_3_), custom_call_target="tpu_custom_call" | custom-call | tf_op jit(solution)/shard_map/pallas_call | solution.py:282
  80.3 3.3 %collective-permute-start.2 = (s16[264,1024]{1,0:T(8,128)(2,1)S(1)}, s16[264,1024]{1,0:T(8,128)(2,1)}, u32[]{:S(2)}, u32[]{:S(2)}) collective-permute-start(s16[264,1024]{1,0:T(8,128)(2,1)S(1)} %shard_map.49), channel_id=1, source_target_pairs={{0,66},{1,2},{2,64},{3,0},{4,70},{5,6},{6,68},{7,4},{8,74},{9,10},... | collective-permute-start | bytes 1622024 | tf_op jit(solution)/shard_map/ppermute | solution.py:288
  83.6 3.0 %shard_map.50 = s16[264,1024]{1,0:T(8,128)(2,1)} custom-call(bf16[4,48,16,128]{3,2,1,0:T(8,128)(2,1)S(1)} %bitcast.9, bf16[768,1024]{1,0:T(8,128)(2,1)S(1)} %copy-done, bf16[768,1024]{1,0:T(8,128)(2,1)} %collective-permute-done.refs_2_, s32[2]{0:T(128)S(1)} %pad_add_fusion.refs_3_), custom_call_target="tpu_custom_call" | custom-call | tf_op jit(solution)/shard_map/pallas_call | solution.py:282
  86.6 1.9 %collective-permute-start.3 = (s16[264,1024]{1,0:T(8,128)(2,1)}, s16[264,1024]{1,0:T(8,128)(2,1)}, u32[]{:S(2)}, u32[]{:S(2)}) collective-permute-start(s16[264,1024]{1,0:T(8,128)(2,1)} %shard_map.50), channel_id=1, source_target_pairs={{0,0},{1,64},{2,2},{3,66},{4,4},{5,68},{6,6},{7,70},{8,8},{9,72},{... | collective-permute-start | bytes 1622024 | tf_op jit(solution)/shard_map/ppermute | solution.py:288
  88.5 3.0 %shard_map.51 = s16[264,1024]{1,0:T(8,128)(2,1)} custom-call(bf16[4,48,16,128]{3,2,1,0:T(8,128)(2,1)S(1)} %bitcast.10, bf16[768,1024]{1,0:T(8,128)(2,1)S(1)} %copy-done, bf16[768,1024]{1,0:T(8,128)(2,1)} %collective-permute-done.refs_2_, s32[2]{0:T(128)S(1)} %pad_add_fusion.3.refs_3_), custom_call_target="tpu_custom_call" | custom-call | tf_op jit(solution)/shard_map/pallas_call | solution.py:282
  91.5 8.2 %collective-permute-start.4 = (s16[264,1024]{1,0:T(8,128)(2,1)}, s16[264,1024]{1,0:T(8,128)(2,1)S(1)}, u32[]{:S(2)}, u32[]{:S(2)}) collective-permute-start(s16[264,1024]{1,0:T(8,128)(2,1)} %shard_map.51), channel_id=1, source_target_pairs={{0,64},{1,0},{2,66},{3,2},{4,68},{5,4},{6,70},{7,6},{8,72},{9,8},{... | collective-permute-start | bytes 1622024 | tf_op jit(solution)/shard_map/ppermute | solution.py:288
  99.7 1.3 collective-permute-done.2.refs_1_
  101.1 5.8 %collective-permute-done.4.refs_3_ = s16[264,1024]{1,0:T(8,128)(2,1)S(1)} collective-permute-done((s16[264,1024]{1,0:T(8,128)(2,1)}, s16[264,1024]{1,0:T(8,128)(2,1)S(1)}, u32[]{:S(2)}, u32[]{:S(2)}) %collective-permute-start.4) | collective-permute-done | bytes 540704 | tf_op jit(solution)/shard_map/ppermute | solution.py:288
  106.9 2.2 %shard_map.52 = (f32[8,16,8,128]{3,2,1,0:T(8,128)S(1)}, s16[8,136,128]{2,1,0:T(8,128)(2,1)S(1)}) custom-call(s32[1]{0:T(128)} %bitcast.which, s16[264,1024]{1,0:T(8,128)(2,1)} %collective-permute-done.1.refs_0_, s16[264,1024]{1,0:T(8,128)(2,1)} %collective-permute-done.2.refs_1_, s16[264,1024]{1,0:T(8,128)(2,1)} %collective-permute-done.3.refs_2_, ...), custom_call_target="tpu_custom_call" | custom-call | tf_op jit(solution)/shard_map/pallas_call | solution.py:292
  109.0 1.9 %collective-permute-start.5 = (s16[8,136,128]{2,1,0:T(8,128)(2,1)S(1)}, s16[8,136,128]{2,1,0:T(8,128)(2,1)S(1)}, u32[]{:S(2)}, u32[]{:S(2)}) collective-permute-start(s16[8,136,128]{2,1,0:T(8,128)(2,1)S(1)} %get-tuple-element.8), channel_id=1, source_target_pairs={{0,4},{1,5},{2,6},{3,7},{4,0},{5,1},{6,2},{7,3},{8,12},{9,13},{10,... | collective-permute-start | bytes 835592 | tf_op jit(solution)/shard_map/ppermute | solution.py:298
  110.9 6.5 %collective-permute-done.5.got = s16[8,136,128]{2,1,0:T(8,128)(2,1)S(1)} collective-permute-done((s16[8,136,128]{2,1,0:T(8,128)(2,1)S(1)}, s16[8,136,128]{2,1,0:T(8,128)(2,1)S(1)}, u32[]{:S(2)}, u32[]{:S(2)}) %collective-permute-start.5) | collective-permute-done | bytes 278560 | tf_op jit(solution)/shard_map/ppermute | solution.py:298
  117.5 0.2 shard_map.53
  117.6 23.8 %all_to_all.15.got = s16[8,136,128]{2,1,0:T(8,128)(2,1)S(1)} all-to-all(s16[8,136,128]{2,1,0:T(8,128)(2,1)S(1)} %shard_map.53), channel_id=1, replica_groups={{0,8,16,24,32,40,48,56},{1,9,17,25,33,41,49,57},{2,10,18,26,34,42,50,58..., dimensions={0} | all-to-all | bytes 557056 | tf_op jit(solution)/shard_map/all_to_all | solution.py:232
  141.4 0.7 shard_map.54
  (8 shorter events, 0.2 us)
Async XLA Ops:
  2.2 52.8 %all-to-all-start = ((bf16[64,17,2,128]{3,2,1,0:T(2,128)(2,1)}), bf16[64,17,2,128]{3,2,1,0:T(2,128)(2,1)}, u32[]{:S(2)}, u32[]{:S(2)}) async-start(bf16[64,17,2,128]{3,2,1,0:T(2,128)(2,1)} %shard_map.46), calls=%async_computation | async-start | bytes 1114112 | tf_op jit(solution)/shard_map/all_to_all | solution.py:232
  21.0 41.7 %collective-permute-start = (bf16[768,1024]{1,0:T(8,128)(2,1)}, bf16[768,1024]{1,0:T(8,128)(2,1)}, u32[]{:S(2)}, u32[]{:S(2)}) collective-permute-start(bf16[768,1024]{1,0:T(8,128)(2,1)} %refs_1_.9), channel_id=1, source_target_pairs={{0,64},{64,0},{128,192},{192,128},{256,320},{320,256},{384,448},{4... | collective-permute-start | bytes 4718600 | tf_op jit(solution)/shard_map/ppermute | solution.py:263
  57.8 16.2 %copy-start = (bf16[768,1024]{1,0:T(8,128)(2,1)S(1)}, bf16[768,1024]{1,0:T(8,128)(2,1)}, u32[]{:S(2)}) copy-start(bf16[768,1024]{1,0:T(8,128)(2,1)} %refs_1_.9) | copy-start | bytes 4718596
  57.8 16.2 %all-to-all-start.1 = ((bf16[4,48,8,2,128]{4,3,2,1,0:T(2,128)(2,1)}), bf16[4,48,8,2,128]{4,3,2,1,0:T(2,128)(2,1)S(1)}, u32[]{:S(2)}, u32[]{:S(2)}) async-start(bf16[4,48,8,2,128]{4,3,2,1,0:T(2,128)(2,1)} %shard_map.47), calls=%async_computation.1 | async-start | bytes 1572864 | tf_op jit(solution)/shard_map/all_to_all | solution.py:232
  76.2 23.6 %collective-permute-start.1 = (s16[264,1024]{1,0:T(8,128)(2,1)S(1)}, s16[264,1024]{1,0:T(8,128)(2,1)}, u32[]{:S(2)}, u32[]{:S(2)}) collective-permute-start(s16[264,1024]{1,0:T(8,128)(2,1)S(1)} %shard_map.48), channel_id=1, source_target_pairs={{0,2},{1,66},{2,0},{3,64},{4,6},{5,70},{6,4},{7,68},{8,10},{9,74},... | collective-permute-start | bytes 1622024 | tf_op jit(solution)/shard_map/ppermute | solution.py:288
  80.3 20.8 %collective-permute-start.2 = (s16[264,1024]{1,0:T(8,128)(2,1)S(1)}, s16[264,1024]{1,0:T(8,128)(2,1)}, u32[]{:S(2)}, u32[]{:S(2)}) collective-permute-start(s16[264,1024]{1,0:T(8,128)(2,1)S(1)} %shard_map.49), channel_id=1, source_target_pairs={{0,66},{1,2},{2,64},{3,0},{4,70},{5,6},{6,68},{7,4},{8,74},{9,10},... | collective-permute-start | bytes 1622024 | tf_op jit(solution)/shard_map/ppermute | solution.py:288
  86.6 14.4 %collective-permute-start.3 = (s16[264,1024]{1,0:T(8,128)(2,1)}, s16[264,1024]{1,0:T(8,128)(2,1)}, u32[]{:S(2)}, u32[]{:S(2)}) collective-permute-start(s16[264,1024]{1,0:T(8,128)(2,1)} %shard_map.50), channel_id=1, source_target_pairs={{0,0},{1,64},{2,2},{3,66},{4,4},{5,68},{6,6},{7,70},{8,8},{9,72},{... | collective-permute-start | bytes 1622024 | tf_op jit(solution)/shard_map/ppermute | solution.py:288
  91.5 15.3 %collective-permute-start.4 = (s16[264,1024]{1,0:T(8,128)(2,1)}, s16[264,1024]{1,0:T(8,128)(2,1)S(1)}, u32[]{:S(2)}, u32[]{:S(2)}) collective-permute-start(s16[264,1024]{1,0:T(8,128)(2,1)} %shard_map.51), channel_id=1, source_target_pairs={{0,64},{1,0},{2,66},{3,2},{4,68},{5,4},{6,70},{7,6},{8,72},{9,8},{... | collective-permute-start | bytes 1622024 | tf_op jit(solution)/shard_map/ppermute | solution.py:288
  109.0 8.4 %collective-permute-start.5 = (s16[8,136,128]{2,1,0:T(8,128)(2,1)S(1)}, s16[8,136,128]{2,1,0:T(8,128)(2,1)S(1)}, u32[]{:S(2)}, u32[]{:S(2)}) collective-permute-start(s16[8,136,128]{2,1,0:T(8,128)(2,1)S(1)} %get-tuple-element.8), channel_id=1, source_target_pairs={{0,4},{1,5},{2,6},{3,7},{4,0},{5,1},{6,2},{7,3},{8,12},{9,13},{10,... | collective-permute-start | bytes 835592 | tf_op jit(solution)/shard_map/ppermute | solution.py:298

commit v11 on v10

--- a/solution.py
+++ b/solution.py
@@ -154,27 +154,32 @@
 
 
 def add_x(which, *refs):
-    *gots, kept, out, held = refs
-    parts, blocks = held.shape[0], held.shape[1]
-    rows = (gots[0].shape[0] - 8) // parts
+    *gots, kept, out = refs
+    blocks = kept.shape[0]
+    rows = (gots[0].shape[0] - 8) // PAIR
     cols = gots[0].shape[1]
     occ = rows // blocks
-    lanes = cols // 128
-    scales = [scale_of(got[parts * rows :, :]) for got in gots]
-    for h in range(parts):
-        for b in range(blocks):
-            for u in range(occ // UNIT):
-                total = None
-                at = h * rows + b * occ + u * UNIT
-                for got, scale in zip(gots, scales):
-                    term = plain(got[at : at + UNIT, :]) * scale
-                    total = term if total is None else total + term
-                for t in range(lanes):
-                    held[h, b, u * lanes + t] = total[:, 128 * t : 128 * (t + 1)]
-    other = 1 - which[0]
-    for b in range(blocks):
-        recoded([held[other, b, n] for n in range(held.shape[2])], out, b)
-    kept[...] = held[which[0]]
+    scales = [scale_of(got[PAIR * rows :, :]) for got in gots]
+
+    def tiles_of(h, b):
+        tiles = []
+        for u in range(occ // UNIT):
+            total = None
+            at = h * rows + b * occ + u * UNIT
+            for got, scale in zip(gots, scales):
+                term = plain(got[at : at + UNIT, :]) * scale
+                total = term if total is None else total + term
+            tiles += [total[:, 128 * t : 128 * (t + 1)] for t in range(cols // 128)]
+        return tiles
+
+    for parity in range(PAIR):
+
+        @pl.when(which[0] == parity)
+        def _(parity=parity):
+            for b in range(blocks):
+                recoded(tiles_of(1 - parity, b), out, b)
+                for n, tile in enumerate(tiles_of(parity, b)):
+                    kept[b, n] = tile
 
 
 def add_pair(kept, got, out):
@@ -293,7 +298,6 @@
         add_x,
         [struct((NB, count, UNIT, 128), jnp.float32), coded_sums],
         [SMEM] + [VMEM] * len(gots),
-        [pltpu.VMEM((PAIR, NB, count, UNIT, 128), jnp.float32)],
     )(parity, *gots)
     sent = call(add_pair, coded_sums, [VMEM, VMEM])(kept, lax.ppermute(sent, ("grp", "own"), z_pairs))
     return call(add_z, struct((occ, cols), jnp.float32), [VMEM])(exchange(sent, z_groups))

time: 143 us -> 143 us (level)
  no operation moved by 1% of the time
where the time goes in v11:
time: 143 us; the launch traced here: 142 us
  waiting for transfers between devices  57.1 us (40%)
  starting transfers between devices  42.5 us (30%)
  blocking collectives  23.8 us (17%)
  Pallas kernels  18.3 us (13%)
    all_to_all x2, waiting for transfers between devices, exchange(): lax.all_to_all(array, axis, 0, 0, axis_index_groups=groups, tiled=True)  43.4 us
    all_to_all x1, blocking collectives, exchange(): lax.all_to_all(array, axis, 0, 0, axis_index_groups=groups, tiled=True)  23.8 us
    all_to_all x2, starting transfers between devices, exchange(): lax.all_to_all(array, axis, 0, 0, axis_index_groups=groups, tiled=True)  23.4 us
    ppermute x4, starting transfers between devices, local(): gots.append(lax.ppermute(sent, ('grp', 'own'), round_pairs(r)))  15.3 us
    pallas_call x4, Pallas kernels, local(): call(lambda *refs: multiply(tile_dev, *refs), struct((parts * rows + 8, c...  10.3 us
    ppermute x4, waiting for transfers between devices, local(): gots.append(lax.ppermute(sent, ('grp', 'own'), round_pairs(r)))  7.13 us
    ppermute x1, waiting for transfers between devices, local(): lax.ppermute(sent, ('grp', 'own'), z_pairs)  6.51 us
  transfers between devices with their start and end apart: 8, of which 5 were waited for; matrix products, arithmetic and copies ran while one was open for 0% of the time, Pallas kernels for 8%

profile of v11, /device:TPU:6, one launch (start us, length us, event | category | flops | bytes accessed | tf_op | source)
XLA Modules:
  0.0 142.1 jit_solution(10891518182150009532)
XLA Ops:
  0.0 2.2 %shard_map.46 = bf16[64,17,2,128]{3,2,1,0:T(2,128)(2,1)} custom-call(bf16[48,8,2,128]{3,2,1,0:T(2,128)(2,1)} %bitcast.11, s32[48]{0:T(128)} %refs_1_.5, s32[48]{0:T(128)} %refs_2_.1), custom_call_target="tpu_custom_call" | custom-call | tf_op jit(solution)/shard_map/pallas_call | solution.py:254
  2.2 18.8 %all-to-all-start = ((bf16[64,17,2,128]{3,2,1,0:T(2,128)(2,1)}), bf16[64,17,2,128]{3,2,1,0:T(2,128)(2,1)}, u32[]{:S(2)}, u32[]{:S(2)}) async-start(bf16[64,17,2,128]{3,2,1,0:T(2,128)(2,1)} %shard_map.46), calls=%async_computation | async-start | bytes 1114112 | tf_op jit(solution)/shard_map/all_to_all | solution.py:237
  21.0 1.9 %collective-permute-start = (bf16[768,1024]{1,0:T(8,128)(2,1)}, bf16[768,1024]{1,0:T(8,128)(2,1)}, u32[]{:S(2)}, u32[]{:S(2)}) collective-permute-start(bf16[768,1024]{1,0:T(8,128)(2,1)} %refs_1_.9), channel_id=1, source_target_pairs={{0,64},{64,0},{128,192},{192,128},{256,320},{320,256},{384,448},{4... | collective-permute-start | bytes 4718600 | tf_op jit(solution)/shard_map/ppermute | solution.py:268
  22.9 32.1 %all-to-all-done.refs_0_ = bf16[64,17,2,128]{3,2,1,0:T(2,128)(2,1)} async-done(((bf16[64,17,2,128]{3,2,1,0:T(2,128)(2,1)}), bf16[64,17,2,128]{3,2,1,0:T(2,128)(2,1)}, u32[]{:S(2)}, u32[]{:S(2)}) %all-to-all-start) | async-done | bytes 557088 | tf_op jit(solution)/shard_map/all_to_all | solution.py:237
  55.1 2.7 %shard_map.47 = bf16[4,48,8,2,128]{4,3,2,1,0:T(2,128)(2,1)} custom-call(bf16[64,17,2,128]{3,2,1,0:T(2,128)(2,1)} %all-to-all-done.refs_0_), custom_call_target="tpu_custom_call" | custom-call | tf_op jit(solution)/shard_map/pallas_call | solution.py:269
  57.8 4.6 %all-to-all-start.1 = ((bf16[4,48,8,2,128]{4,3,2,1,0:T(2,128)(2,1)}), bf16[4,48,8,2,128]{4,3,2,1,0:T(2,128)(2,1)S(1)}, u32[]{:S(2)}, u32[]{:S(2)}) async-start(bf16[4,48,8,2,128]{4,3,2,1,0:T(2,128)(2,1)} %shard_map.47), calls=%async_computation.1 | async-start | bytes 1572864 | tf_op jit(solution)/shard_map/all_to_all | solution.py:237
  62.4 0.1 pad_add_fusion.2.refs_3_
  62.7 11.3 %all-to-all-done.1 = bf16[4,48,8,2,128]{4,3,2,1,0:T(2,128)(2,1)S(1)} async-done(((bf16[4,48,8,2,128]{4,3,2,1,0:T(2,128)(2,1)}), bf16[4,48,8,2,128]{4,3,2,1,0:T(2,128)(2,1)S(1)}, u32[]{:S(2)}, u32[]{:S(2)}) %all-to-all-start.1) | async-done | bytes 786464 | tf_op jit(solution)/shard_map/all_to_all | solution.py:237
  74.0 2.2 %shard_map.48 = s16[264,1024]{1,0:T(8,128)(2,1)S(1)} custom-call(bf16[4,48,16,128]{3,2,1,0:T(8,128)(2,1)S(1)} %bitcast.7, bf16[768,1024]{1,0:T(8,128)(2,1)S(1)} %copy-done, bf16[768,1024]{1,0:T(8,128)(2,1)} %collective-permute-done.refs_2_, s32[2]{0:T(128)S(1)} %pad_add_fusion.1.refs_3_), custom_call_target="tpu_custom_call" | custom-call | tf_op jit(solution)/shard_map/pallas_call | solution.py:287
  76.2 1.9 %collective-permute-start.1 = (s16[264,1024]{1,0:T(8,128)(2,1)S(1)}, s16[264,1024]{1,0:T(8,128)(2,1)}, u32[]{:S(2)}, u32[]{:S(2)}) collective-permute-start(s16[264,1024]{1,0:T(8,128)(2,1)S(1)} %shard_map.48), channel_id=1, source_target_pairs={{0,2},{1,66},{2,0},{3,64},{4,6},{5,70},{6,4},{7,68},{8,10},{9,74},... | collective-permute-start | bytes 1622024 | tf_op jit(solution)/shard_map/ppermute | solution.py:293
  78.1 2.2 %shard_map.49 = s16[264,1024]{1,0:T(8,128)(2,1)S(1)} custom-call(bf16[4,48,16,128]{3,2,1,0:T(8,128)(2,1)S(1)} %bitcast.8, bf16[768,1024]{1,0:T(8,128)(2,1)S(1)} %copy-done, bf16[768,1024]{1,0:T(8,128)(2,1)} %collective-permute-done.refs_2_, s32[2]{0:T(128)S(1)} %pad_add_fusion.2.refs_3_), custom_call_target="tpu_custom_call" | custom-call | tf_op jit(solution)/shard_map/pallas_call | solution.py:287
  80.3 3.3 %collective-permute-start.2 = (s16[264,1024]{1,0:T(8,128)(2,1)S(1)}, s16[264,1024]{1,0:T(8,128)(2,1)}, u32[]{:S(2)}, u32[]{:S(2)}) collective-permute-start(s16[264,1024]{1,0:T(8,128)(2,1)S(1)} %shard_map.49), channel_id=1, source_target_pairs={{0,66},{1,2},{2,64},{3,0},{4,70},{5,6},{6,68},{7,4},{8,74},{9,10},... | collective-permute-start | bytes 1622024 | tf_op jit(solution)/shard_map/ppermute | solution.py:293
  83.6 3.0 %shard_map.50 = s16[264,1024]{1,0:T(8,128)(2,1)} custom-call(bf16[4,48,16,128]{3,2,1,0:T(8,128)(2,1)S(1)} %bitcast.9, bf16[768,1024]{1,0:T(8,128)(2,1)S(1)} %copy-done, bf16[768,1024]{1,0:T(8,128)(2,1)} %collective-permute-done.refs_2_, s32[2]{0:T(128)S(1)} %pad_add_fusion.refs_3_), custom_call_target="tpu_custom_call" | custom-call | tf_op jit(solution)/shard_map/pallas_call | solution.py:287
  86.6 1.9 %collective-permute-start.3 = (s16[264,1024]{1,0:T(8,128)(2,1)}, s16[264,1024]{1,0:T(8,128)(2,1)}, u32[]{:S(2)}, u32[]{:S(2)}) collective-permute-start(s16[264,1024]{1,0:T(8,128)(2,1)} %shard_map.50), channel_id=1, source_target_pairs={{0,0},{1,64},{2,2},{3,66},{4,4},{5,68},{6,6},{7,70},{8,8},{9,72},{... | collective-permute-start | bytes 1622024 | tf_op jit(solution)/shard_map/ppermute | solution.py:293
  88.5 3.0 %shard_map.51 = s16[264,1024]{1,0:T(8,128)(2,1)} custom-call(bf16[4,48,16,128]{3,2,1,0:T(8,128)(2,1)S(1)} %bitcast.10, bf16[768,1024]{1,0:T(8,128)(2,1)S(1)} %copy-done, bf16[768,1024]{1,0:T(8,128)(2,1)} %collective-permute-done.refs_2_, s32[2]{0:T(128)S(1)} %pad_add_fusion.3.refs_3_), custom_call_target="tpu_custom_call" | custom-call | tf_op jit(solution)/shard_map/pallas_call | solution.py:287
  91.5 8.2 %collective-permute-start.4 = (s16[264,1024]{1,0:T(8,128)(2,1)}, s16[264,1024]{1,0:T(8,128)(2,1)S(1)}, u32[]{:S(2)}, u32[]{:S(2)}) collective-permute-start(s16[264,1024]{1,0:T(8,128)(2,1)} %shard_map.51), channel_id=1, source_target_pairs={{0,64},{1,0},{2,66},{3,2},{4,68},{5,4},{6,70},{7,6},{8,72},{9,8},{... | collective-permute-start | bytes 1622024 | tf_op jit(solution)/shard_map/ppermute | solution.py:293
  99.7 1.3 collective-permute-done.2.refs_1_
  101.1 5.8 %collective-permute-done.4.refs_3_ = s16[264,1024]{1,0:T(8,128)(2,1)S(1)} collective-permute-done((s16[264,1024]{1,0:T(8,128)(2,1)}, s16[264,1024]{1,0:T(8,128)(2,1)S(1)}, u32[]{:S(2)}, u32[]{:S(2)}) %collective-permute-start.4) | collective-permute-done | bytes 540704 | tf_op jit(solution)/shard_map/ppermute | solution.py:293
  106.9 2.1 %shard_map.52 = (f32[8,16,8,128]{3,2,1,0:T(8,128)S(1)}, s16[8,136,128]{2,1,0:T(8,128)(2,1)S(1)}) custom-call(s32[1]{0:T(128)} %bitcast.which, s16[264,1024]{1,0:T(8,128)(2,1)} %collective-permute-done.1.refs_0_, s16[264,1024]{1,0:T(8,128)(2,1)} %collective-permute-done.2.refs_1_, s16[264,1024]{1,0:T(8,128)(2,1)} %collective-permute-done.3.refs_2_, ...), custom_call_target="tpu_custom_call" | custom-call | tf_op jit(solution)/shard_map/pallas_call | solution.py:297
  109.0 1.9 %collective-permute-start.5 = (s16[8,136,128]{2,1,0:T(8,128)(2,1)S(1)}, s16[8,136,128]{2,1,0:T(8,128)(2,1)S(1)}, u32[]{:S(2)}, u32[]{:S(2)}) collective-permute-start(s16[8,136,128]{2,1,0:T(8,128)(2,1)S(1)} %get-tuple-element.8), channel_id=1, source_target_pairs={{0,4},{1,5},{2,6},{3,7},{4,0},{5,1},{6,2},{7,3},{8,12},{9,13},{10,... | collective-permute-start | bytes 835592 | tf_op jit(solution)/shard_map/ppermute | solution.py:302
  110.9 6.5 %collective-permute-done.5.got = s16[8,136,128]{2,1,0:T(8,128)(2,1)S(1)} collective-permute-done((s16[8,136,128]{2,1,0:T(8,128)(2,1)S(1)}, s16[8,136,128]{2,1,0:T(8,128)(2,1)S(1)}, u32[]{:S(2)}, u32[]{:S(2)}) %collective-permute-start.5) | collective-permute-done | bytes 278560 | tf_op jit(solution)/shard_map/ppermute | solution.py:302
  117.4 0.2 shard_map.53
  117.6 23.8 %all_to_all.15.got = s16[8,136,128]{2,1,0:T(8,128)(2,1)S(1)} all-to-all(s16[8,136,128]{2,1,0:T(8,128)(2,1)S(1)} %shard_map.53), channel_id=1, replica_groups={{0,8,16,24,32,40,48,56},{1,9,17,25,33,41,49,57},{2,10,18,26,34,42,50,58..., dimensions={0} | all-to-all | bytes 557056 | tf_op jit(solution)/shard_map/all_to_all | solution.py:237
  141.4 0.7 shard_map.54
  (8 shorter events, 0.2 us)
Async XLA Ops:
  2.2 52.8 %all-to-all-start = ((bf16[64,17,2,128]{3,2,1,0:T(2,128)(2,1)}), bf16[64,17,2,128]{3,2,1,0:T(2,128)(2,1)}, u32[]{:S(2)}, u32[]{:S(2)}) async-start(bf16[64,17,2,128]{3,2,1,0:T(2,128)(2,1)} %shard_map.46), calls=%async_computation | async-start | bytes 1114112 | tf_op jit(solution)/shard_map/all_to_all | solution.py:237
  21.0 41.7 %collective-permute-start = (bf16[768,1024]{1,0:T(8,128)(2,1)}, bf16[768,1024]{1,0:T(8,128)(2,1)}, u32[]{:S(2)}, u32[]{:S(2)}) collective-permute-start(bf16[768,1024]{1,0:T(8,128)(2,1)} %refs_1_.9), channel_id=1, source_target_pairs={{0,64},{64,0},{128,192},{192,128},{256,320},{320,256},{384,448},{4... | collective-permute-start | bytes 4718600 | tf_op jit(solution)/shard_map/ppermute | solution.py:268
  57.8 16.2 %copy-start = (bf16[768,1024]{1,0:T(8,128)(2,1)S(1)}, bf16[768,1024]{1,0:T(8,128)(2,1)}, u32[]{:S(2)}) copy-start(bf16[768,1024]{1,0:T(8,128)(2,1)} %refs_1_.9) | copy-start | bytes 4718596
  57.8 16.2 %all-to-all-start.1 = ((bf16[4,48,8,2,128]{4,3,2,1,0:T(2,128)(2,1)}), bf16[4,48,8,2,128]{4,3,2,1,0:T(2,128)(2,1)S(1)}, u32[]{:S(2)}, u32[]{:S(2)}) async-start(bf16[4,48,8,2,128]{4,3,2,1,0:T(2,128)(2,1)} %shard_map.47), calls=%async_computation.1 | async-start | bytes 1572864 | tf_op jit(solution)/shard_map/all_to_all | solution.py:237
  76.2 23.6 %collective-permute-start.1 = (s16[264,1024]{1,0:T(8,128)(2,1)S(1)}, s16[264,1024]{1,0:T(8,128)(2,1)}, u32[]{:S(2)}, u32[]{:S(2)}) collective-permute-start(s16[264,1024]{1,0:T(8,128)(2,1)S(1)} %shard_map.48), channel_id=1, source_target_pairs={{0,2},{1,66},{2,0},{3,64},{4,6},{5,70},{6,4},{7,68},{8,10},{9,74},... | collective-permute-start | bytes 1622024 | tf_op jit(solution)/shard_map/ppermute | solution.py:293
  80.3 20.8 %collective-permute-start.2 = (s16[264,1024]{1,0:T(8,128)(2,1)S(1)}, s16[264,1024]{1,0:T(8,128)(2,1)}, u32[]{:S(2)}, u32[]{:S(2)}) collective-permute-start(s16[264,1024]{1,0:T(8,128)(2,1)S(1)} %shard_map.49), channel_id=1, source_target_pairs={{0,66},{1,2},{2,64},{3,0},{4,70},{5,6},{6,68},{7,4},{8,74},{9,10},... | collective-permute-start | bytes 1622024 | tf_op jit(solution)/shard_map/ppermute | solution.py:293
  86.6 14.4 %collective-permute-start.3 = (s16[264,1024]{1,0:T(8,128)(2,1)}, s16[264,1024]{1,0:T(8,128)(2,1)}, u32[]{:S(2)}, u32[]{:S(2)}) collective-permute-start(s16[264,1024]{1,0:T(8,128)(2,1)} %shard_map.50), channel_id=1, source_target_pairs={{0,0},{1,64},{2,2},{3,66},{4,4},{5,68},{6,6},{7,70},{8,8},{9,72},{... | collective-permute-start | bytes 1622024 | tf_op jit(solution)/shard_map/ppermute | solution.py:293
  91.5 15.3 %collective-permute-start.4 = (s16[264,1024]{1,0:T(8,128)(2,1)}, s16[264,1024]{1,0:T(8,128)(2,1)S(1)}, u32[]{:S(2)}, u32[]{:S(2)}) collective-permute-start(s16[264,1024]{1,0:T(8,128)(2,1)} %shard_map.51), channel_id=1, source_target_pairs={{0,64},{1,0},{2,66},{3,2},{4,68},{5,4},{6,70},{7,6},{8,72},{9,8},{... | collective-permute-start | bytes 1622024 | tf_op jit(solution)/shard_map/ppermute | solution.py:293
  109.0 8.4 %collective-permute-start.5 = (s16[8,136,128]{2,1,0:T(8,128)(2,1)S(1)}, s16[8,136,128]{2,1,0:T(8,128)(2,1)S(1)}, u32[]{:S(2)}, u32[]{:S(2)}) collective-permute-start(s16[8,136,128]{2,1,0:T(8,128)(2,1)S(1)} %get-tuple-element.8), channel_id=1, source_target_pairs={{0,4},{1,5},{2,6},{3,7},{4,0},{5,1},{6,2},{7,3},{8,12},{9,13},{10,... | collective-permute-start | bytes 835592 | tf_op jit(solution)/shard_map/ppermute | solution.py:302
